TPU v7x, 32 devices: a whole 2x2x4 slice. The times are simulated.
32 devices in a mesh: groups: 2 (over y), req: 2 (over core), ctx: 8 (over z, x).
Axes of the slice: x: 2, y: 2, z: 4, core: 2. Of those that a mesh axis runs over, the one named last changes fastest.
Arguments:
- queries: bfloat16 [4, 1024, 4096], P(('groups', 'req'), 'ctx'), parts along dimension 0, may hold values from -6 to 6
- keys: bfloat16 [4, 1024, 512], P(('groups', 'req'), 'ctx'), parts along dimension 0, may hold values from -6 to 6
- values: bfloat16 [4, 1024, 512], P(('groups', 'req'), 'ctx'), parts along dimension 0, may hold values from -6 to 6
- cache_keys: bfloat16 [16, 256, 512], P(('groups', 'ctx')), parts along dimension 0, may hold values from -6 to 6
- cache_values: bfloat16 [16, 256, 512], P(('groups', 'ctx')), parts along dimension 0, may hold values from -6 to 6
- doc_lengths: int32 [4], P('groups'), parts along dimension 0, may hold values from 32 to 256, as said below
- doc_owners: int32 [4], P('groups'), parts along dimension 0, may hold values from 0 to 7, as said below
- block_offsets: int32 [4], P('groups'), parts along dimension 0, may hold values from 1 to 7
Outputs:
- attended: bfloat16 [4, 1024, 4096], P(('groups', 'req'), 'ctx'), parts along dimension 0
There are 2 independent parts, one for each index of `groups`. A program takes and returns all parts, laid end to end along the dimension named above; each array names one. Nothing has to cross between parts.
Inputs may be any that keep to these rules, and one draw needn't show every extreme that they name: `doc_lengths`: one document block has exactly 256 live rows. `doc_owners`: the owners of the two document blocks differ.
All inputs are finite; a program needn't handle non-finite values.
Results may differ from a plain program's by a relative error of at most 0.0065.
Values may be sent and summed in bfloat16 or wider, within the bound.
No kernel may reach another device: no remote copies, remote signals or barrier semaphores. Data moves between devices by JAX's collectives and lax.ppermute only.
A program may use at most 64 MiB of HBM per device.

v0:
```python
import math

import jax
import jax.numpy as jnp
from jax import lax
from jax.sharding import PartitionSpec as P

HD = 128
HOPS = 3


NEGATIVE = -1e30


def broadcast(block, axis, source):
    block = jnp.where(lax.axis_index(axis) == source, block, jnp.zeros_like(block))
    return lax.psum(block, axis)


def from_behind(value, axis, steps):
    count = lax.axis_size(axis)
    pairs = [(source, (source + steps) % count) for source in range(count)]
    return lax.ppermute(value, axis, pairs)


def merge_block(carried, query_rows, key_rows, value_rows, allowed):
    running, totals, summed = carried
    scores = jnp.einsum(
        "tid,sd->its", query_rows, key_rows, preferred_element_type=jnp.float32
    ) / math.sqrt(HD)
    scores = jnp.where(allowed[None], scores, NEGATIVE)
    highest = jnp.maximum(running, jnp.max(scores, axis=-1))
    weights = jnp.where(allowed[None], jnp.exp(scores - highest[..., None]), 0.0)
    shrink = jnp.exp(running - highest)
    totals = totals * shrink + jnp.sum(weights, axis=-1)
    summed = summed * shrink[..., None] + jnp.einsum(
        "its,sd->itd", weights.astype(jnp.bfloat16), value_rows, preferred_element_type=jnp.float32
    )
    return (highest, totals, summed)


def per_device(
    queries, keys, values, cache_keys, cache_values, doc_lengths, doc_owners, block_offsets
):
    cycle_size = lax.axis_size("ctx")
    position = lax.axis_index("ctx")
    request = lax.axis_index("req")
    tokens = queries.shape[1]
    kv_width = keys.shape[2]
    kv_heads = kv_width // HD
    group_size = queries.shape[2] // kv_width
    doc_rows = cache_keys.shape[1]
    offset = jnp.sum(jnp.where(jnp.arange(block_offsets.shape[0]) == request, block_offsets, 0))
    placed = (position - offset) % cycle_size
    inside = jnp.arange(tokens)
    resident = jnp.stack([keys[0], values[0]])
    blocks = [(resident, inside[None, :] <= inside[:, None])]
    cached = jnp.stack([cache_keys[0], cache_values[0]])
    doc_pairs = [broadcast(cached, "ctx", doc_owners[number]) for number in range(2)]
    for number in range(2):
        doc_live = jnp.broadcast_to(
            jnp.arange(doc_rows)[None, :] < doc_lengths[number], (tokens, doc_rows)
        )
        blocks.append((doc_pairs[number], doc_live))
    moving = resident
    for hop_count in range(1, HOPS + 1):
        moving = from_behind(moving, "ctx", 1)
        blocks.append((moving, jnp.broadcast_to(placed >= hop_count, (tokens, tokens))))
    query_heads = queries[0].reshape(tokens, kv_heads, group_size, HD)
    outputs = []
    for head_index in range(kv_heads):
        columns = slice(head_index * HD, (head_index + 1) * HD)
        query_rows = query_heads[:, head_index]
        carried = (
            jnp.full((group_size, tokens), NEGATIVE, jnp.float32),
            jnp.zeros((group_size, tokens), jnp.float32),
            jnp.zeros((group_size, tokens, HD), jnp.float32),
        )
        for paired, allowed in blocks:
            carried = merge_block(
                carried, query_rows, paired[0][:, columns], paired[1][:, columns], allowed
            )
        outputs.append(jnp.transpose(carried[2] / carried[1][..., None], (1, 0, 2)))
    attended = jnp.stack(outputs, axis=1).reshape(tokens, kv_heads * group_size * HD)
    return attended.astype(jnp.bfloat16)[None]


def solution(mesh):
    return jax.shard_map(
        per_device,
        mesh=mesh,
        in_specs=(
            P(("groups", "req"), "ctx", None),
            P(("groups", "req"), "ctx", None),
            P(("groups", "req"), "ctx", None),
            P(("groups", "ctx"), None, None),
            P(("groups", "ctx"), None, None),
            P("groups"),
            P("groups"),
            P("groups"),
        ),
        out_specs=P(("groups", "req"), "ctx", None),
        check_vma=False,
    )
```

profile of v0, /device:TPU:0, one launch (start us, length us, event | category | flops | bytes accessed | tf_op | source)
XLA Modules:
  0.0 129.9 jit_solution(4399630337771953146)
XLA Ops:
  6.5 1.0 pad_maximum_fusion.1
  7.6 3.0 %collective-permute-start = (bf16[2,128,512]{2,1,0:T(8,128)(2,1)S(1)}, bf16[2,128,512]{2,1,0:T(8,128)(2,1)S(1)}, u32[]{:S(2)}, u32[]{:S(2)}) collective-permute-start(bf16[2,128,512]{2,1,0:T(8,128)(2,1)S(1)} %pad_maximum_fusion.1), channel_id=1, source_target_pairs={{0,1},{1,2},{2,3},{3,4},{4,5},{5,6},{6,7},{7,0},{8,9},{9,10},{10,1... | collective-permute-start | bytes 786440 | tf_op jit(solution)/shard_map/ppermute | solution.py:23
  14.3 1.1 broadcast_select_fusion.1
  16.8 1.6 %fusion.350 = (f32[8,128]{1,0:T(8,128)}, f32[8,128,128]{1,2,0:T(8,128)}) fusion(bf16[128,4,8,128]{0,3,2,1:T(8,128)(2,1)S(1)} %bitcast.900, bf16[128,512]{1,0:T(8,128)(2,1)S(1)} %bitcast.929, pred[128,128]{0,1:T(8,128)(4,1)S(1)} %iota_compare_fusion), kind=kOutput, calls=%fused_computation.530 | convolution fusion | flops 33946624 | bytes 839680 | tf_op jit(solution)/shard_map/tid,sd->its/dot_general | solution.py:28
  18.4 1.6 %fusion.344 = (f32[8,128]{1,0:T(8,128)}, f32[8,128,128]{1,2,0:T(8,128)}) fusion(bf16[128,4,8,128]{0,3,2,1:T(8,128)(2,1)S(1)} %bitcast.901, bf16[128,512]{1,0:T(8,128)(2,1)S(1)} %bitcast.930, pred[128,128]{0,1:T(8,128)(4,1)S(1)} %iota_compare_fusion), kind=kOutput, calls=%fused_computation.524 | convolution fusion | flops 33946624 | bytes 839680 | tf_op jit(solution)/shard_map/tid,sd->its/dot_general | solution.py:28
  20.0 1.6 %fusion.338 = (f32[8,128]{1,0:T(8,128)}, f32[8,128,128]{1,2,0:T(8,128)}) fusion(bf16[128,4,8,128]{0,3,2,1:T(8,128)(2,1)S(1)} %bitcast.902, bf16[128,512]{1,0:T(8,128)(2,1)S(1)} %bitcast.931, pred[128,128]{0,1:T(8,128)(4,1)S(1)} %iota_compare_fusion), kind=kOutput, calls=%fused_computation.518 | convolution fusion | flops 33946624 | bytes 839680 | tf_op jit(solution)/shard_map/tid,sd->its/dot_general | solution.py:28
  22.9 1.2 iota_compare_fusion.1
  24.8 1.2 iota_compare_fusion.2
  26.9 1.6 %fusion.332 = (f32[8,128]{1,0:T(8,128)}, f32[8,128,128]{1,2,0:T(8,128)}) fusion(bf16[128,4,8,128]{0,3,2,1:T(8,128)(2,1)S(1)} %bitcast.903, bf16[128,512]{1,0:T(8,128)(2,1)S(1)} %bitcast.932, pred[128,128]{0,1:T(8,128)(4,1)S(1)} %iota_compare_fusion), kind=kOutput, calls=%fused_computation.512 | convolution fusion | flops 33946624 | bytes 839680 | tf_op jit(solution)/shard_map/tid,sd->its/dot_general | solution.py:28
  29.3 1.6 %fusion.341 = (f32[8,128]{1,0:T(8,128)}, f32[8,128,128]{1,2,0:T(8,128)}) fusion(bf16[128,4,8,128]{0,3,2,1:T(8,128)(2,1)S(1)} %bitcast.905, bf16[128,512]{1,0:T(8,128)(2,1)S(1)} %get-tuple-element.70, pred[]{:T(512)S(6)} %ge.9), kind=kOutput, calls=%fused_computation.521 | convolution fusion | flops 33946624 | bytes 823297 | tf_op jit(solution)/shard_map/tid,sd->its/dot_general | solution.py:28
  30.9 1.5 %collective-permute-start.1 = (bf16[2,128,512]{2,1,0:T(8,128)(2,1)S(1)}, bf16[2,128,512]{2,1,0:T(8,128)(2,1)S(1)}, u32[]{:S(2)}, u32[]{:S(2)}) collective-permute-start(bf16[2,128,512]{2,1,0:T(8,128)(2,1)S(1)} %collective-permute-done), channel_id=1, source_target_pairs={{0,1},{1,2},{2,3},{3,4},{4,5},{5,6},{6,7},{7,0},{8,9},{9,10},{10,1... | collective-permute-start | bytes 786440 | tf_op jit(solution)/shard_map/ppermute | solution.py:23
  32.5 1.6 %fusion.335 = (f32[8,128]{1,0:T(8,128)}, f32[8,128,128]{1,2,0:T(8,128)}) fusion(bf16[128,4,8,128]{0,3,2,1:T(8,128)(2,1)S(1)} %bitcast.906, bf16[128,512]{1,0:T(8,128)(2,1)S(1)} %get-tuple-element.70, pred[]{:T(512)S(6)} %ge.9), kind=kOutput, calls=%fused_computation.515 | convolution fusion | flops 33946624 | bytes 823297 | tf_op jit(solution)/shard_map/tid,sd->its/dot_general | solution.py:28
  34.9 8.0 %collective-permute-done.1 = bf16[2,128,512]{2,1,0:T(8,128)(2,1)S(1)} collective-permute-done((bf16[2,128,512]{2,1,0:T(8,128)(2,1)S(1)}, bf16[2,128,512]{2,1,0:T(8,128)(2,1)S(1)}, u32[]{:S(2)}, u32[]{:S(2)}) %collective-permute-start.1) | collective-permute-done | bytes 262176 | tf_op jit(solution)/shard_map/ppermute | solution.py:23
  43.8 1.6 %fusion.340 = (f32[8,128]{1,0:T(8,128)}, f32[8,128,128]{1,2,0:T(8,128)}) fusion(bf16[128,4,8,128]{0,3,2,1:T(8,128)(2,1)S(1)} %bitcast.909, bf16[128,512]{1,0:T(8,128)(2,1)S(1)} %get-tuple-element.68, pred[]{:T(512)S(6)} %ge.10), kind=kOutput, calls=%fused_computation.520 | convolution fusion | flops 33946624 | bytes 823297 | tf_op jit(solution)/shard_map/tid,sd->its/dot_general | solution.py:28
  45.4 1.6 %fusion.334 = (f32[8,128]{1,0:T(8,128)}, f32[8,128,128]{1,2,0:T(8,128)}) fusion(bf16[128,4,8,128]{0,3,2,1:T(8,128)(2,1)S(1)} %bitcast.910, bf16[128,512]{1,0:T(8,128)(2,1)S(1)} %get-tuple-element.68, pred[]{:T(512)S(6)} %ge.10), kind=kOutput, calls=%fused_computation.514 | convolution fusion | flops 33946624 | bytes 823297 | tf_op jit(solution)/shard_map/tid,sd->its/dot_general | solution.py:28
  47.9 10.0 %collective-permute-done.2 = bf16[2,128,512]{2,1,0:T(8,128)(2,1)S(1)} collective-permute-done((bf16[2,128,512]{2,1,0:T(8,128)(2,1)S(1)}, bf16[2,128,512]{2,1,0:T(8,128)(2,1)S(1)}, u32[]{:S(2)}, u32[]{:S(2)}) %collective-permute-start.2) | collective-permute-done | bytes 262176 | tf_op jit(solution)/shard_map/ppermute | solution.py:23
  58.5 1.6 %fusion.345 = (f32[8,128]{1,0:T(8,128)}, f32[8,128,128]{1,2,0:T(8,128)}) fusion(bf16[128,4,8,128]{0,3,2,1:T(8,128)(2,1)S(1)} %bitcast.912, bf16[128,512]{1,0:T(8,128)(2,1)S(1)} %get-tuple-element.66, pred[]{:T(512)S(6)} %ge.11), kind=kOutput, calls=%fused_computation.525 | convolution fusion | flops 33946624 | bytes 823297 | tf_op jit(solution)/shard_map/tid,sd->its/dot_general | solution.py:28
  60.2 1.6 %fusion.339 = (f32[8,128]{1,0:T(8,128)}, f32[8,128,128]{1,2,0:T(8,128)}) fusion(bf16[128,4,8,128]{0,3,2,1:T(8,128)(2,1)S(1)} %bitcast.913, bf16[128,512]{1,0:T(8,128)(2,1)S(1)} %get-tuple-element.66, pred[]{:T(512)S(6)} %ge.11), kind=kOutput, calls=%fused_computation.519 | convolution fusion | flops 33946624 | bytes 823297 | tf_op jit(solution)/shard_map/tid,sd->its/dot_general | solution.py:28
  61.8 1.6 %fusion.333 = (f32[8,128]{1,0:T(8,128)}, f32[8,128,128]{1,2,0:T(8,128)}) fusion(bf16[128,4,8,128]{0,3,2,1:T(8,128)(2,1)S(1)} %bitcast.914, bf16[128,512]{1,0:T(8,128)(2,1)S(1)} %get-tuple-element.66, pred[]{:T(512)S(6)} %ge.11), kind=kOutput, calls=%fused_computation.513 | convolution fusion | flops 33946624 | bytes 823297 | tf_op jit(solution)/shard_map/tid,sd->its/dot_general | solution.py:28
  63.4 1.6 %fusion.327 = (f32[8,128]{1,0:T(8,128)}, f32[8,128,128]{1,2,0:T(8,128)}) fusion(bf16[128,4,8,128]{0,3,2,1:T(8,128)(2,1)S(1)} %bitcast.915, bf16[128,512]{1,0:T(8,128)(2,1)S(1)} %get-tuple-element.66, pred[]{:T(512)S(6)} %ge.11), kind=kOutput, calls=%fused_computation.507 | convolution fusion | flops 33946624 | bytes 823297 | tf_op jit(solution)/shard_map/tid,sd->its/dot_general | solution.py:28
  65.0 32.8 %all-reduce.3.cloned.1.call-done = (bf16[2,256,512]{2,1,0:T(8,128)(2,1)}, bf16[2,256,512]{2,1,0:T(8,128)(2,1)}) async-done(((bf16[2,256,512]{2,1,0:T(8,128)(2,1)}, bf16[2,256,512]{2,1,0:T(8,128)(2,1)}), (bf16[2,256,512]{2,1,0:T(8,128)(2,1)}, bf16[2,256,512]{2,1,0:T(8,128)(2,1)})) %all-reduce.3.cloned.1.call-update) | async-done | bytes 1048592 | tf_op jit(solution)/shard_map/psum | solution.py:17
  97.8 1.3 slice_bitcast_fusion.3
  108.1 1.0 copy-done.3
  121.7 1.3 %copy.105 = bf16[1,128,4096]{2,1,0:T(8,128)(2,1)} copy(bf16[1,128,4096]{1,2,0:T(8,128)(2,1)S(1)} %bitcast.924) | data formatting | bytes 2097152 | tf_op jit(solution)/shard_map/convert_element_type | solution.py:85
  (152 shorter events, 30.9 us)
Async XLA Ops:
  6.5 6.7 %copy-start.15 = (bf16[1,256,512]{2,1,0:T(8,128)(2,1)S(1)}, bf16[1,256,512]{2,1,0:T(8,128)(2,1)}, u32[]{:S(2)}) copy-start(bf16[1,256,512]{2,1,0:T(8,128)(2,1)} %param.11) | copy-start | bytes 786436
  6.5 91.3 %all-reduce.3.cloned.1.call-start = ((), (), s32[]{:S(2)}) async-start(), calls=%async_computation | async-start | bytes 2097152 | tf_op jit(solution)/shard_map/psum | solution.py:17
  7.6 20.9 %collective-permute-start = (bf16[2,128,512]{2,1,0:T(8,128)(2,1)S(1)}, bf16[2,128,512]{2,1,0:T(8,128)(2,1)S(1)}, u32[]{:S(2)}, u32[]{:S(2)}) collective-permute-start(bf16[2,128,512]{2,1,0:T(8,128)(2,1)S(1)} %pad_maximum_fusion.1), channel_id=1, source_target_pairs={{0,1},{1,2},{2,3},{3,4},{4,5},{5,6},{6,7},{7,0},{8,9},{9,10},{10,1... | collective-permute-start | bytes 786440 | tf_op jit(solution)/shard_map/ppermute | solution.py:23
  13.3 1.0 copy-start.16
  14.2 1.6 %copy-start.12 = (bf16[1,128,4096]{2,1,0:T(8,128)(2,1)S(1)}, bf16[1,128,4096]{2,1,0:T(8,128)(2,1)}, u32[]{:S(2)}) copy-start(bf16[1,128,4096]{2,1,0:T(8,128)(2,1)} %param.8) | copy-start | bytes 3145732
  15.8 0.9 copy-start.13
  20.0 6.7 %copy-start.14 = (bf16[1,128,512]{2,1,0:T(8,128)(2,1)S(1)}, bf16[1,128,512]{2,1,0:T(8,128)(2,1)}, u32[]{:S(2)}) copy-start(bf16[1,128,512]{2,1,0:T(8,128)(2,1)} %param.10) | copy-start | bytes 393220
  22.9 1.2 copy-start.38
  30.9 12.0 %collective-permute-start.1 = (bf16[2,128,512]{2,1,0:T(8,128)(2,1)S(1)}, bf16[2,128,512]{2,1,0:T(8,128)(2,1)S(1)}, u32[]{:S(2)}, u32[]{:S(2)}) collective-permute-start(bf16[2,128,512]{2,1,0:T(8,128)(2,1)S(1)} %collective-permute-done), channel_id=1, source_target_pairs={{0,1},{1,2},{2,3},{3,4},{4,5},{5,6},{6,7},{7,0},{8,9},{9,10},{10,1... | collective-permute-start | bytes 786440 | tf_op jit(solution)/shard_map/ppermute | solution.py:23
  45.4 12.5 %collective-permute-start.2 = (bf16[2,128,512]{2,1,0:T(8,128)(2,1)S(1)}, bf16[2,128,512]{2,1,0:T(8,128)(2,1)S(1)}, u32[]{:S(2)}, u32[]{:S(2)}) collective-permute-start(bf16[2,128,512]{2,1,0:T(8,128)(2,1)S(1)} %collective-permute-done.1), channel_id=1, source_target_pairs={{0,1},{1,2},{2,3},{3,4},{4,5},{5,6},{6,7},{7,0},{8,9},{9,10},{10,1... | collective-permute-start | bytes 786440 | tf_op jit(solution)/shard_map/ppermute | solution.py:23
  103.9 0.7 copy-start.26
  106.7 1.3 copy-start.11
  107.6 1.8 %copy-start.10 = (f32[8,128,128]{1,2,0:T(8,128)S(1)}, f32[8,128,128]{1,2,0:T(8,128)}, u32[]{:S(2)}) copy-start(f32[8,128,128]{1,2,0:T(8,128)} %get-tuple-element.112) | copy-start | bytes 1572868
  107.6 3.0 %copy-start.6 = (f32[8,128,128]{1,2,0:T(8,128)S(1)}, f32[8,128,128]{1,2,0:T(8,128)}, u32[]{:S(2)}) copy-start(f32[8,128,128]{1,2,0:T(8,128)} %get-tuple-element.122) | copy-start | bytes 1572868
  107.6 3.0 %copy-start.7 = (f32[8,128,128]{1,2,0:T(8,128)S(1)}, f32[8,128,128]{1,2,0:T(8,128)}, u32[]{:S(2)}) copy-start(f32[8,128,128]{1,2,0:T(8,128)} %get-tuple-element.110) | copy-start | bytes 1572868
  108.0 1.1 copy-start.3
  108.0 1.3 copy-start.2
  109.3 1.0 copy-start.1
  109.4 1.1 copy-start
  110.3 1.0 copy-start.4
  110.3 1.2 copy-start.5
  114.9 0.9 copy-start.17
  116.1 1.0 copy-start.9
  118.9 1.0 copy-start.8
  (19 other events, 12.8 us)
Sparse Core Ops, SparseCore 0:
  15.5 82.2 all-reduce.2
where the time goes:
time: 131 us; the launch traced here: 130 us
  waiting for transfers between devices  50.9 us (39%)
  matrix products  32.1 us (25%)
  local copies, waits for them, and re-layouts  17.4 us (13%)
  between operations  16.1 us (12%)
  other arithmetic  8.85 us (7%)
  starting transfers between devices  4.57 us (3%)
    psum x1, waiting for transfers between devices, broadcast(): return lax.psum(block, axis)  32.8 us
    dot_general x24, matrix products, merge_block(): jnp.einsum('tid,sd->its', query_rows, key_rows, preferred_element_type=jn...  25.1 us
    ppermute x3, waiting for transfers between devices, from_behind(): return lax.ppermute(value, axis, pairs)  18.1 us
    unnamed x81, local copies, waits for them, and re-layouts  12.8 us
    dot_general x24, matrix products, merge_block(): jnp.einsum('its,sd->itd', weights.astype(jnp.bfloat16), value_rows, prefe...  7.01 us
    ppermute x3, starting transfers between devices, from_behind(): return lax.ppermute(value, axis, pairs)  4.57 us
    reduce_sum x15, other arithmetic, merge_block(): totals = totals * shrink + jnp.sum(weights, axis=-1)  3.35 us
  transfers between devices with their start and end apart: 4, of which 3 were waited for; matrix products, arithmetic and copies ran while one was open for 23% of the time, Pallas kernels for 0%

commit v1 on v0

v1 whole, which is shorter than its diff:
```python
import functools
import math

import jax
import jax.numpy as jnp
from jax import lax
from jax.experimental import pallas as pl
from jax.experimental.pallas import tpu as pltpu
from jax.sharding import PartitionSpec as P

HD = 128
HOPS = 3
DOCS = 2
RING_LIMIT = 16

NEGATIVE = -1e30
SCALE = math.log2(math.e) / math.sqrt(HD)


def broadcast(block, axis, source):
    block = jnp.where(lax.axis_index(axis) == source, block, jnp.zeros_like(block))
    return lax.psum(block, axis)


def shifted(value, axis, steps):
    count = lax.axis_size(axis)
    pairs = [(source, (source + steps) % count) for source in range(count)]
    return lax.ppermute(value, axis, pairs)


def attention_body(rows, group, tile, own, *refs):
    count = len(rows)
    live, q_ref = refs[0], refs[1]
    key_refs, value_refs = refs[2 : 2 + count], refs[2 + count : 2 + 2 * count]
    out_ref, keys, values = refs[2 + 2 * count :]
    total = sum(rows)
    starts = [sum(rows[:number]) for number in range(count)]
    tokens = q_ref.shape[0]

    @pl.when(pl.program_id(0) == 0)
    def _():
        values[:, HD:] = jnp.ones((total, HD), jnp.bfloat16)
        for number, (start, height) in enumerate(zip(starts, rows)):
            lane = lax.broadcasted_iota(jnp.int32, (height, HD), 1)
            row = lax.broadcasted_iota(jnp.int32, (height, HD), 0)
            dead = (row >= live[number]) & (lane == 0)
            keys[start : start + height, HD:] = jnp.where(dead, NEGATIVE, 0.0).astype(jnp.bfloat16)

    for key_ref, value_ref, start, height in zip(key_refs, value_refs, starts, rows):
        keys[start : start + height, :HD] = key_ref[...].reshape(height, HD)
        values[start : start + height, :HD] = value_ref[...].reshape(height, HD)

    lane = lax.broadcasted_iota(jnp.int32, (tile * tokens, HD), 1)
    first = jnp.where(lane == 0, 1.0, 0.0).astype(jnp.bfloat16)
    query = lax.broadcasted_iota(jnp.int32, (tokens, rows[own]), 0)
    key = lax.broadcasted_iota(jnp.int32, (tokens, rows[own]), 1)
    causal = jnp.concatenate([key <= query] * tile, axis=0)
    for head in range(0, group, tile):
        heads = [q_ref[:, (head + i) * HD : (head + i + 1) * HD] for i in range(tile)]
        block = jnp.concatenate([jnp.concatenate(heads, axis=0), first], axis=1)
        scores = lax.dot_general(
            block, keys[...], (((1,), (1,)), ((), ())), preferred_element_type=jnp.float32
        )
        begin, end = starts[own], starts[own] + rows[own]
        masked = jnp.where(causal, scores[:, begin:end], NEGATIVE)
        pieces = [scores[:, :begin], masked, scores[:, end:]]
        scores = jnp.concatenate([piece for piece in pieces if piece.shape[1]], axis=1)
        highest = jnp.max(scores, axis=1, keepdims=True) * SCALE
        weights = jnp.exp2(scores * SCALE - highest).astype(jnp.bfloat16)
        summed = jnp.dot(weights, values[...], preferred_element_type=jnp.float32)
        result = (summed[:, :HD] / summed[:, HD:]).astype(jnp.bfloat16)
        for i in range(tile):
            out_ref[:, (head + i) * HD : (head + i + 1) * HD] = result[i * tokens : (i + 1) * tokens]


def attention(live, queries, segments, own):
    tokens, width = queries.shape
    kv_heads = segments[0][0].shape[-1] // HD
    group = width // HD // kv_heads
    rows = tuple(segment[4] for segment in segments)

    def spec(array, lead, height):
        return pl.BlockSpec((1,) * len(lead) + (height, HD), lambda g, s: (*lead, 0, g))

    heads = pl.BlockSpec((tokens, group * HD), lambda g, s: (0, g))
    return pl.pallas_call(
        functools.partial(attention_body, rows, group, 2 if group % 2 == 0 else 1, own),
        out_shape=jax.ShapeDtypeStruct((tokens, width), jnp.bfloat16),
        grid_spec=pltpu.PrefetchScalarGridSpec(
            num_scalar_prefetch=1,
            grid=(kv_heads,),
            in_specs=[heads]
            + [spec(segment[0], segment[1], segment[4]) for segment in segments]
            + [spec(segment[2], segment[3], segment[4]) for segment in segments],
            out_specs=heads,
            scratch_shapes=[pltpu.VMEM((sum(rows), 2 * HD), jnp.bfloat16)] * 2,
        ),
        compiler_params=pltpu.CompilerParams(vmem_limit_bytes=48 << 20),
    )(live, queries, *[s[0] for s in segments], *[s[2] for s in segments])


def pick_body(holds, picks, *refs):
    pieces, out_ref, sems = refs[: len(holds)], refs[len(holds)], refs[len(holds) + 1]
    for act in ("start", "wait"):
        for number in range(DOCS):
            for (delta, begin), piece in zip(holds, pieces):

                @pl.when(picks[number] == delta)
                def _():
                    target = out_ref.at[number, :, pl.ds(begin, piece.shape[1])]
                    slot = sems.at[number, 0 if begin == 0 else 1]
                    copy = pltpu.make_async_copy(piece, target, slot)
                    getattr(copy, act)()


def pick(picks, holds, pieces, shape):
    return pl.pallas_call(
        functools.partial(pick_body, holds),
        out_shape=jax.ShapeDtypeStruct((DOCS,) + shape, jnp.bfloat16),
        grid_spec=pltpu.PrefetchScalarGridSpec(
            num_scalar_prefetch=1,
            grid=(1,),
            in_specs=[pl.BlockSpec(memory_space=pl.ANY)] * len(pieces),
            out_specs=pl.BlockSpec((DOCS,) + shape, lambda i, s: (0, 0, 0, 0)),
            scratch_shapes=[pltpu.SemaphoreType.DMA((DOCS, 2))],
        ),
    )(picks, *pieces)


def ring_documents(cache_keys, cache_values, doc_owners):
    count = lax.axis_size("ctx")
    cores = lax.axis_size("req")
    core = lax.axis_index("req")
    ring = list(range(0, count, 2)) + list(range(1, count, 2))[::-1]
    place = jnp.array([ring.index(index) for index in range(count)], jnp.int32)
    doc_rows = cache_keys.shape[1]
    half = doc_rows // cores
    mine = [lax.dynamic_slice_in_dim(part[0], core * half, half, 0) for part in (cache_keys, cache_values)]
    mine = jnp.stack(mine)
    onward = [(ring[i], ring[(i + 1) % count]) for i in range(count)]
    backward = [(target, source) for source, target in onward]
    holds, pieces = [(0, 0)], [mine]
    ahead = behind = mine
    for step in range(1, count // 2 + 1):
        if 2 * step < count:
            ahead = lax.ppermute(ahead, "ctx", onward)
            behind = lax.ppermute(behind, "ctx", backward)
            holds += [(count - step, 0), (step, 0)]
            pieces += [ahead, behind]
        else:
            cut = half // 2
            upper = lax.ppermute(ahead[:, :cut], "ctx", onward)
            lower = lax.ppermute(behind[:, cut:], "ctx", backward)
            holds += [(step, 0), (step, cut)]
            pieces += [upper, lower]
    picks = (place[doc_owners] - place[lax.axis_index("ctx")]) % count
    held = pick(picks, holds, pieces, mine.shape)
    other = shifted(held, "req", 1)
    return [(held, core * half), (other, (1 - core) * half)]


def summed_documents(cache_keys, cache_values, doc_owners):
    cached = jnp.stack([cache_keys[0], cache_values[0]])
    docs = jnp.stack([broadcast(cached, "ctx", doc_owners[number]) for number in range(DOCS)])
    return [(docs, 0)]


def per_device(
    queries, keys, values, cache_keys, cache_values, doc_lengths, doc_owners, block_offsets
):
    count = lax.axis_size("ctx")
    position = lax.axis_index("ctx")
    request = lax.axis_index("req")
    tokens = queries.shape[1]
    offset = jnp.sum(jnp.where(jnp.arange(block_offsets.shape[0]) == request, block_offsets, 0))
    placed = (position - offset) % count
    even = position % 2 == 0

    own = jnp.stack([keys[0], values[0]])
    two = shifted(own, "ctx", 2)
    swapped = lax.ppermute(two, "ctx", [(i, i ^ 1) for i in range(count)])
    passed = shifted(jnp.where(even, own, two), "ctx", 1)
    hop_of_swapped = jnp.where(even, 1, HOPS)
    hop_of_passed = jnp.where(even, HOPS, 1)

    if lax.axis_size("req") == 2 and count <= RING_LIMIT:
        documents = ring_documents(cache_keys, cache_values, doc_owners)
    else:
        documents = summed_documents(cache_keys, cache_values, doc_owners)

    blocks = [(own, tokens), (two, jnp.where(placed >= 2, tokens, 0))]
    blocks += [(swapped, jnp.where(placed >= hop_of_swapped, tokens, 0))]
    blocks += [(passed, jnp.where(placed >= hop_of_passed, tokens, 0))]
    live = [jnp.asarray(count_of, jnp.int32) for _, count_of in blocks]
    segments = [(block, (0,), block, (1,), tokens) for block, _ in blocks]
    for docs, begin in documents:
        for number in range(DOCS):
            segments.append((docs, (number, 0), docs, (number, 1), docs.shape[2]))
            live.append(doc_lengths[number] - begin)
    return attention(jnp.stack(live), queries[0], segments, 0)[None]


def solution(mesh):
    return jax.shard_map(
        per_device,
        mesh=mesh,
        in_specs=(
            P(("groups", "req"), "ctx", None),
            P(("groups", "req"), "ctx", None),
            P(("groups", "req"), "ctx", None),
            P(("groups", "ctx"), None, None),
            P(("groups", "ctx"), None, None),
            P("groups"),
            P("groups"),
            P("groups"),
        ),
        out_specs=P(("groups", "req"), "ctx", None),
        check_vma=False,
    )
```

time: 131 us -> 64.8 us (0.49)
  matrix products: 32.1 us -> 0 us
  waiting for transfers between devices: 50.9 us -> 26.2 us
  between operations: 16.1 us -> 3.26 us
  Pallas kernels: 0 us -> 12.4 us
  local copies, waits for them, and re-layouts: 17.4 us -> 5.59 us
  starting transfers between devices: 4.57 us -> 15.2 us
  other arithmetic: 8.85 us -> 1.93 us
    psum x1 -> x0, waiting for transfers between devices: 32.8 us -> none  [broadcast(): return lax.psum(block, axis)]
    dot_general x48 -> x0, matrix products: 32.1 us -> none  [the longest x24 25.1 us: merge_block(): jnp.einsum('tid,sd->its', query_rows, key_rows, preferred_element_type=jn...]
    pallas_call x0 -> x2, Pallas kernels: none -> 12.4 us  [the longest x1 9.72 us: attention(): pl.pallas_call(functools.partial(attention_body, rows, group, 2 if group...]
    ppermute x3 -> x12, starting transfers between devices: 4.57 us -> 15.2 us  [the longest x3 7.06 us: ring_documents(): behind = lax.ppermute(behind, 'ctx', backward)]
    unnamed x81 -> x35, local copies, waits for them, and re-layouts: 12.8 us -> 2.61 us
    ppermute x3 -> x12, waiting for transfers between devices: 18.1 us -> 26.2 us  [the longest x3 15.3 us: ring_documents(): behind = lax.ppermute(behind, 'ctx', backward)]
    reduce_sum x16 -> x0, other arithmetic: 4.05 us -> none  [the longest x15 3.35 us: merge_block(): totals = totals * shrink + jnp.sum(weights, axis=-1)]
    lt x2 -> x0, other arithmetic: 2.41 us -> none  [per_device(): jnp.arange(doc_rows)[None, :] < doc_lengths[number]]
  transfers between devices with their start and end apart: 4 -> 12, of which waited for: 3 -> 7; matrix products, arithmetic and copies ran while one was open for 23% -> 6% of each run, Pallas kernels for 0% -> 4%
where the time goes in v1:
time: 64.8 us; the launch traced here: 64.5 us
  waiting for transfers between devices  26.2 us (40%)
  starting transfers between devices  15.2 us (23%)
  Pallas kernels  12.4 us (19%)
  local copies, waits for them, and re-layouts  5.59 us (9%)
  between operations  3.26 us (5%)
  other arithmetic  1.93 us (3%)
    ppermute x3, waiting for transfers between devices, ring_documents(): behind = lax.ppermute(behind, 'ctx', backward)  15.3 us
    pallas_call x1, Pallas kernels, attention(): pl.pallas_call(functools.partial(attention_body, rows, group, 2 if group...  9.72 us
    ppermute x3, starting transfers between devices, ring_documents(): behind = lax.ppermute(behind, 'ctx', backward)  7.06 us
    ppermute x1, waiting for transfers between devices, per_device(): swapped = lax.ppermute(two, 'ctx', [(i, i ^ 1) for i in range(count)])  4.4 us
    ppermute x3, waiting for transfers between devices, shifted(): return lax.ppermute(value, axis, pairs)  4.18 us
    ppermute x3, starting transfers between devices, shifted(): return lax.ppermute(value, axis, pairs)  3.78 us
    pallas_call x1, Pallas kernels, pick(): pl.pallas_call(functools.partial(pick_body, holds), out_shape=jax.ShapeDt...  2.71 us
    unnamed x35, local copies, waits for them, and re-layouts  2.61 us
  transfers between devices with their start and end apart: 12, of which 7 were waited for; matrix products, arithmetic and copies ran while one was open for 6% of the time, Pallas kernels for 4%

profile of v1, /device:TPU:0, one launch (start us, length us, event | category | flops | bytes accessed | tf_op | source)
XLA Modules:
  0.0 64.5 jit_solution(3911410618287488822)
XLA Ops:
  0.0 1.0 %constant_dynamic-slice_fusion = (bf16[1,128,512]{2,1,0:T(8,128)(2,1)S(1)}, bf16[1,128,512]{2,1,0:T(8,128)(2,1)S(1)}) fusion(bf16[1,256,512]{2,1,0:T(8,128)(2,1)} %param.13, s32[]{:T(128)S(6)} %select_n.68, bf16[1,256,512]{2,1,0:T(8,128)(2,1)} %param.12), kind=kLoop, calls=%fused_computation.13 | loop fusion | bytes 524292 | tf_op jit(solution)/shard_map/dynamic_slice | solution.py:138
  1.1 3.0 %collective-permute-start.4 = (bf16[2,128,512]{2,1,0:T(8,128)(2,1)S(1)}, bf16[2,128,512]{2,1,0:T(8,128)(2,1)S(1)}, u32[]{:S(2)}, u32[]{:S(2)}) collective-permute-start(bf16[2,128,512]{2,1,0:T(8,128)(2,1)S(1)} %pad_maximum_fusion.refs_0_), channel_id=1, source_target_pairs={{2,0},{4,2},{6,4},{7,6},{5,7},{3,5},{1,3},{0,1},{10,8},{12,10},{14... | collective-permute-start | bytes 786440 | tf_op jit(solution)/shard_map/ppermute | solution.py:147
  4.2 6.2 %collective-permute-done.4.refs_2_ = bf16[2,128,512]{2,1,0:T(8,128)(2,1)S(1)} collective-permute-done((bf16[2,128,512]{2,1,0:T(8,128)(2,1)S(1)}, bf16[2,128,512]{2,1,0:T(8,128)(2,1)S(1)}, u32[]{:S(2)}, u32[]{:S(2)}) %collective-permute-start.4) | collective-permute-done | bytes 262176 | tf_op jit(solution)/shard_map/ppermute | solution.py:147
  10.5 1.7 %collective-permute-start.6 = (bf16[2,128,512]{2,1,0:T(8,128)(2,1)S(1)}, bf16[2,128,512]{2,1,0:T(8,128)(2,1)S(1)}, u32[]{:S(2)}, u32[]{:S(2)}) collective-permute-start(bf16[2,128,512]{2,1,0:T(8,128)(2,1)S(1)} %collective-permute-done.4.refs_2_), channel_id=1, source_target_pairs={{2,0},{4,2},{6,4},{7,6},{5,7},{3,5},{1,3},{0,1},{10,8},{12,10},{14... | collective-permute-start | bytes 786440 | tf_op jit(solution)/shard_map/ppermute | solution.py:147
  12.6 1.8 %collective-permute-start = (bf16[2,128,512]{2,1,0:T(8,128)(2,1)S(1)}, bf16[2,128,512]{2,1,0:T(8,128)(2,1)S(1)}, u32[]{:S(2)}, u32[]{:S(2)}) collective-permute-start(bf16[2,128,512]{2,1,0:T(8,128)(2,1)S(1)} %constant_dynamic-update-slice_fusion.refs_2_.refs_10_), channel_id=1, source_target_pairs={{0,2},{1,3},{2,4},{3,5},{4,6},{5,7},{6,0},{7,1},{8,10},{9,11},{10,... | collective-permute-start | bytes 786440 | tf_op jit(solution)/shard_map/ppermute | solution.py:28
  14.4 3.6 %collective-permute-done.6.refs_4_ = bf16[2,128,512]{2,1,0:T(8,128)(2,1)S(1)} collective-permute-done((bf16[2,128,512]{2,1,0:T(8,128)(2,1)S(1)}, bf16[2,128,512]{2,1,0:T(8,128)(2,1)S(1)}, u32[]{:S(2)}, u32[]{:S(2)}) %collective-permute-start.6) | collective-permute-done | bytes 262176 | tf_op jit(solution)/shard_map/ppermute | solution.py:147
  18.0 2.4 %collective-permute-start.8 = (bf16[2,128,512]{2,1,0:T(8,128)(2,1)S(1)}, bf16[2,128,512]{2,1,0:T(8,128)(2,1)S(1)}, u32[]{:S(2)}, u32[]{:S(2)}) collective-permute-start(bf16[2,128,512]{2,1,0:T(8,128)(2,1)S(1)} %collective-permute-done.6.refs_4_), channel_id=1, source_target_pairs={{2,0},{4,2},{6,4},{7,6},{5,7},{3,5},{1,3},{0,1},{10,8},{12,10},{14... | collective-permute-start | bytes 786440 | tf_op jit(solution)/shard_map/ppermute | solution.py:147
  20.4 1.3 %collective-permute-start.7 = (bf16[2,128,512]{2,1,0:T(8,128)(2,1)S(1)}, bf16[2,128,512]{2,1,0:T(8,128)(2,1)S(1)}, u32[]{:S(2)}, u32[]{:S(2)}) collective-permute-start(bf16[2,128,512]{2,1,0:T(8,128)(2,1)S(1)} %collective-permute-done.5.refs_3_), channel_id=1, source_target_pairs={{0,2},{2,4},{4,6},{6,7},{7,5},{5,3},{3,1},{1,0},{8,10},{10,12},{12... | collective-permute-start | bytes 786440 | tf_op jit(solution)/shard_map/ppermute | solution.py:146
  22.3 0.6 %copy-done.2 = s32[8]{0:T(128)S(1)} copy-done((s32[8]{0:T(128)S(1)}, s32[8]{0:T(128)}, u32[]{:S(2)}) %copy-start.2) | copy-done | bytes 56
  23.6 0.6 gather_fusion
  24.2 5.4 %collective-permute-done.8.refs_6_ = bf16[2,128,512]{2,1,0:T(8,128)(2,1)S(1)} collective-permute-done((bf16[2,128,512]{2,1,0:T(8,128)(2,1)S(1)}, bf16[2,128,512]{2,1,0:T(8,128)(2,1)S(1)}, u32[]{:S(2)}, u32[]{:S(2)}) %collective-permute-start.8) | collective-permute-done | bytes 262176 | tf_op jit(solution)/shard_map/ppermute | solution.py:147
  30.4 1.5 %collective-permute-start.9 = (bf16[2,64,512]{2,1,0:T(8,128)(2,1)S(1)}, bf16[2,64,512]{2,1,0:T(8,128)(2,1)S(1)}, u32[]{:S(2)}, u32[]{:S(2)}) collective-permute-start(bf16[2,64,512]{2,1,0:T(8,128)(2,1)S(1)} %slice.20), channel_id=1, source_target_pairs={{0,2},{2,4},{4,6},{6,7},{7,5},{5,3},{3,1},{1,0},{8,10},{10,12},{12... | collective-permute-start | bytes 393224 | tf_op jit(solution)/shard_map/ppermute | solution.py:152
  31.8 1.2 %and_select_fusion.picks = s32[2]{0:T(128)} fusion(s32[2]{0:T(128)S(1)} %gather_fusion, s32[]{:T(128)} %bitcast.10), kind=kLoop, calls=%fused_computation.9 | loop fusion | flops 24 | bytes 20 | tf_op jit(solution)/shard_map/jit(remainder)/select_n | solution.py:156
  33.1 1.6 %collective-permute-done.10.refs_8_ = bf16[2,64,512]{2,1,0:T(8,128)(2,1)S(1)} collective-permute-done((bf16[2,64,512]{2,1,0:T(8,128)(2,1)S(1)}, bf16[2,64,512]{2,1,0:T(8,128)(2,1)S(1)}, u32[]{:S(2)}, u32[]{:S(2)}) %collective-permute-start.10) | collective-permute-done | bytes 131104 | tf_op jit(solution)/shard_map/ppermute | solution.py:153
  34.7 0.7 %collective-permute-done.9.refs_7_ = bf16[2,64,512]{2,1,0:T(8,128)(2,1)S(1)} collective-permute-done((bf16[2,64,512]{2,1,0:T(8,128)(2,1)S(1)}, bf16[2,64,512]{2,1,0:T(8,128)(2,1)S(1)}, u32[]{:S(2)}, u32[]{:S(2)}) %collective-permute-start.9) | collective-permute-done | bytes 131104 | tf_op jit(solution)/shard_map/ppermute | solution.py:152
  35.3 0.6 copy-done.11
  36.0 2.7 %shard_map.91.refs_6_.refs_7_.refs_14_.refs_15_ = bf16[2,2,128,512]{3,2,1,0:T(8,128)(2,1)} custom-call(s32[2]{0:T(128)} %and_select_fusion.picks, bf16[2,128,512]{2,1,0:T(8,128)(2,1)} %copy-done.3, bf16[2,128,512]{2,1,0:T(8,128)(2,1)} %copy-done.7, bf16[2,128,512]{2,1,0:T(8,128)(2,1)} %copy-done.6, bf16[2,128,512]{2,1,0:T(8,128)(2,1)} %copy-done.9, ...), custom_call_target="tpu_custom_call" | custom-call | tf_op jit(solution)/shard_map/pallas_call | solution.py:117
  38.9 1.9 %collective-permute-start.2 = (bf16[2,128,512]{2,1,0:T(8,128)(2,1)S(1)}, bf16[2,128,512]{2,1,0:T(8,128)(2,1)S(1)}, u32[]{:S(2)}, u32[]{:S(2)}) collective-permute-start(bf16[2,128,512]{2,1,0:T(8,128)(2,1)S(1)} %broadcast_select_fusion), channel_id=1, source_target_pairs={{0,1},{1,2},{2,3},{3,4},{4,5},{5,6},{6,7},{7,0},{8,9},{9,10},{10,1... | collective-permute-start | bytes 786440 | tf_op jit(solution)/shard_map/ppermute | solution.py:28
  40.8 1.0 %collective-permute-start.1 = (bf16[2,128,512]{2,1,0:T(8,128)(2,1)S(1)}, bf16[2,128,512]{2,1,0:T(8,128)(2,1)S(1)}, u32[]{:S(2)}, u32[]{:S(2)}) collective-permute-start(bf16[2,128,512]{2,1,0:T(8,128)(2,1)S(1)} %collective-permute-done.refs_3_.refs_11_), channel_id=1, source_target_pairs={{0,1},{1,0},{2,3},{3,2},{4,5},{5,4},{6,7},{7,6},{8,9},{9,8},{10,11... | collective-permute-start | bytes 786440 | tf_op jit(solution)/shard_map/ppermute | solution.py:181
  42.4 0.6 %copy-done.14 = s32[2]{0:T(128)S(1)} copy-done((s32[2]{0:T(128)S(1)}, s32[2]{0:T(128)}, u32[]{:S(2)}) %copy-start.14) | copy-done | bytes 32
  43.0 0.7 %fusion.2 = (s32[1]{0:T(128)}, s32[1]{0:T(128)}) fusion(s32[2]{0:T(128)S(1)} %copy-done.14), kind=kLoop, calls=%fused_computation.15 | loop fusion | bytes 16 | tf_op jit(solution)/shard_map/slice | solution.py:199
  46.2 4.2 %collective-permute-done.2.refs_5_.refs_13_ = bf16[2,128,512]{2,1,0:T(8,128)(2,1)S(1)} collective-permute-done((bf16[2,128,512]{2,1,0:T(8,128)(2,1)S(1)}, bf16[2,128,512]{2,1,0:T(8,128)(2,1)S(1)}, u32[]{:S(2)}, u32[]{:S(2)}) %collective-permute-start.2) | collective-permute-done | bytes 262176 | tf_op jit(solution)/shard_map/ppermute | solution.py:28
  50.4 4.4 %collective-permute-done.1.refs_4_.refs_12_ = bf16[2,128,512]{2,1,0:T(8,128)(2,1)S(1)} collective-permute-done((bf16[2,128,512]{2,1,0:T(8,128)(2,1)S(1)}, bf16[2,128,512]{2,1,0:T(8,128)(2,1)S(1)}, u32[]{:S(2)}, u32[]{:S(2)}) %collective-permute-start.1) | collective-permute-done | bytes 262176 | tf_op jit(solution)/shard_map/ppermute | solution.py:181
  54.8 9.7 %shard_map.92 = bf16[128,4096]{1,0:T(8,128)(2,1)} custom-call(s32[8]{0:T(128)S(1)} %stack.39.refs_0_, bf16[128,4096]{1,0:T(8,128)(2,1)S(1)} %bitcast.12, bf16[2,128,512]{2,1,0:T(8,128)(2,1)S(1)} %constant_dynamic-update-slice_fusion.refs_2_.refs_10_, bf16[2,128,512]{2,1,0:T(8,128)(2,1)S(1)} %collective-permute-done.refs_3_.refs_11_, ...), custom_call_target="tpu_custom_call" | custom-call | tf_op jit(solution)/shard_map/pallas_call | solution.py:86
  (50 shorter events, 2.7 us)
Async XLA Ops:
  1.0 11.5 %copy-start.12 = (bf16[1,128,512]{2,1,0:T(8,128)(2,1)S(1)}, bf16[1,128,512]{2,1,0:T(8,128)(2,1)}, u32[]{:S(2)}) copy-start(bf16[1,128,512]{2,1,0:T(8,128)(2,1)} %param.10) | copy-start | bytes 393220
  1.0 21.3 %copy-start.3 = (bf16[2,128,512]{2,1,0:T(8,128)(2,1)}, bf16[2,128,512]{2,1,0:T(8,128)(2,1)S(1)}, u32[]{:S(2)}) copy-start(bf16[2,128,512]{2,1,0:T(8,128)(2,1)S(1)} %pad_maximum_fusion.refs_0_) | copy-start | bytes 786436
  1.0 11.5 %copy-start.13 = (bf16[1,128,512]{2,1,0:T(8,128)(2,1)S(1)}, bf16[1,128,512]{2,1,0:T(8,128)(2,1)}, u32[]{:S(2)}) copy-start(bf16[1,128,512]{2,1,0:T(8,128)(2,1)} %param.11) | copy-start | bytes 393220
  1.1 9.4 %collective-permute-start.4 = (bf16[2,128,512]{2,1,0:T(8,128)(2,1)S(1)}, bf16[2,128,512]{2,1,0:T(8,128)(2,1)S(1)}, u32[]{:S(2)}, u32[]{:S(2)}) collective-permute-start(bf16[2,128,512]{2,1,0:T(8,128)(2,1)S(1)} %pad_maximum_fusion.refs_0_), channel_id=1, source_target_pairs={{2,0},{4,2},{6,4},{7,6},{5,7},{3,5},{1,3},{0,1},{10,8},{12,10},{14... | collective-permute-start | bytes 786440 | tf_op jit(solution)/shard_map/ppermute | solution.py:147
  4.1 8.1 %collective-permute-start.3 = (bf16[2,128,512]{2,1,0:T(8,128)(2,1)S(1)}, bf16[2,128,512]{2,1,0:T(8,128)(2,1)S(1)}, u32[]{:S(2)}, u32[]{:S(2)}) collective-permute-start(bf16[2,128,512]{2,1,0:T(8,128)(2,1)S(1)} %pad_maximum_fusion.refs_0_), channel_id=1, source_target_pairs={{0,2},{2,4},{4,6},{6,7},{7,5},{5,3},{3,1},{1,0},{8,10},{10,12},{12... | collective-permute-start | bytes 786440 | tf_op jit(solution)/shard_map/ppermute | solution.py:146
  10.5 11.8 %copy-start.6 = (bf16[2,128,512]{2,1,0:T(8,128)(2,1)}, bf16[2,128,512]{2,1,0:T(8,128)(2,1)S(1)}, u32[]{:S(2)}) copy-start(bf16[2,128,512]{2,1,0:T(8,128)(2,1)S(1)} %collective-permute-done.4.refs_2_) | copy-start | bytes 786436
  10.5 7.5 %collective-permute-start.6 = (bf16[2,128,512]{2,1,0:T(8,128)(2,1)S(1)}, bf16[2,128,512]{2,1,0:T(8,128)(2,1)S(1)}, u32[]{:S(2)}, u32[]{:S(2)}) collective-permute-start(bf16[2,128,512]{2,1,0:T(8,128)(2,1)S(1)} %collective-permute-done.4.refs_2_), channel_id=1, source_target_pairs={{2,0},{4,2},{6,4},{7,6},{5,7},{3,5},{1,3},{0,1},{10,8},{12,10},{14... | collective-permute-start | bytes 786440 | tf_op jit(solution)/shard_map/ppermute | solution.py:147
  12.1 17.6 %copy-start.7 = (bf16[2,128,512]{2,1,0:T(8,128)(2,1)}, bf16[2,128,512]{2,1,0:T(8,128)(2,1)S(1)}, u32[]{:S(2)}) copy-start(bf16[2,128,512]{2,1,0:T(8,128)(2,1)S(1)} %collective-permute-done.3.refs_1_) | copy-start | bytes 786436
  12.1 8.3 %collective-permute-start.5 = (bf16[2,128,512]{2,1,0:T(8,128)(2,1)S(1)}, bf16[2,128,512]{2,1,0:T(8,128)(2,1)S(1)}, u32[]{:S(2)}, u32[]{:S(2)}) collective-permute-start(bf16[2,128,512]{2,1,0:T(8,128)(2,1)S(1)} %collective-permute-done.3.refs_1_), channel_id=1, source_target_pairs={{0,2},{2,4},{4,6},{6,7},{7,5},{5,3},{3,1},{1,0},{8,10},{10,12},{12... | collective-permute-start | bytes 786440 | tf_op jit(solution)/shard_map/ppermute | solution.py:146
  12.5 9.2 %copy-start.15 = (s32[2]{0:T(128)S(1)}, s32[2]{0:T(128)}, u32[]{:S(2)}) copy-start(s32[2]{0:T(128)} %param.15) | copy-start | bytes 28
  12.5 9.1 %copy-start.16 = (s32[2]{0:T(128)S(1)}, s32[2]{0:T(128)}, u32[]{:S(2)}) copy-start(s32[2]{0:T(128)} %param.16) | copy-start | bytes 28
  12.6 26.2 %collective-permute-start = (bf16[2,128,512]{2,1,0:T(8,128)(2,1)S(1)}, bf16[2,128,512]{2,1,0:T(8,128)(2,1)S(1)}, u32[]{:S(2)}, u32[]{:S(2)}) collective-permute-start(bf16[2,128,512]{2,1,0:T(8,128)(2,1)S(1)} %constant_dynamic-update-slice_fusion.refs_2_.refs_10_), channel_id=1, source_target_pairs={{0,2},{1,3},{2,4},{3,5},{4,6},{5,7},{6,0},{7,1},{8,10},{9,11},{10,... | collective-permute-start | bytes 786440 | tf_op jit(solution)/shard_map/ppermute | solution.py:28
  18.0 6.2 %copy-start.8 = (bf16[2,128,512]{2,1,0:T(8,128)(2,1)}, bf16[2,128,512]{2,1,0:T(8,128)(2,1)S(1)}, u32[]{:S(2)}) copy-start(bf16[2,128,512]{2,1,0:T(8,128)(2,1)S(1)} %collective-permute-done.6.refs_4_) | copy-start | bytes 786436
  18.0 11.6 %collective-permute-start.8 = (bf16[2,128,512]{2,1,0:T(8,128)(2,1)S(1)}, bf16[2,128,512]{2,1,0:T(8,128)(2,1)S(1)}, u32[]{:S(2)}, u32[]{:S(2)}) collective-permute-start(bf16[2,128,512]{2,1,0:T(8,128)(2,1)S(1)} %collective-permute-done.6.refs_4_), channel_id=1, source_target_pairs={{2,0},{4,2},{6,4},{7,6},{5,7},{3,5},{1,3},{0,1},{10,8},{12,10},{14... | collective-permute-start | bytes 786440 | tf_op jit(solution)/shard_map/ppermute | solution.py:147
  20.4 14.3 %copy-start.9 = (bf16[2,128,512]{2,1,0:T(8,128)(2,1)}, bf16[2,128,512]{2,1,0:T(8,128)(2,1)S(1)}, u32[]{:S(2)}) copy-start(bf16[2,128,512]{2,1,0:T(8,128)(2,1)S(1)} %collective-permute-done.5.refs_3_) | copy-start | bytes 786436
  20.4 9.3 %collective-permute-start.7 = (bf16[2,128,512]{2,1,0:T(8,128)(2,1)S(1)}, bf16[2,128,512]{2,1,0:T(8,128)(2,1)S(1)}, u32[]{:S(2)}, u32[]{:S(2)}) collective-permute-start(bf16[2,128,512]{2,1,0:T(8,128)(2,1)S(1)} %collective-permute-done.5.refs_3_), channel_id=1, source_target_pairs={{0,2},{2,4},{4,6},{6,7},{7,5},{5,3},{3,1},{1,0},{8,10},{10,12},{12... | collective-permute-start | bytes 786440 | tf_op jit(solution)/shard_map/ppermute | solution.py:146
  29.7 5.0 %collective-permute-start.10 = (bf16[2,64,512]{2,1,0:T(8,128)(2,1)S(1)}, bf16[2,64,512]{2,1,0:T(8,128)(2,1)S(1)}, u32[]{:S(2)}, u32[]{:S(2)}) collective-permute-start(bf16[2,64,512]{2,1,0:T(8,128)(2,1)S(1)} %slice.21), channel_id=1, source_target_pairs={{2,0},{4,2},{6,4},{7,6},{5,7},{3,5},{1,3},{0,1},{10,8},{12,10},{14... | collective-permute-start | bytes 393224 | tf_op jit(solution)/shard_map/ppermute | solution.py:153
  29.7 5.6 %copy-start.5 = (bf16[2,128,512]{2,1,0:T(8,128)(2,1)}, bf16[2,128,512]{2,1,0:T(8,128)(2,1)S(1)}, u32[]{:S(2)}) copy-start(bf16[2,128,512]{2,1,0:T(8,128)(2,1)S(1)} %collective-permute-done.7.refs_5_) | copy-start | bytes 786436
  30.4 5.0 %collective-permute-start.9 = (bf16[2,64,512]{2,1,0:T(8,128)(2,1)S(1)}, bf16[2,64,512]{2,1,0:T(8,128)(2,1)S(1)}, u32[]{:S(2)}, u32[]{:S(2)}) collective-permute-start(bf16[2,64,512]{2,1,0:T(8,128)(2,1)S(1)} %slice.20), channel_id=1, source_target_pairs={{0,2},{2,4},{4,6},{6,7},{7,5},{5,3},{3,1},{1,0},{8,10},{10,12},{12... | collective-permute-start | bytes 393224 | tf_op jit(solution)/shard_map/ppermute | solution.py:152
  36.0 18.8 %copy-start.1 = (bf16[1,128,4096]{2,1,0:T(8,128)(2,1)S(1)}, bf16[1,128,4096]{2,1,0:T(8,128)(2,1)}, u32[]{:S(2)}) copy-start(bf16[1,128,4096]{2,1,0:T(8,128)(2,1)} %param.9) | copy-start | bytes 3145732
  38.7 16.1 %copy-start = (bf16[2,2,128,512]{3,2,1,0:T(8,128)(2,1)S(1)}, bf16[2,2,128,512]{3,2,1,0:T(8,128)(2,1)}, u32[]{:S(2)}) copy-start(bf16[2,2,128,512]{3,2,1,0:T(8,128)(2,1)} %shard_map.91.refs_6_.refs_7_.refs_14_.refs_15_) | copy-start | bytes 1572868
  38.7 16.1 %collective-permute-start.11 = (bf16[2,2,128,512]{3,2,1,0:T(8,128)(2,1)}, bf16[2,2,128,512]{3,2,1,0:T(8,128)(2,1)S(1)}, u32[]{:S(2)}, u32[]{:S(2)}) collective-permute-start(bf16[2,2,128,512]{3,2,1,0:T(8,128)(2,1)} %shard_map.91.refs_6_.refs_7_.refs_14_.refs_15_), channel_id=1, source_target_pairs={{0,8},{8,0},{1,9},{9,1},{2,10},{10,2},{3,11},{11,3},{4,12},{12,4},... | collective-permute-start | bytes 1572872 | tf_op jit(solution)/shard_map/ppermute | solution.py:28
  38.9 11.5 %collective-permute-start.2 = (bf16[2,128,512]{2,1,0:T(8,128)(2,1)S(1)}, bf16[2,128,512]{2,1,0:T(8,128)(2,1)S(1)}, u32[]{:S(2)}, u32[]{:S(2)}) collective-permute-start(bf16[2,128,512]{2,1,0:T(8,128)(2,1)S(1)} %broadcast_select_fusion), channel_id=1, source_target_pairs={{0,1},{1,2},{2,3},{3,4},{4,5},{5,6},{6,7},{7,0},{8,9},{9,10},{10,1... | collective-permute-start | bytes 786440 | tf_op jit(solution)/shard_map/ppermute | solution.py:28
  40.8 14.0 %collective-permute-start.1 = (bf16[2,128,512]{2,1,0:T(8,128)(2,1)S(1)}, bf16[2,128,512]{2,1,0:T(8,128)(2,1)S(1)}, u32[]{:S(2)}, u32[]{:S(2)}) collective-permute-start(bf16[2,128,512]{2,1,0:T(8,128)(2,1)S(1)} %collective-permute-done.refs_3_.refs_11_), channel_id=1, source_target_pairs={{0,1},{1,0},{2,3},{3,2},{4,5},{5,4},{6,7},{7,6},{8,9},{9,8},{10,11... | collective-permute-start | bytes 786440 | tf_op jit(solution)/shard_map/ppermute | solution.py:181
  (5 other events, 3.3 us)

commit v2 on v0

v2 whole, which is shorter than its diff:
```python
import functools
import math

import jax
import jax.numpy as jnp
from jax import lax
from jax.experimental import pallas as pl
from jax.experimental.pallas import tpu as pltpu
from jax.sharding import PartitionSpec as P

HD = 128
HOPS = 3
DOCS = 2
RING_LIMIT = 16

NEGATIVE = -1e30
SCALE = math.log2(math.e) / math.sqrt(HD)


def broadcast(block, axis, source):
    block = jnp.where(lax.axis_index(axis) == source, block, jnp.zeros_like(block))
    return lax.psum(block, axis)


def shifted(value, axis, steps):
    count = lax.axis_size(axis)
    pairs = [(source, (source + steps) % count) for source in range(count)]
    return lax.ppermute(value, axis, pairs)

def score_tile(block, keys, values, carried, causal, begin, end):
    scores = lax.dot_general(
        block, keys[...], (((1,), (1,)), ((), ())), preferred_element_type=jnp.float32
    )
    if causal is not None:
        masked = jnp.where(causal, scores[:, begin:end], NEGATIVE)
        pieces = [scores[:, :begin], masked, scores[:, end:]]
        scores = jnp.concatenate([piece for piece in pieces if piece.shape[1]], axis=1)
    highest = jnp.max(scores, axis=1, keepdims=True) * SCALE
    if carried is not None:
        highest = jnp.maximum(highest, carried[:, :1])
    weights = jnp.exp2(scores * SCALE - highest).astype(jnp.bfloat16)
    return jnp.dot(weights, values[...], preferred_element_type=jnp.float32), highest


def bias_rows(keys, start, height, live):
    lane = lax.broadcasted_iota(jnp.int32, (height, HD), 1)
    row = lax.broadcasted_iota(jnp.int32, (height, HD), 0)
    dead = (row >= live) & (lane == 0)
    keys[start : start + height, HD:] = jnp.where(dead, NEGATIVE, 0.0).astype(jnp.bfloat16)


def query_tile(q_ref, head, tile):
    heads = [q_ref[:, (head + i) * HD : (head + i + 1) * HD] for i in range(tile)]
    rows = jnp.concatenate(heads, axis=0)
    lane = lax.broadcasted_iota(jnp.int32, rows.shape, 1)
    return jnp.concatenate([rows, jnp.where(lane == 0, 1.0, 0.0).astype(jnp.bfloat16)], axis=1)


def ring_place(index, count):
    return jnp.where(index % 2 == 0, index // 2, count - 1 - index // 2)


def window_body(group, tile, offsets, q_ref, own, two, swapped, passed, out_ref, log_ref, keys, values):
    count = lax.axis_size("ctx")
    tokens = q_ref.shape[0]
    position = lax.axis_index("ctx")
    placed = lax.rem(position - offsets[lax.axis_index("req")] + count, count)
    even = lax.rem(position, 2) == 0
    hops = (0, 2, jnp.where(even, 1, HOPS), jnp.where(even, HOPS, 1))

    @pl.when(pl.program_id(0) == 0)
    def _():
        values[:, HD:] = jnp.ones((values.shape[0], HD), jnp.bfloat16)
        for number, hop in enumerate(hops):
            bias_rows(keys, number * tokens, tokens, jnp.where(placed >= hop, tokens, 0))

    for number, ref in enumerate((own, two, swapped, passed)):
        keys[number * tokens : (number + 1) * tokens, :HD] = ref[0]
        values[number * tokens : (number + 1) * tokens, :HD] = ref[1]

    query = lax.broadcasted_iota(jnp.int32, (tokens, tokens), 0)
    key = lax.broadcasted_iota(jnp.int32, (tokens, tokens), 1)
    causal = jnp.concatenate([key <= query] * tile, axis=0)
    for head in range(0, group, tile):
        block = query_tile(q_ref, head, tile)
        summed, highest = score_tile(block, keys, values, None, causal, 0, tokens)
        rows = slice(head * tokens, (head + tile) * tokens)
        out_ref[0, rows] = summed[:, :HD] / summed[:, HD:]
        log_ref[0, rows] = highest + jnp.log2(summed[:, HD:])


def document_body(
    group, tile, count, ring, owners, lengths, q_ref, in_ref, log_ref, *refs
):
    pieces = refs[:count]
    out_ref, keys, values = refs[count:]
    tokens = q_ref.shape[0]
    height = keys.shape[0] // DOCS
    head_index = pl.program_id(0)

    @pl.when(head_index == 0)
    def _():
        values[:, HD:] = jnp.ones((values.shape[0], HD), jnp.bfloat16)
        for number in range(DOCS):
            bias_rows(keys, number * height, height, lengths[number])

    columns = pl.ds(pl.multiple_of(head_index * HD, HD), HD)
    for number in range(DOCS):
        if ring:
            slots = lax.axis_size("ctx")
            gap = ring_place(lax.axis_index("ctx"), slots) - ring_place(owners[number], slots)
            gap = jnp.where(lax.axis_index("req") == 0, gap, -gap)
            gap = jnp.where(gap < 0, gap + slots, gap)
        rows = slice(number * height, (number + 1) * height)
        for index, piece in enumerate(pieces):

            @pl.when((gap if ring else number) == index)
            def _():
                keys[rows, :HD] = piece[0, :, columns]
                values[rows, :HD] = piece[1, :, columns]

    for head in range(0, group, tile):
        block = query_tile(q_ref, head, tile)
        rows = slice(head * tokens, (head + tile) * tokens)
        log = log_ref[0, rows]
        summed, highest = score_tile(block, keys, values, log, None, 0, 0)
        share = jnp.exp2(log - highest)
        total = summed[:, :HD] + in_ref[0, rows] * share
        result = (total / (summed[:, HD:] + share)).astype(jnp.bfloat16)
        for i in range(tile):
            out_ref[:, (head + i) * HD : (head + i + 1) * HD] = result[i * tokens : (i + 1) * tokens]


def attend_window(queries, blocks, block_offsets):
    tokens, width = queries.shape
    kv_heads = blocks[0].shape[-1] // HD
    group = width // HD // kv_heads
    rows = group * tokens
    partial = pl.BlockSpec((1, rows, HD), lambda g, *s: (g, 0, 0))
    total = len(blocks) * tokens
    return pl.pallas_call(
        functools.partial(window_body, group, 2 if group % 2 == 0 else 1),
        out_shape=[jax.ShapeDtypeStruct((kv_heads, rows, HD), jnp.float32)] * 2,
        grid_spec=pltpu.PrefetchScalarGridSpec(
            num_scalar_prefetch=1,
            grid=(kv_heads,),
            in_specs=[pl.BlockSpec((tokens, group * HD), lambda g, *s: (0, g))]
            + [pl.BlockSpec((2, tokens, HD), lambda g, *s: (0, 0, g))] * len(blocks),
            out_specs=[partial] * 2,
            scratch_shapes=[pltpu.VMEM((total, 2 * HD), jnp.bfloat16)] * 2,
        ),
        compiler_params=pltpu.CompilerParams(vmem_limit_bytes=32 << 20),
        cost_estimate=pl.CostEstimate(
            flops=4 * kv_heads * rows * total * HD,
            bytes_accessed=8 * kv_heads * rows * HD,
            transcendentals=kv_heads * rows * total,
        ),
        name="window",
    )(block_offsets, queries, *blocks)


def attend_documents(queries, partials, pieces, ring, doc_owners, doc_lengths):
    tokens, width = queries.shape
    doc_rows, kv_width = pieces[0].shape[1:]
    kv_heads = kv_width // HD
    group = width // HD // kv_heads
    rows = group * tokens
    heads = pl.BlockSpec((tokens, group * HD), lambda g, *s: (0, g))
    partial = pl.BlockSpec((1, rows, HD), lambda g, *s: (g, 0, 0))
    total = DOCS * doc_rows
    return pl.pallas_call(
        functools.partial(document_body, group, 2 if group % 2 == 0 else 1, len(pieces), ring),
        out_shape=jax.ShapeDtypeStruct((tokens, width), jnp.bfloat16),
        grid_spec=pltpu.PrefetchScalarGridSpec(
            num_scalar_prefetch=2,
            grid=(kv_heads,),
            in_specs=[heads, partial, partial]
            + [pl.BlockSpec(memory_space=pltpu.VMEM)] * len(pieces),
            out_specs=heads,
            scratch_shapes=[pltpu.VMEM((total, 2 * HD), jnp.bfloat16)] * 2,
        ),
        compiler_params=pltpu.CompilerParams(vmem_limit_bytes=32 << 20),
        cost_estimate=pl.CostEstimate(
            flops=4 * kv_heads * rows * total * HD,
            bytes_accessed=8 * kv_heads * rows * HD,
            transcendentals=kv_heads * rows * total,
        ),
        name="documents",
    )(doc_owners, doc_lengths, queries, *partials, *pieces)


def per_device(
    queries, keys, values, cache_keys, cache_values, doc_lengths, doc_owners, block_offsets
):
    count = lax.axis_size("ctx")
    even = lax.axis_index("ctx") % 2 == 0
    ring = lax.axis_size("req") == 2 and count <= RING_LIMIT
    slot = jnp.stack([cache_keys[0], cache_values[0]])
    own = jnp.stack([keys[0], values[0]])

    if ring:
        order = list(range(0, count, 2)) + list(range(1, count, 2))[::-1]
        onward = [(order[i], order[(i + 1) % count]) for i in range(count)]
        both = onward + [(count + target, count + source) for source, target in onward]
        pieces = [slot] + [None] * (count - 1)
        for step in range(1, count // 2 + 1):
            with jax.named_scope(f"ring{step}"):
                pieces[step] = lax.ppermute(pieces[step - 1], ("req", "ctx"), both)
            if 2 * step < count:
                with jax.named_scope(f"exchange{step}"):
                    pieces[count - step] = shifted(pieces[step], "req", 1)
    else:
        pieces = [broadcast(slot, "ctx", doc_owners[number]) for number in range(DOCS)]

    with jax.named_scope("two"):
        two = shifted(own, "ctx", 2)
    with jax.named_scope("swapped"):
        swapped = lax.ppermute(two, "ctx", [(i, i ^ 1) for i in range(count)])
    with jax.named_scope("passed"):
        passed = shifted(jnp.where(even, own, two), "ctx", 1)

    partials = attend_window(queries[0], (own, two, swapped, passed), block_offsets)
    attended = attend_documents(queries[0], partials, pieces, ring, doc_owners, doc_lengths)
    return attended[None]


def solution(mesh):
    return jax.shard_map(
        per_device,
        mesh=mesh,
        in_specs=(
            P(("groups", "req"), "ctx", None),
            P(("groups", "req"), "ctx", None),
            P(("groups", "req"), "ctx", None),
            P(("groups", "ctx"), None, None),
            P(("groups", "ctx"), None, None),
            P("groups"),
            P("groups"),
            P("groups"),
        ),
        out_specs=P(("groups", "req"), "ctx", None),
        check_vma=False,
    )
```

time: 131 us -> 68 us (0.52)
  matrix products: 32.1 us -> 0 us
  waiting for transfers between devices: 50.9 us -> 33.1 us
  between operations: 16.1 us -> 0.1 us
  Pallas kernels: 0 us -> 14 us
  local copies, waits for them, and re-layouts: 17.4 us -> 3.87 us
  starting transfers between devices: 4.57 us -> 16.7 us
  other arithmetic: 8.85 us -> 0.03 us
    psum x1 -> x0, waiting for transfers between devices: 32.8 us -> none  [broadcast(): return lax.psum(block, axis)]
    dot_general x48 -> x0, matrix products: 32.1 us -> none  [the longest x24 25.1 us: merge_block(): jnp.einsum('tid,sd->its', query_rows, key_rows, preferred_element_type=jn...]
    ppermute x3 -> x10, waiting for transfers between devices: 18.1 us -> 33.1 us  [the longest x4 13.6 us: per_device(): pieces[step] = lax.ppermute(pieces[step - 1], ('req', 'ctx'), both)]
    pallas_call x0 -> x2, Pallas kernels: none -> 14 us  [the longest x1 7.96 us: attend_documents(): pl.pallas_call(functools.partial(document_body, group, 2 if group % 2 ==...]
    ppermute x3 -> x10, starting transfers between devices: 4.57 us -> 16.7 us  [the longest x4 9.72 us: per_device(): pieces[step] = lax.ppermute(pieces[step - 1], ('req', 'ctx'), both)]
    unnamed x81 -> x10, local copies, waits for them, and re-layouts: 12.8 us -> 1.99 us
    reduce_sum x16 -> x0, other arithmetic: 4.05 us -> none  [the longest x15 3.35 us: merge_block(): totals = totals * shrink + jnp.sum(weights, axis=-1)]
    lt x2 -> x0, other arithmetic: 2.41 us -> none  [per_device(): jnp.arange(doc_rows)[None, :] < doc_lengths[number]]
  transfers between devices with their start and end apart: 4 -> 10, of which waited for: 3 -> 6; matrix products, arithmetic and copies ran while one was open for 23% -> 3% of each run, Pallas kernels for 0% -> 9%
where the time goes in v2:
time: 68 us; the launch traced here: 67.8 us
  waiting for transfers between devices  33.1 us (49%)
  starting transfers between devices  16.7 us (25%)
  Pallas kernels  14 us (21%)
  local copies, waits for them, and re-layouts  3.87 us (6%)
    ppermute x4, waiting for transfers between devices, per_device(): pieces[step] = lax.ppermute(pieces[step - 1], ('req', 'ctx'), both)  13.6 us
    ppermute x1, waiting for transfers between devices, per_device(): swapped = lax.ppermute(two, 'ctx', [(i, i ^ 1) for i in range(count)])  11.1 us
    ppermute x4, starting transfers between devices, per_device(): pieces[step] = lax.ppermute(pieces[step - 1], ('req', 'ctx'), both)  9.72 us
    ppermute x5, waiting for transfers between devices, shifted(): return lax.ppermute(value, axis, pairs)  8.37 us
    pallas_call x1, Pallas kernels, attend_documents(): pl.pallas_call(functools.partial(document_body, group, 2 if group % 2 ==...  7.96 us
    ppermute x5, starting transfers between devices, shifted(): return lax.ppermute(value, axis, pairs)  7.02 us
    pallas_call x1, Pallas kernels, attend_window(): pl.pallas_call(functools.partial(window_body, group, 2 if group % 2 == 0...  6 us
    unnamed x10, local copies, waits for them, and re-layouts  1.99 us
  transfers between devices with their start and end apart: 10, of which 6 were waited for; matrix products, arithmetic and copies ran while one was open for 3% of the time, Pallas kernels for 9%

profile of v2, /device:TPU:0, one launch (start us, length us, event | category | flops | bytes accessed | tf_op | source)
XLA Modules:
  0.0 67.8 jit_solution(10615302331404433868)
XLA Ops:
  0.0 1.1 %constant_dynamic-update-slice_fusion.3 = bf16[2,256,512]{2,1,0:T(8,128)(2,1)S(1)} fusion(bf16[1,256,512]{2,1,0:T(8,128)(2,1)} %param.11), kind=kLoop, calls=%fused_computation.4 | loop fusion | bytes 524288
  1.1 1.0 %constant_dynamic-update-slice_fusion.2.refs_0_ = bf16[2,256,512]{2,1,0:T(8,128)(2,1)S(1)} fusion(bf16[2,256,512]{2,1,0:T(8,128)(2,1)S(1)} %constant_dynamic-update-slice_fusion.3, bf16[1,256,512]{2,1,0:T(8,128)(2,1)} %param.12), kind=kLoop, calls=%fused_computation.3 | loop fusion | bytes 524288 | tf_op jit(solution)/shard_map/stack | solution.py:198
  2.0 3.1 %collective-permute-start.3 = (bf16[2,256,512]{2,1,0:T(8,128)(2,1)S(1)}, bf16[2,256,512]{2,1,0:T(8,128)(2,1)S(1)}, u32[]{:S(2)}, u32[]{:S(2)}) collective-permute-start(bf16[2,256,512]{2,1,0:T(8,128)(2,1)S(1)} %constant_dynamic-update-slice_fusion.2.refs_0_), channel_id=1, source_target_pairs={{0,2},{2,4},{4,6},{6,7},{7,5},{5,3},{3,1},{1,0},{10,8},{12,10},{14... | collective-permute-start | bytes 1572872 | tf_op jit(solution)/shard_map/ring1/ppermute | solution.py:208
  5.1 7.1 %collective-permute-done.3.refs_1_ = bf16[2,256,512]{2,1,0:T(8,128)(2,1)S(1)} collective-permute-done((bf16[2,256,512]{2,1,0:T(8,128)(2,1)S(1)}, bf16[2,256,512]{2,1,0:T(8,128)(2,1)S(1)}, u32[]{:S(2)}, u32[]{:S(2)}) %collective-permute-start.3) | collective-permute-done | bytes 524320 | tf_op jit(solution)/shard_map/ring1/ppermute | solution.py:208
  12.2 2.1 %collective-permute-start.4 = (bf16[2,256,512]{2,1,0:T(8,128)(2,1)S(1)}, bf16[2,256,512]{2,1,0:T(8,128)(2,1)S(1)}, u32[]{:S(2)}, u32[]{:S(2)}) collective-permute-start(bf16[2,256,512]{2,1,0:T(8,128)(2,1)S(1)} %collective-permute-done.3.refs_1_), channel_id=1, source_target_pairs={{0,2},{2,4},{4,6},{6,7},{7,5},{5,3},{3,1},{1,0},{10,8},{12,10},{14... | collective-permute-start | bytes 1572872 | tf_op jit(solution)/shard_map/ring2/ppermute | solution.py:208
  14.3 0.9 %constant_dynamic-update-slice_fusion.1 = bf16[2,128,512]{2,1,0:T(8,128)(2,1)S(1)} fusion(bf16[1,128,512]{2,1,0:T(8,128)(2,1)} %param.9), kind=kLoop, calls=%fused_computation.2 | loop fusion | bytes 262144
  15.2 0.9 %constant_dynamic-update-slice_fusion.own = bf16[2,128,512]{2,1,0:T(8,128)(2,1)S(1)} fusion(bf16[2,128,512]{2,1,0:T(8,128)(2,1)S(1)} %constant_dynamic-update-slice_fusion.1, bf16[1,128,512]{2,1,0:T(8,128)(2,1)} %param.10), kind=kLoop, calls=%fused_computation.1 | loop fusion | bytes 262144 | tf_op jit(solution)/shard_map/stack | solution.py:199
  16.2 1.6 %collective-permute-start = (bf16[2,128,512]{2,1,0:T(8,128)(2,1)S(1)}, bf16[2,128,512]{2,1,0:T(8,128)(2,1)}, u32[]{:S(2)}, u32[]{:S(2)}) collective-permute-start(bf16[2,128,512]{2,1,0:T(8,128)(2,1)S(1)} %constant_dynamic-update-slice_fusion.own), channel_id=1, source_target_pairs={{0,2},{1,3},{2,4},{3,5},{4,6},{5,7},{6,0},{7,1},{8,10},{9,11},{10,... | collective-permute-start | bytes 786440 | tf_op jit(solution)/shard_map/two/ppermute | solution.py:28
  17.8 5.9 %collective-permute-done.4.refs_2_ = bf16[2,256,512]{2,1,0:T(8,128)(2,1)S(1)} collective-permute-done((bf16[2,256,512]{2,1,0:T(8,128)(2,1)S(1)}, bf16[2,256,512]{2,1,0:T(8,128)(2,1)S(1)}, u32[]{:S(2)}, u32[]{:S(2)}) %collective-permute-start.4) | collective-permute-done | bytes 524320 | tf_op jit(solution)/shard_map/ring2/ppermute | solution.py:208
  23.7 2.5 %collective-permute-start.5 = (bf16[2,256,512]{2,1,0:T(8,128)(2,1)S(1)}, bf16[2,256,512]{2,1,0:T(8,128)(2,1)S(1)}, u32[]{:S(2)}, u32[]{:S(2)}) collective-permute-start(bf16[2,256,512]{2,1,0:T(8,128)(2,1)S(1)} %collective-permute-done.4.refs_2_), channel_id=1, source_target_pairs={{0,2},{2,4},{4,6},{6,7},{7,5},{5,3},{3,1},{1,0},{10,8},{12,10},{14... | collective-permute-start | bytes 1572872 | tf_op jit(solution)/shard_map/ring3/ppermute | solution.py:208
  26.2 1.2 %collective-permute-done.two = bf16[2,128,512]{2,1,0:T(8,128)(2,1)} collective-permute-done((bf16[2,128,512]{2,1,0:T(8,128)(2,1)S(1)}, bf16[2,128,512]{2,1,0:T(8,128)(2,1)}, u32[]{:S(2)}, u32[]{:S(2)}) %collective-permute-start) | collective-permute-done | bytes 262176 | tf_op jit(solution)/shard_map/two/ppermute | solution.py:28
  27.4 0.0 copy-start.1
  27.4 0.0 copy-start.2
  27.5 4.9 %collective-permute-start.2 = (bf16[2,128,512]{2,1,0:T(8,128)(2,1)S(1)}, bf16[2,128,512]{2,1,0:T(8,128)(2,1)S(1)}, u32[]{:S(2)}, u32[]{:S(2)}) collective-permute-start(bf16[2,128,512]{2,1,0:T(8,128)(2,1)S(1)} %broadcast_select_fusion), channel_id=1, source_target_pairs={{0,1},{1,2},{2,3},{3,4},{4,5},{5,6},{6,7},{7,0},{8,9},{9,10},{10,1... | collective-permute-start | bytes 786440 | tf_op jit(solution)/shard_map/passed/ppermute | solution.py:28
  32.3 0.0 collective-permute-start.9
  32.3 0.5 collective-permute-start.8
  32.8 0.5 collective-permute-done.5.refs_3_
  33.4 2.0 %collective-permute-start.6 = (bf16[2,256,512]{2,1,0:T(8,128)(2,1)S(1)}, bf16[2,256,512]{2,1,0:T(8,128)(2,1)S(1)}, u32[]{:S(2)}, u32[]{:S(2)}) collective-permute-start(bf16[2,256,512]{2,1,0:T(8,128)(2,1)S(1)} %collective-permute-done.5.refs_3_), channel_id=1, source_target_pairs={{0,2},{2,4},{4,6},{6,7},{7,5},{5,3},{3,1},{1,0},{10,8},{12,10},{14... | collective-permute-start | bytes 1572872 | tf_op jit(solution)/shard_map/ring4/ppermute | solution.py:208
  35.4 0.0 collective-permute-start.7
  35.4 7.2 %collective-permute-done.2.passed = bf16[2,128,512]{2,1,0:T(8,128)(2,1)S(1)} collective-permute-done((bf16[2,128,512]{2,1,0:T(8,128)(2,1)S(1)}, bf16[2,128,512]{2,1,0:T(8,128)(2,1)S(1)}, u32[]{:S(2)}, u32[]{:S(2)}) %collective-permute-start.2) | collective-permute-done | bytes 262176 | tf_op jit(solution)/shard_map/passed/ppermute | solution.py:28
  42.6 11.1 %collective-permute-done.1.swapped = bf16[2,128,512]{2,1,0:T(8,128)(2,1)S(1)} collective-permute-done((bf16[2,128,512]{2,1,0:T(8,128)(2,1)}, bf16[2,128,512]{2,1,0:T(8,128)(2,1)S(1)}, u32[]{:S(2)}, u32[]{:S(2)}) %collective-permute-start.1) | collective-permute-done | bytes 262176 | tf_op jit(solution)/shard_map/swapped/ppermute | solution.py:218
  53.7 6.0 %window.1 = (f32[4,1024,128]{2,1,0:T(8,128)S(1)}, f32[4,1024,128]{2,1,0:T(8,128)S(1)}) custom-call(s32[2]{0:T(128)S(1)} %copy-done.3, bf16[128,4096]{1,0:T(8,128)(2,1)S(1)} %bitcast.2, bf16[2,128,512]{2,1,0:T(8,128)(2,1)S(1)} %constant_dynamic-update-slice_fusion.own, bf16[2,128,512]{2,1,0:T(8,128)(2,1)} %collective-permute-done.two, ...), custom_call_target="tpu_custom_call" | custom-call | flops 1073741824 | bytes 4194304 | tf_op jit(solution)/shard_map/window/pallas_call | solution.py:141
  59.7 0.0 collective-permute-done.9.refs_7_
  59.8 8.0 %documents.1 = bf16[128,4096]{1,0:T(8,128)(2,1)} custom-call(s32[2]{0:T(128)S(1)} %copy-done.1, s32[2]{0:T(128)S(1)} %copy-done.2, bf16[128,4096]{1,0:T(8,128)(2,1)S(1)} %bitcast.3, f32[4,1024,128]{2,1,0:T(8,128)S(1)} %get-tuple-element.7.in_ref, f32[4,1024,128]{2,1,0:T(8,128)S(1)} %get-tuple-element.8.log_ref, ...), custom_call_target="tpu_custom_call" | custom-call | flops 1073741824 | bytes 4194304 | tf_op jit(solution)/shard_map/documents/pallas_call | solution.py:171
  (11 shorter events, 0.1 us)
Async XLA Ops:
  0.0 53.7 %copy-start = (bf16[1,128,4096]{2,1,0:T(8,128)(2,1)S(1)}, bf16[1,128,4096]{2,1,0:T(8,128)(2,1)}, u32[]{:S(2)}) copy-start(bf16[1,128,4096]{2,1,0:T(8,128)(2,1)} %param.8) | copy-start | bytes 3145732
  0.0 53.7 %copy-start.3 = (s32[2]{0:T(128)S(1)}, s32[2]{0:T(128)}, u32[]{:S(2)}) copy-start(s32[2]{0:T(128)} %offsets.1) | copy-start | bytes 28
  2.0 10.2 %collective-permute-start.3 = (bf16[2,256,512]{2,1,0:T(8,128)(2,1)S(1)}, bf16[2,256,512]{2,1,0:T(8,128)(2,1)S(1)}, u32[]{:S(2)}, u32[]{:S(2)}) collective-permute-start(bf16[2,256,512]{2,1,0:T(8,128)(2,1)S(1)} %constant_dynamic-update-slice_fusion.2.refs_0_), channel_id=1, source_target_pairs={{0,2},{2,4},{4,6},{6,7},{7,5},{5,3},{3,1},{1,0},{10,8},{12,10},{14... | collective-permute-start | bytes 1572872 | tf_op jit(solution)/shard_map/ring1/ppermute | solution.py:208
  12.2 11.5 %collective-permute-start.4 = (bf16[2,256,512]{2,1,0:T(8,128)(2,1)S(1)}, bf16[2,256,512]{2,1,0:T(8,128)(2,1)S(1)}, u32[]{:S(2)}, u32[]{:S(2)}) collective-permute-start(bf16[2,256,512]{2,1,0:T(8,128)(2,1)S(1)} %collective-permute-done.3.refs_1_), channel_id=1, source_target_pairs={{0,2},{2,4},{4,6},{6,7},{7,5},{5,3},{3,1},{1,0},{10,8},{12,10},{14... | collective-permute-start | bytes 1572872 | tf_op jit(solution)/shard_map/ring2/ppermute | solution.py:208
  16.2 11.2 %collective-permute-start = (bf16[2,128,512]{2,1,0:T(8,128)(2,1)S(1)}, bf16[2,128,512]{2,1,0:T(8,128)(2,1)}, u32[]{:S(2)}, u32[]{:S(2)}) collective-permute-start(bf16[2,128,512]{2,1,0:T(8,128)(2,1)S(1)} %constant_dynamic-update-slice_fusion.own), channel_id=1, source_target_pairs={{0,2},{1,3},{2,4},{3,5},{4,6},{5,7},{6,0},{7,1},{8,10},{9,11},{10,... | collective-permute-start | bytes 786440 | tf_op jit(solution)/shard_map/two/ppermute | solution.py:28
  23.7 9.6 %collective-permute-start.5 = (bf16[2,256,512]{2,1,0:T(8,128)(2,1)S(1)}, bf16[2,256,512]{2,1,0:T(8,128)(2,1)S(1)}, u32[]{:S(2)}, u32[]{:S(2)}) collective-permute-start(bf16[2,256,512]{2,1,0:T(8,128)(2,1)S(1)} %collective-permute-done.4.refs_2_), channel_id=1, source_target_pairs={{0,2},{2,4},{4,6},{6,7},{7,5},{5,3},{3,1},{1,0},{10,8},{12,10},{14... | collective-permute-start | bytes 1572872 | tf_op jit(solution)/shard_map/ring3/ppermute | solution.py:208
  27.4 32.4 %copy-start.1 = (s32[2]{0:T(128)S(1)}, s32[2]{0:T(128)}, u32[]{:S(2)}) copy-start(s32[2]{0:T(128)} %owners.1) | copy-start | bytes 28
  27.4 32.3 %copy-start.2 = (s32[2]{0:T(128)S(1)}, s32[2]{0:T(128)}, u32[]{:S(2)}) copy-start(s32[2]{0:T(128)} %lengths.1) | copy-start | bytes 28
  27.5 15.1 %collective-permute-start.2 = (bf16[2,128,512]{2,1,0:T(8,128)(2,1)S(1)}, bf16[2,128,512]{2,1,0:T(8,128)(2,1)S(1)}, u32[]{:S(2)}, u32[]{:S(2)}) collective-permute-start(bf16[2,128,512]{2,1,0:T(8,128)(2,1)S(1)} %broadcast_select_fusion), channel_id=1, source_target_pairs={{0,1},{1,2},{2,3},{3,4},{4,5},{5,6},{6,7},{7,0},{8,9},{9,10},{10,1... | collective-permute-start | bytes 786440 | tf_op jit(solution)/shard_map/passed/ppermute | solution.py:28
  32.3 27.4 %collective-permute-start.9 = (bf16[2,256,512]{2,1,0:T(8,128)(2,1)S(1)}, bf16[2,256,512]{2,1,0:T(8,128)(2,1)S(1)}, u32[]{:S(2)}, u32[]{:S(2)}) collective-permute-start(bf16[2,256,512]{2,1,0:T(8,128)(2,1)S(1)} %collective-permute-done.3.refs_1_), channel_id=1, source_target_pairs={{0,8},{8,0},{1,9},{9,1},{2,10},{10,2},{3,11},{11,3},{4,12},{12,4},... | collective-permute-start | bytes 1572872 | tf_op jit(solution)/shard_map/exchange1/ppermute | solution.py:28
  32.3 27.4 %collective-permute-start.8 = (bf16[2,256,512]{2,1,0:T(8,128)(2,1)S(1)}, bf16[2,256,512]{2,1,0:T(8,128)(2,1)S(1)}, u32[]{:S(2)}, u32[]{:S(2)}) collective-permute-start(bf16[2,256,512]{2,1,0:T(8,128)(2,1)S(1)} %collective-permute-done.4.refs_2_), channel_id=1, source_target_pairs={{0,8},{8,0},{1,9},{9,1},{2,10},{10,2},{3,11},{11,3},{4,12},{12,4},... | collective-permute-start | bytes 1572872 | tf_op jit(solution)/shard_map/exchange2/ppermute | solution.py:28
  33.4 26.4 %collective-permute-start.6 = (bf16[2,256,512]{2,1,0:T(8,128)(2,1)S(1)}, bf16[2,256,512]{2,1,0:T(8,128)(2,1)S(1)}, u32[]{:S(2)}, u32[]{:S(2)}) collective-permute-start(bf16[2,256,512]{2,1,0:T(8,128)(2,1)S(1)} %collective-permute-done.5.refs_3_), channel_id=1, source_target_pairs={{0,2},{2,4},{4,6},{6,7},{7,5},{5,3},{3,1},{1,0},{10,8},{12,10},{14... | collective-permute-start | bytes 1572872 | tf_op jit(solution)/shard_map/ring4/ppermute | solution.py:208
  35.4 24.4 %collective-permute-start.7 = (bf16[2,256,512]{2,1,0:T(8,128)(2,1)S(1)}, bf16[2,256,512]{2,1,0:T(8,128)(2,1)S(1)}, u32[]{:S(2)}, u32[]{:S(2)}) collective-permute-start(bf16[2,256,512]{2,1,0:T(8,128)(2,1)S(1)} %collective-permute-done.5.refs_3_), channel_id=1, source_target_pairs={{0,8},{8,0},{1,9},{9,1},{2,10},{10,2},{3,11},{11,3},{4,12},{12,4},... | collective-permute-start | bytes 1572872 | tf_op jit(solution)/shard_map/exchange3/ppermute | solution.py:28
  42.6 11.1 %collective-permute-start.1 = (bf16[2,128,512]{2,1,0:T(8,128)(2,1)}, bf16[2,128,512]{2,1,0:T(8,128)(2,1)S(1)}, u32[]{:S(2)}, u32[]{:S(2)}) collective-permute-start(bf16[2,128,512]{2,1,0:T(8,128)(2,1)} %collective-permute-done.two), channel_id=1, source_target_pairs={{0,1},{1,0},{2,3},{3,2},{4,5},{5,4},{6,7},{7,6},{8,9},{9,8},{10,11... | collective-permute-start | bytes 786440 | tf_op jit(solution)/shard_map/swapped/ppermute | solution.py:218

commit v3 on v0

v3 whole, which is shorter than its diff:
```python
import functools
import math

import jax
import jax.numpy as jnp
from jax import lax
from jax.experimental import pallas as pl
from jax.experimental.pallas import tpu as pltpu
from jax.sharding import PartitionSpec as P


HD = 128
DOCS = 2
TILE = {"near": 2, "middle": 2, "far": 4}
RING_LIMIT = 16

NEGATIVE = -1e30
SCALE = math.log2(math.e) / math.sqrt(HD)


def broadcast(block, axis, source):
    block = jnp.where(lax.axis_index(axis) == source, block, jnp.zeros_like(block))
    return lax.psum(block, axis)


def shifted(value, axis, steps):
    count = lax.axis_size(axis)
    pairs = [(source, (source + steps) % count) for source in range(count)]
    return lax.ppermute(value, axis, pairs)


def bias_rows(keys, start, height, live):
    lane = lax.broadcasted_iota(jnp.int32, (height, HD), 1)
    row = lax.broadcasted_iota(jnp.int32, (height, HD), 0)
    dead = (row >= live) & (lane == 0)
    keys[start : start + height, HD:] = jnp.where(dead, NEGATIVE, 0.0).astype(jnp.bfloat16)


def ring_place(index, count):
    return jnp.where(index % 2 == 0, index // 2, count - 1 - index // 2)


def slot_gap(owner):
    count = lax.axis_size("ctx")
    gap = ring_place(lax.axis_index("ctx"), count) - ring_place(owner, count)
    gap = jnp.where(lax.axis_index("req") == 0, gap, -gap)
    return jnp.where(gap < 0, gap + count, gap)


def attention_body(group, tile, hops, labels, which, carried, final, scalars, *refs):
    requests = scalars.shape[0] - 2 * DOCS
    offsets = scalars
    owners = [scalars[requests + number] for number in range(DOCS)]
    refs = list(refs)
    take = lambda number: [refs.pop(0) for _ in range(number)]
    (q_ref,) = take(1)
    blocks = take(len(hops))
    slots = [take(2) for _ in labels] if which else []
    before = take(3) if carried else None
    (out_ref,) = take(1)
    sum_ref, top_ref = (None, None) if final else take(2)
    keys, values = refs
    tokens = q_ref.shape[0]
    height = slots[0][0].shape[0] if which else 0
    base = len(hops) * tokens
    ring = labels is not None and len(labels) > 0 and labels[0] is not None
    head_index = pl.program_id(0)
    documents = []
    if which and ring:
        count = lax.axis_size("ctx")
        gaps = [slot_gap(owners[number]) for number in range(DOCS)]
        late = (gaps[0] == count // 2) if count % 2 == 0 else False
        early = jnp.where(late, 1, 0)
        for place in which:
            number = early if place == 0 else 1 - early
            gap = jnp.where(number == 0, gaps[0], gaps[1])
            documents.append((number, gap))
    elif which:
        documents = [(place, place) for place in which]

    @pl.when(head_index == 0)
    def _():
        values[:, HD:] = jnp.ones((values.shape[0], HD), jnp.bfloat16)
        count = lax.axis_size("ctx")
        placed = lax.axis_index("ctx") - offsets[lax.axis_index("req")] + count
        placed = lax.rem(placed, count)
        for number, hop in enumerate(hops):
            bias_rows(keys, number * tokens, tokens, jnp.where(placed >= hop, tokens, 0))
        for place, (number, _) in enumerate(documents):
            bias_rows(keys, base + place * height, height, scalars[requests + DOCS + number])

    columns = pl.ds(pl.multiple_of(head_index * HD, HD), HD)
    for number, ref in enumerate(blocks):
        keys[number * tokens : (number + 1) * tokens, :HD] = ref[0, :, columns]
        values[number * tokens : (number + 1) * tokens, :HD] = ref[1, :, columns]
    for place, (_, gap) in enumerate(documents):
        rows = slice(base + place * height, base + (place + 1) * height)
        for index, (key_ref, value_ref) in enumerate(slots):

            @pl.when(gap == (labels[index] if ring else index))
            def _():
                keys[rows, :HD] = key_ref[:, columns]
                values[rows, :HD] = value_ref[:, columns]

    lane = lax.broadcasted_iota(jnp.int32, (tile * tokens, HD), 1)
    first = jnp.where(lane == 0, 1.0, 0.0).astype(jnp.bfloat16)
    if 0 in hops:
        query = lax.broadcasted_iota(jnp.int32, (tokens, tokens), 0)
        key = lax.broadcasted_iota(jnp.int32, (tokens, tokens), 1)
        causal = jnp.concatenate([key <= query] * tile, axis=0)

    def scored(head):
        heads = []
        for i in range(head, head + tile):
            begin = pl.multiple_of((head_index * group + i) * HD, HD)
            heads.append(q_ref[:, pl.ds(begin, HD)])
        block = jnp.concatenate([jnp.concatenate(heads, axis=0), first], axis=1)
        scores = lax.dot_general(
            block, keys[...], (((1,), (1,)), ((), ())), preferred_element_type=jnp.float32
        )
        if 0 in hops:
            masked = jnp.where(causal, scores[:, :tokens], NEGATIVE)
            scores = jnp.concatenate([masked, scores[:, tokens:]], axis=1)
        return scores

    def weighed(head, scores):
        highest = jnp.max(scores, axis=1, keepdims=True) * SCALE
        highest = jnp.broadcast_to(highest, (tile * tokens, HD))
        if carried:
            highest = jnp.maximum(highest, before[2][head_index, head * tokens : (head + tile) * tokens])
        repeated = jnp.concatenate([highest] * (scores.shape[1] // HD), axis=1)
        weights = jnp.exp2(scores * SCALE - repeated).astype(jnp.bfloat16)
        return highest, jnp.dot(weights, values[...], preferred_element_type=jnp.float32)

    def finish(head, highest, summed):
        rows = slice(head * tokens, (head + tile) * tokens)
        total, denominator = summed[:, :HD], summed[:, HD:]
        if carried:
            share = jnp.exp2(before[2][head_index, rows] - highest)
            total = total + before[0][head_index, rows] * share
            denominator = denominator + before[1][head_index, rows] * share
        if final:
            result = total / denominator
            for i in range(tile):
                columns_of = slice((head + i) * HD, (head + i + 1) * HD)
                out_ref[:, columns_of] = result[i * tokens : (i + 1) * tokens].astype(jnp.bfloat16)
        else:
            out_ref[head_index, rows] = total
            sum_ref[head_index, rows] = denominator
            top_ref[head_index, rows] = highest

    starts = list(range(0, group, tile))
    scores = scored(starts[0])
    pending = None
    for number, head in enumerate(starts):
        following = scored(starts[number + 1]) if number + 1 < len(starts) else None
        result = weighed(head, scores)
        if pending is not None:
            finish(*pending)
        pending = (head, *result)
        scores = following
    finish(*pending)


def attend(name, scalars, queries, blocks, slots, which, before, final):
    tokens, width = queries.shape
    kv_width = (blocks[0][1] if blocks else slots[0][1]).shape[-1]
    kv_heads = kv_width // HD
    group = width // kv_width
    rows = group * tokens
    heads = pl.BlockSpec((tokens, group * HD), lambda g, *s: (0, g))
    whole = pl.BlockSpec(memory_space=pltpu.VMEM)
    total = len(blocks) * tokens + (len(which) * slots[0][1].shape[0] if which else 0)
    operands = [queries] + [block for _, block in blocks]
    for _, key_rows, value_rows in slots:
        operands += [key_rows, value_rows]
    if before is not None:
        operands += before
    partials = jax.ShapeDtypeStruct((kv_heads, rows, HD), jnp.float32)
    return pl.pallas_call(
        functools.partial(
            attention_body,
            group,
            math.gcd(group, TILE[name]),
            tuple(hop for hop, _ in blocks),
            tuple(label for label, _, _ in slots),
            which,
            before is not None,
            final,
        ),
        out_shape=jax.ShapeDtypeStruct((tokens, width), jnp.bfloat16) if final else [partials] * 3,
        grid_spec=pltpu.PrefetchScalarGridSpec(
            num_scalar_prefetch=1,
            grid=(kv_heads,),
            in_specs=[whole] * len(operands),
            out_specs=heads if final else [whole] * 3,
            scratch_shapes=[pltpu.VMEM((total, 2 * HD), jnp.bfloat16)] * 2,
        ),
        compiler_params=pltpu.CompilerParams(vmem_limit_bytes=32 << 20),
        cost_estimate=pl.CostEstimate(
            flops=4 * kv_heads * rows * total * HD,
            bytes_accessed=8 * kv_heads * rows * HD,
            transcendentals=kv_heads * rows * total,
        ),
    )(scalars, *operands)


def per_device(
    queries, keys, values, cache_keys, cache_values, doc_lengths, doc_owners, block_offsets
):
    count = lax.axis_size("ctx")
    even = lax.axis_index("ctx") % 2 == 0
    ring = lax.axis_size("req") == 2 and count <= RING_LIMIT
    own = jnp.stack([keys[0], values[0]])
    slot = (cache_keys[0], cache_values[0])

    if ring:
        order = list(range(0, count, 2)) + list(range(1, count, 2))[::-1]
        onward = [(order[i], order[(i + 1) % count]) for i in range(count)]
        both = onward + [(count + target, count + source) for source, target in onward]
        pieces = [slot] + [[None, None] for _ in range(count - 1)]
        for step in range(1, count // 2 + 1):
            for part in range(2):
                pieces[step][part] = lax.ppermute(pieces[step - 1][part], ("req", "ctx"), both)
                if 2 * step < count:
                    pieces[count - step][part] = shifted(pieces[step][part], "req", 1)
    else:
        pieces = [
            [broadcast(part, "ctx", doc_owners[number]) for part in slot] for number in range(DOCS)
        ]

    two = shifted(own, "ctx", 2)
    one = lax.ppermute(jnp.where(even, own, two), "ctx", [(i, i ^ 1) for i in range(count)])
    three = shifted(one, "ctx", 2)

    scalars = jnp.concatenate([block_offsets, doc_owners, doc_lengths])
    labels = range(count) if ring else [None] * DOCS
    slots = [(label, *piece) for label, piece in zip(labels, pieces)]
    soon = [s for s in slots if not (ring and 2 * s[0] == count)]
    window = [(0, own), (1, one), (2, two)]
    state = attend("near", scalars, queries[0], window, [], (), None, False)
    state = attend("middle", scalars, queries[0], [(3, three)], soon, (0,), state, False)
    return attend("far", scalars, queries[0], [], slots, (1,), state, True)[None]


def solution(mesh):
    return jax.shard_map(
        per_device,
        mesh=mesh,
        in_specs=(
            P(("groups", "req"), "ctx", None),
            P(("groups", "req"), "ctx", None),
            P(("groups", "req"), "ctx", None),
            P(("groups", "ctx"), None, None),
            P(("groups", "ctx"), None, None),
            P("groups"),
            P("groups"),
            P("groups"),
        ),
        out_specs=P(("groups", "req"), "ctx", None),
        check_vma=False,
    )
```

time: 131 us -> 53.2 us (0.41)
  waiting for transfers between devices: 50.9 us -> 15.4 us
  matrix products: 32.1 us -> 0 us
  between operations: 16.1 us -> 0.12 us
  starting transfers between devices: 4.57 us -> 19.9 us
  local copies, waits for them, and re-layouts: 17.4 us -> 3.12 us
  Pallas kernels: 0 us -> 13.7 us
  other arithmetic: 8.85 us -> 0.79 us
    psum x1 -> x0, waiting for transfers between devices: 32.8 us -> none  [broadcast(): return lax.psum(block, axis)]
    dot_general x48 -> x0, matrix products: 32.1 us -> none  [the longest x24 25.1 us: merge_block(): jnp.einsum('tid,sd->its', query_rows, key_rows, preferred_element_type=jn...]
    ppermute x3 -> x17, starting transfers between devices: 4.57 us -> 19.9 us  [the longest x8 14.4 us: per_device(): lax.ppermute(pieces[step - 1][part], ('req', 'ctx'), both)]
    pallas_call x0 -> x3, Pallas kernels: none -> 13.7 us  [attend(): pl.pallas_call(functools.partial(attention_body, group, math.gcd(group, T...]
    unnamed x81 -> x7, local copies, waits for them, and re-layouts: 12.8 us -> 2.15 us
    reduce_sum x16 -> x0, other arithmetic: 4.05 us -> none  [the longest x15 3.35 us: merge_block(): totals = totals * shrink + jnp.sum(weights, axis=-1)]
    ppermute x3 -> x17, waiting for transfers between devices: 18.1 us -> 15.4 us  [the longest x8 6.22 us: per_device(): lax.ppermute(pieces[step - 1][part], ('req', 'ctx'), both)]
    lt x2 -> x0, other arithmetic: 2.41 us -> none  [per_device(): jnp.arange(doc_rows)[None, :] < doc_lengths[number]]
  transfers between devices with their start and end apart: 4 -> 17, of which waited for: 3 -> 7; matrix products, arithmetic and copies ran while one was open for 23% -> 5% of each run, Pallas kernels for 0% -> 17%
where the time goes in v3:
time: 53.2 us; the launch traced here: 53 us
  starting transfers between devices  19.9 us (37%)
  waiting for transfers between devices  15.4 us (29%)
  Pallas kernels  13.7 us (26%)
  local copies, waits for them, and re-layouts  3.12 us (6%)
  other arithmetic  0.79 us (1%)
    ppermute x8, starting transfers between devices, per_device(): lax.ppermute(pieces[step - 1][part], ('req', 'ctx'), both)  14.4 us
    pallas_call x3, Pallas kernels, attend(): pl.pallas_call(functools.partial(attention_body, group, math.gcd(group, T...  13.7 us
    ppermute x8, waiting for transfers between devices, per_device(): lax.ppermute(pieces[step - 1][part], ('req', 'ctx'), both)  6.22 us
    ppermute x8, waiting for transfers between devices, shifted(): return lax.ppermute(value, axis, pairs)  5.96 us
    ppermute x1, waiting for transfers between devices, per_device(): lax.ppermute(jnp.where(even, own, two), 'ctx', [(i, i ^ 1) for i in range...  3.22 us
    ppermute x8, starting transfers between devices, shifted(): return lax.ppermute(value, axis, pairs)  2.95 us
    ppermute x1, starting transfers between devices, per_device(): lax.ppermute(jnp.where(even, own, two), 'ctx', [(i, i ^ 1) for i in range...  2.55 us
    unnamed x7, local copies, waits for them, and re-layouts  2.15 us
  transfers between devices with their start and end apart: 17, of which 7 were waited for; matrix products, arithmetic and copies ran while one was open for 5% of the time, Pallas kernels for 17%

profile of v3, /device:TPU:0, one launch (start us, length us, event | category | flops | bytes accessed | tf_op | source)
XLA Modules:
  0.0 53.0 jit_solution(7637476229012474370)
XLA Ops:
  0.0 3.1 %collective-permute-start = (bf16[256,512]{1,0:T(8,128)(2,1)}, bf16[256,512]{1,0:T(8,128)(2,1)S(1)}, u32[]{:S(2)}, u32[]{:S(2)}) collective-permute-start(bf16[256,512]{1,0:T(8,128)(2,1)} %bitcast.7), channel_id=1, source_target_pairs={{0,2},{2,4},{4,6},{6,7},{7,5},{5,3},{3,1},{1,0},{10,8},{12,10},{14... | collective-permute-start | bytes 786440 | tf_op jit(solution)/shard_map/ppermute | solution.py:224
  3.1 1.6 %collective-permute-start.1 = (bf16[256,512]{1,0:T(8,128)(2,1)}, bf16[256,512]{1,0:T(8,128)(2,1)S(1)}, u32[]{:S(2)}, u32[]{:S(2)}) collective-permute-start(bf16[256,512]{1,0:T(8,128)(2,1)} %bitcast.10), channel_id=1, source_target_pairs={{0,2},{2,4},{4,6},{6,7},{7,5},{5,3},{3,1},{1,0},{10,8},{12,10},{14... | collective-permute-start | bytes 786440 | tf_op jit(solution)/shard_map/ppermute | solution.py:224
  4.6 0.9 %constant_dynamic-update-slice_fusion.1 = bf16[2,128,512]{2,1,0:T(8,128)(2,1)S(1)} fusion(bf16[1,128,512]{2,1,0:T(8,128)(2,1)} %param.9), kind=kLoop, calls=%fused_computation.2 | loop fusion | bytes 262144
  5.6 1.0 %constant_dynamic-update-slice_fusion.refs_1_ = bf16[2,128,512]{2,1,0:T(8,128)(2,1)S(1)} fusion(bf16[2,128,512]{2,1,0:T(8,128)(2,1)S(1)} %constant_dynamic-update-slice_fusion.1, bf16[1,128,512]{2,1,0:T(8,128)(2,1)} %param.10), kind=kLoop, calls=%fused_computation.1 | loop fusion | bytes 262144 | tf_op jit(solution)/shard_map/stack | solution.py:214
  6.5 1.6 %collective-permute-start.14 = (bf16[2,128,512]{2,1,0:T(8,128)(2,1)S(1)}, bf16[2,128,512]{2,1,0:T(8,128)(2,1)S(1)}, u32[]{:S(2)}, u32[]{:S(2)}) collective-permute-start(bf16[2,128,512]{2,1,0:T(8,128)(2,1)S(1)} %constant_dynamic-update-slice_fusion.refs_1_), channel_id=1, source_target_pairs={{0,2},{1,3},{2,4},{3,5},{4,6},{5,7},{6,0},{7,1},{8,10},{9,11},{10,... | collective-permute-start | bytes 786440 | tf_op jit(solution)/shard_map/ppermute | solution.py:29
  8.2 2.7 %collective-permute-start.2 = (bf16[256,512]{1,0:T(8,128)(2,1)S(1)}, bf16[256,512]{1,0:T(8,128)(2,1)S(1)}, u32[]{:S(2)}, u32[]{:S(2)}) collective-permute-start(bf16[256,512]{1,0:T(8,128)(2,1)S(1)} %collective-permute-done.refs_4_.refs_3_), channel_id=1, source_target_pairs={{0,2},{2,4},{4,6},{6,7},{7,5},{5,3},{3,1},{1,0},{10,8},{12,10},{14... | collective-permute-start | bytes 786440 | tf_op jit(solution)/shard_map/ppermute | solution.py:224
  10.8 2.0 %collective-permute-done.1.refs_5_.refs_4_ = bf16[256,512]{1,0:T(8,128)(2,1)S(1)} collective-permute-done((bf16[256,512]{1,0:T(8,128)(2,1)}, bf16[256,512]{1,0:T(8,128)(2,1)S(1)}, u32[]{:S(2)}, u32[]{:S(2)}) %collective-permute-start.1) | collective-permute-done | bytes 262176 | tf_op jit(solution)/shard_map/ppermute | solution.py:224
  12.9 2.4 %collective-permute-start.3 = (bf16[256,512]{1,0:T(8,128)(2,1)S(1)}, bf16[256,512]{1,0:T(8,128)(2,1)S(1)}, u32[]{:S(2)}, u32[]{:S(2)}) collective-permute-start(bf16[256,512]{1,0:T(8,128)(2,1)S(1)} %collective-permute-done.1.refs_5_.refs_4_), channel_id=1, source_target_pairs={{0,2},{2,4},{4,6},{6,7},{7,5},{5,3},{3,1},{1,0},{10,8},{12,10},{14... | collective-permute-start | bytes 786440 | tf_op jit(solution)/shard_map/ppermute | solution.py:224
  15.3 2.4 %collective-permute-done.14.refs_3_ = bf16[2,128,512]{2,1,0:T(8,128)(2,1)S(1)} collective-permute-done((bf16[2,128,512]{2,1,0:T(8,128)(2,1)S(1)}, bf16[2,128,512]{2,1,0:T(8,128)(2,1)S(1)}, u32[]{:S(2)}, u32[]{:S(2)}) %collective-permute-start.14) | collective-permute-done | bytes 262176 | tf_op jit(solution)/shard_map/ppermute | solution.py:29
  17.7 2.5 %collective-permute-start.15 = (bf16[2,128,512]{2,1,0:T(8,128)(2,1)S(1)}, bf16[2,128,512]{2,1,0:T(8,128)(2,1)S(1)}, u32[]{:S(2)}, u32[]{:S(2)}) collective-permute-start(bf16[2,128,512]{2,1,0:T(8,128)(2,1)S(1)} %broadcast_select_fusion), channel_id=1, source_target_pairs={{0,1},{1,0},{2,3},{3,2},{4,5},{5,4},{6,7},{7,6},{8,9},{9,8},{10,11... | collective-permute-start | bytes 786440 | tf_op jit(solution)/shard_map/ppermute | solution.py:233
  20.2 0.5 collective-permute-start.13
  21.2 2.5 %collective-permute-start.5 = (bf16[256,512]{1,0:T(8,128)(2,1)S(1)}, bf16[256,512]{1,0:T(8,128)(2,1)S(1)}, u32[]{:S(2)}, u32[]{:S(2)}) collective-permute-start(bf16[256,512]{1,0:T(8,128)(2,1)S(1)} %collective-permute-done.3.refs_7_.refs_6_), channel_id=1, source_target_pairs={{0,2},{2,4},{4,6},{6,7},{7,5},{5,3},{3,1},{1,0},{10,8},{12,10},{14... | collective-permute-start | bytes 786440 | tf_op jit(solution)/shard_map/ppermute | solution.py:224
  23.7 3.2 %collective-permute-done.15.refs_2_ = bf16[2,128,512]{2,1,0:T(8,128)(2,1)S(1)} collective-permute-done((bf16[2,128,512]{2,1,0:T(8,128)(2,1)S(1)}, bf16[2,128,512]{2,1,0:T(8,128)(2,1)S(1)}, u32[]{:S(2)}, u32[]{:S(2)}) %collective-permute-start.15) | collective-permute-done | bytes 262176 | tf_op jit(solution)/shard_map/ppermute | solution.py:233
  26.9 0.5 collective-permute-start.11
  27.4 1.0 %collective-permute-done.4.refs_8_.refs_7_ = bf16[256,512]{1,0:T(8,128)(2,1)S(1)} collective-permute-done((bf16[256,512]{1,0:T(8,128)(2,1)S(1)}, bf16[256,512]{1,0:T(8,128)(2,1)S(1)}, u32[]{:S(2)}, u32[]{:S(2)}) %collective-permute-start.4) | collective-permute-done | bytes 262176 | tf_op jit(solution)/shard_map/ppermute | solution.py:224
  28.5 2.8 %collective-permute-done.5.refs_9_.refs_8_ = bf16[256,512]{1,0:T(8,128)(2,1)S(1)} collective-permute-done((bf16[256,512]{1,0:T(8,128)(2,1)S(1)}, bf16[256,512]{1,0:T(8,128)(2,1)S(1)}, u32[]{:S(2)}, u32[]{:S(2)}) %collective-permute-start.5) | collective-permute-done | bytes 262176 | tf_op jit(solution)/shard_map/ppermute | solution.py:224
  31.6 3.6 %collective-permute-done.16.refs_1_ = bf16[2,128,512]{2,1,0:T(8,128)(2,1)S(1)} collective-permute-done((bf16[2,128,512]{2,1,0:T(8,128)(2,1)S(1)}, bf16[2,128,512]{2,1,0:T(8,128)(2,1)S(1)}, u32[]{:S(2)}, u32[]{:S(2)}) %collective-permute-start.16) | collective-permute-done | bytes 262176 | tf_op jit(solution)/shard_map/ppermute | solution.py:29
  35.1 0.5 %collective-permute-start.6 = (bf16[256,512]{1,0:T(8,128)(2,1)S(1)}, bf16[256,512]{1,0:T(8,128)(2,1)S(1)}, u32[]{:S(2)}, u32[]{:S(2)}) collective-permute-start(bf16[256,512]{1,0:T(8,128)(2,1)S(1)} %collective-permute-done.4.refs_8_.refs_7_), channel_id=1, source_target_pairs={{0,2},{2,4},{4,6},{6,7},{7,5},{5,3},{3,1},{1,0},{10,8},{12,10},{14... | collective-permute-start | bytes 786440 | tf_op jit(solution)/shard_map/ppermute | solution.py:224
  35.7 1.6 %collective-permute-start.7 = (bf16[256,512]{1,0:T(8,128)(2,1)S(1)}, bf16[256,512]{1,0:T(8,128)(2,1)S(1)}, u32[]{:S(2)}, u32[]{:S(2)}) collective-permute-start(bf16[256,512]{1,0:T(8,128)(2,1)S(1)} %collective-permute-done.5.refs_9_.refs_8_), channel_id=1, source_target_pairs={{0,2},{2,4},{4,6},{6,7},{7,5},{5,3},{3,1},{1,0},{10,8},{12,10},{14... | collective-permute-start | bytes 786440 | tf_op jit(solution)/shard_map/ppermute | solution.py:224
  37.3 0.8 %pad_add_fusion.scalars = s32[6]{0:T(128)S(1)} fusion(s32[2]{0:T(128)} %param.13, s32[2]{0:T(128)} %param.14, s32[2]{0:T(128)} %param.15), kind=kLoop, calls=%fused_computation.3 | loop fusion | flops 12 | bytes 48 | tf_op jit(solution)/shard_map/concatenate | solution.py:236
  38.0 1.2 %copy-done = bf16[1,128,4096]{2,1,0:T(8,128)(2,1)S(1)} copy-done((bf16[1,128,4096]{2,1,0:T(8,128)(2,1)S(1)}, bf16[1,128,4096]{2,1,0:T(8,128)(2,1)}, u32[]{:S(2)}) %copy-start) | copy-done | bytes 1048600
  39.2 4.3 %shard_map.82 = (f32[4,1024,128]{2,1,0:T(8,128)S(1)}, f32[4,1024,128]{2,1,0:T(8,128)S(1)}, f32[4,1024,128]{2,1,0:T(8,128)S(1)}) custom-call(s32[6]{0:T(128)S(1)} %pad_add_fusion.scalars, bf16[128,4096]{1,0:T(8,128)(2,1)S(1)} %bitcast.4, bf16[2,128,512]{2,1,0:T(8,128)(2,1)S(1)} %constant_dynamic-update-slice_fusion.refs_1_, ...), custom_call_target="tpu_custom_call" | custom-call | flops 805306368 | bytes 4194304 | tf_op jit(solution)/shard_map/pallas_call | solution.py:180
  43.6 4.9 %shard_map.83 = (f32[4,1024,128]{2,1,0:T(8,128)S(1)}, f32[4,1024,128]{2,1,0:T(8,128)S(1)}, f32[4,1024,128]{2,1,0:T(8,128)S(1)}) custom-call(s32[6]{0:T(128)S(1)} %pad_add_fusion.scalars, bf16[128,4096]{1,0:T(8,128)(2,1)S(1)} %bitcast.5, bf16[2,128,512]{2,1,0:T(8,128)(2,1)S(1)} %collective-permute-done.16.refs_1_, bf16[256,512]{1,0:T(8,128)(2,1)S(1)} %bitcast.8, ...), custom_call_target="tpu_custom_call" | custom-call | flops 805306368 | bytes 4194304 | tf_op jit(solution)/shard_map/pallas_call | solution.py:180
  48.5 4.5 %shard_map.84 = bf16[128,4096]{1,0:T(8,128)(2,1)} custom-call(s32[6]{0:T(128)S(1)} %pad_add_fusion.scalars, bf16[128,4096]{1,0:T(8,128)(2,1)S(1)} %bitcast.6, bf16[256,512]{1,0:T(8,128)(2,1)S(1)} %bitcast.9, bf16[256,512]{1,0:T(8,128)(2,1)S(1)} %bitcast.12, bf16[256,512]{1,0:T(8,128)(2,1)S(1)} %collective-permute-done.refs_4_.refs_3_, ...), custom_call_target="tpu_custom_call" | custom-call | flops 536870912 | bytes 4194304 | tf_op jit(solution)/shard_map/pallas_call | solution.py:180
  (23 shorter events, 0.9 us)
Async XLA Ops:
  0.0 8.2 %collective-permute-start = (bf16[256,512]{1,0:T(8,128)(2,1)}, bf16[256,512]{1,0:T(8,128)(2,1)S(1)}, u32[]{:S(2)}, u32[]{:S(2)}) collective-permute-start(bf16[256,512]{1,0:T(8,128)(2,1)} %bitcast.7), channel_id=1, source_target_pairs={{0,2},{2,4},{4,6},{6,7},{7,5},{5,3},{3,1},{1,0},{10,8},{12,10},{14... | collective-permute-start | bytes 786440 | tf_op jit(solution)/shard_map/ppermute | solution.py:224
  3.1 9.8 %collective-permute-start.1 = (bf16[256,512]{1,0:T(8,128)(2,1)}, bf16[256,512]{1,0:T(8,128)(2,1)S(1)}, u32[]{:S(2)}, u32[]{:S(2)}) collective-permute-start(bf16[256,512]{1,0:T(8,128)(2,1)} %bitcast.10), channel_id=1, source_target_pairs={{0,2},{2,4},{4,6},{6,7},{7,5},{5,3},{3,1},{1,0},{10,8},{12,10},{14... | collective-permute-start | bytes 786440 | tf_op jit(solution)/shard_map/ppermute | solution.py:224
  5.5 38.0 %copy-start.1 = (bf16[1,256,512]{2,1,0:T(8,128)(2,1)S(1)}, bf16[1,256,512]{2,1,0:T(8,128)(2,1)}, u32[]{:S(2)}) copy-start(bf16[1,256,512]{2,1,0:T(8,128)(2,1)} %param.11) | copy-start | bytes 786436
  5.6 38.0 %copy-start.2 = (bf16[1,256,512]{2,1,0:T(8,128)(2,1)S(1)}, bf16[1,256,512]{2,1,0:T(8,128)(2,1)}, u32[]{:S(2)}) copy-start(bf16[1,256,512]{2,1,0:T(8,128)(2,1)} %param.12) | copy-start | bytes 786436
  6.5 11.1 %collective-permute-start.14 = (bf16[2,128,512]{2,1,0:T(8,128)(2,1)S(1)}, bf16[2,128,512]{2,1,0:T(8,128)(2,1)S(1)}, u32[]{:S(2)}, u32[]{:S(2)}) collective-permute-start(bf16[2,128,512]{2,1,0:T(8,128)(2,1)S(1)} %constant_dynamic-update-slice_fusion.refs_1_), channel_id=1, source_target_pairs={{0,2},{1,3},{2,4},{3,5},{4,6},{5,7},{6,0},{7,1},{8,10},{9,11},{10,... | collective-permute-start | bytes 786440 | tf_op jit(solution)/shard_map/ppermute | solution.py:29
  8.2 12.5 %collective-permute-start.2 = (bf16[256,512]{1,0:T(8,128)(2,1)S(1)}, bf16[256,512]{1,0:T(8,128)(2,1)S(1)}, u32[]{:S(2)}, u32[]{:S(2)}) collective-permute-start(bf16[256,512]{1,0:T(8,128)(2,1)S(1)} %collective-permute-done.refs_4_.refs_3_), channel_id=1, source_target_pairs={{0,2},{2,4},{4,6},{6,7},{7,5},{5,3},{3,1},{1,0},{10,8},{12,10},{14... | collective-permute-start | bytes 786440 | tf_op jit(solution)/shard_map/ppermute | solution.py:224
  12.9 8.3 %collective-permute-start.3 = (bf16[256,512]{1,0:T(8,128)(2,1)S(1)}, bf16[256,512]{1,0:T(8,128)(2,1)S(1)}, u32[]{:S(2)}, u32[]{:S(2)}) collective-permute-start(bf16[256,512]{1,0:T(8,128)(2,1)S(1)} %collective-permute-done.1.refs_5_.refs_4_), channel_id=1, source_target_pairs={{0,2},{2,4},{4,6},{6,7},{7,5},{5,3},{3,1},{1,0},{10,8},{12,10},{14... | collective-permute-start | bytes 786440 | tf_op jit(solution)/shard_map/ppermute | solution.py:224
  17.7 9.2 %collective-permute-start.15 = (bf16[2,128,512]{2,1,0:T(8,128)(2,1)S(1)}, bf16[2,128,512]{2,1,0:T(8,128)(2,1)S(1)}, u32[]{:S(2)}, u32[]{:S(2)}) collective-permute-start(bf16[2,128,512]{2,1,0:T(8,128)(2,1)S(1)} %broadcast_select_fusion), channel_id=1, source_target_pairs={{0,1},{1,0},{2,3},{3,2},{4,5},{5,4},{6,7},{7,6},{8,9},{9,8},{10,11... | collective-permute-start | bytes 786440 | tf_op jit(solution)/shard_map/ppermute | solution.py:233
  20.2 6.7 %collective-permute-start.12 = (bf16[256,512]{1,0:T(8,128)(2,1)S(1)}, bf16[256,512]{1,0:T(8,128)(2,1)S(1)}, u32[]{:S(2)}, u32[]{:S(2)}) collective-permute-start(bf16[256,512]{1,0:T(8,128)(2,1)S(1)} %collective-permute-done.refs_4_.refs_3_), channel_id=1, source_target_pairs={{0,8},{8,0},{1,9},{9,1},{2,10},{10,2},{3,11},{11,3},{4,12},{12,4},... | collective-permute-start | bytes 786440 | tf_op jit(solution)/shard_map/ppermute | solution.py:29
  20.2 6.7 %collective-permute-start.13 = (bf16[256,512]{1,0:T(8,128)(2,1)S(1)}, bf16[256,512]{1,0:T(8,128)(2,1)S(1)}, u32[]{:S(2)}, u32[]{:S(2)}) collective-permute-start(bf16[256,512]{1,0:T(8,128)(2,1)S(1)} %collective-permute-done.1.refs_5_.refs_4_), channel_id=1, source_target_pairs={{0,8},{8,0},{1,9},{9,1},{2,10},{10,2},{3,11},{11,3},{4,12},{12,4},... | collective-permute-start | bytes 786440 | tf_op jit(solution)/shard_map/ppermute | solution.py:29
  20.7 7.7 %collective-permute-start.4 = (bf16[256,512]{1,0:T(8,128)(2,1)S(1)}, bf16[256,512]{1,0:T(8,128)(2,1)S(1)}, u32[]{:S(2)}, u32[]{:S(2)}) collective-permute-start(bf16[256,512]{1,0:T(8,128)(2,1)S(1)} %collective-permute-done.2.refs_6_.refs_5_), channel_id=1, source_target_pairs={{0,2},{2,4},{4,6},{6,7},{7,5},{5,3},{3,1},{1,0},{10,8},{12,10},{14... | collective-permute-start | bytes 786440 | tf_op jit(solution)/shard_map/ppermute | solution.py:224
  21.2 10.1 %collective-permute-start.5 = (bf16[256,512]{1,0:T(8,128)(2,1)S(1)}, bf16[256,512]{1,0:T(8,128)(2,1)S(1)}, u32[]{:S(2)}, u32[]{:S(2)}) collective-permute-start(bf16[256,512]{1,0:T(8,128)(2,1)S(1)} %collective-permute-done.3.refs_7_.refs_6_), channel_id=1, source_target_pairs={{0,2},{2,4},{4,6},{6,7},{7,5},{5,3},{3,1},{1,0},{10,8},{12,10},{14... | collective-permute-start | bytes 786440 | tf_op jit(solution)/shard_map/ppermute | solution.py:224
  26.9 8.2 %collective-permute-start.16 = (bf16[2,128,512]{2,1,0:T(8,128)(2,1)S(1)}, bf16[2,128,512]{2,1,0:T(8,128)(2,1)S(1)}, u32[]{:S(2)}, u32[]{:S(2)}) collective-permute-start(bf16[2,128,512]{2,1,0:T(8,128)(2,1)S(1)} %collective-permute-done.15.refs_2_), channel_id=1, source_target_pairs={{0,2},{1,3},{2,4},{3,5},{4,6},{5,7},{6,0},{7,1},{8,10},{9,11},{10,... | collective-permute-start | bytes 786440 | tf_op jit(solution)/shard_map/ppermute | solution.py:29
  26.9 8.8 %collective-permute-start.10 = (bf16[256,512]{1,0:T(8,128)(2,1)S(1)}, bf16[256,512]{1,0:T(8,128)(2,1)S(1)}, u32[]{:S(2)}, u32[]{:S(2)}) collective-permute-start(bf16[256,512]{1,0:T(8,128)(2,1)S(1)} %collective-permute-done.2.refs_6_.refs_5_), channel_id=1, source_target_pairs={{0,8},{8,0},{1,9},{9,1},{2,10},{10,2},{3,11},{11,3},{4,12},{12,4},... | collective-permute-start | bytes 786440 | tf_op jit(solution)/shard_map/ppermute | solution.py:29
  26.9 16.6 %collective-permute-start.11 = (bf16[256,512]{1,0:T(8,128)(2,1)S(1)}, bf16[256,512]{1,0:T(8,128)(2,1)S(1)}, u32[]{:S(2)}, u32[]{:S(2)}) collective-permute-start(bf16[256,512]{1,0:T(8,128)(2,1)S(1)} %collective-permute-done.3.refs_7_.refs_6_), channel_id=1, source_target_pairs={{0,8},{8,0},{1,9},{9,1},{2,10},{10,2},{3,11},{11,3},{4,12},{12,4},... | collective-permute-start | bytes 786440 | tf_op jit(solution)/shard_map/ppermute | solution.py:29
  28.5 15.1 %collective-permute-start.8 = (bf16[256,512]{1,0:T(8,128)(2,1)S(1)}, bf16[256,512]{1,0:T(8,128)(2,1)S(1)}, u32[]{:S(2)}, u32[]{:S(2)}) collective-permute-start(bf16[256,512]{1,0:T(8,128)(2,1)S(1)} %collective-permute-done.4.refs_8_.refs_7_), channel_id=1, source_target_pairs={{0,8},{8,0},{1,9},{9,1},{2,10},{10,2},{3,11},{11,3},{4,12},{12,4},... | collective-permute-start | bytes 786440 | tf_op jit(solution)/shard_map/ppermute | solution.py:29
  31.3 12.3 %collective-permute-start.9 = (bf16[256,512]{1,0:T(8,128)(2,1)S(1)}, bf16[256,512]{1,0:T(8,128)(2,1)S(1)}, u32[]{:S(2)}, u32[]{:S(2)}) collective-permute-start(bf16[256,512]{1,0:T(8,128)(2,1)S(1)} %collective-permute-done.5.refs_9_.refs_8_), channel_id=1, source_target_pairs={{0,8},{8,0},{1,9},{9,1},{2,10},{10,2},{3,11},{11,3},{4,12},{12,4},... | collective-permute-start | bytes 786440 | tf_op jit(solution)/shard_map/ppermute | solution.py:29
  35.1 13.4 %collective-permute-start.6 = (bf16[256,512]{1,0:T(8,128)(2,1)S(1)}, bf16[256,512]{1,0:T(8,128)(2,1)S(1)}, u32[]{:S(2)}, u32[]{:S(2)}) collective-permute-start(bf16[256,512]{1,0:T(8,128)(2,1)S(1)} %collective-permute-done.4.refs_8_.refs_7_), channel_id=1, source_target_pairs={{0,2},{2,4},{4,6},{6,7},{7,5},{5,3},{3,1},{1,0},{10,8},{12,10},{14... | collective-permute-start | bytes 786440 | tf_op jit(solution)/shard_map/ppermute | solution.py:224
  35.7 12.8 %collective-permute-start.7 = (bf16[256,512]{1,0:T(8,128)(2,1)S(1)}, bf16[256,512]{1,0:T(8,128)(2,1)S(1)}, u32[]{:S(2)}, u32[]{:S(2)}) collective-permute-start(bf16[256,512]{1,0:T(8,128)(2,1)S(1)} %collective-permute-done.5.refs_9_.refs_8_), channel_id=1, source_target_pairs={{0,2},{2,4},{4,6},{6,7},{7,5},{5,3},{3,1},{1,0},{10,8},{12,10},{14... | collective-permute-start | bytes 786440 | tf_op jit(solution)/shard_map/ppermute | solution.py:224
  38.0 1.2 %copy-start = (bf16[1,128,4096]{2,1,0:T(8,128)(2,1)S(1)}, bf16[1,128,4096]{2,1,0:T(8,128)(2,1)}, u32[]{:S(2)}) copy-start(bf16[1,128,4096]{2,1,0:T(8,128)(2,1)} %param.8) | copy-start | bytes 3145732

commit v4 on v3

v4 whole, which is shorter than its diff:
```python
import functools
import math

import jax
import jax.numpy as jnp
from jax import lax
from jax.experimental import pallas as pl
from jax.experimental.pallas import tpu as pltpu
from jax.sharding import PartitionSpec as P


HD = 128
DOCS = 2
HEADROOM = 40.0
TILE = {"near": 2, "middle": 2, "far": 4}
RING_LIMIT = 16

NEGATIVE = -1e30
SCALE = math.log2(math.e) / math.sqrt(HD)


def broadcast(block, axis, source):
    block = jnp.where(lax.axis_index(axis) == source, block, jnp.zeros_like(block))
    return lax.psum(block, axis)


def shifted(value, axis, steps):
    count = lax.axis_size(axis)
    pairs = [(source, (source + steps) % count) for source in range(count)]
    return lax.ppermute(value, axis, pairs)


def bias_rows(keys, start, height, live):
    lane = lax.broadcasted_iota(jnp.int32, (height, HD), 1)
    row = lax.broadcasted_iota(jnp.int32, (height, HD), 0)
    dead = (row >= live) & (lane == 0)
    bias = jnp.where(dead, NEGATIVE, 0.0).astype(jnp.bfloat16)
    for g in range(keys.shape[0]):
        keys[g, start : start + height, HD:] = bias


def ring_place(index, count):
    return jnp.where(index % 2 == 0, index // 2, count - 1 - index // 2)


def slot_gap(owner):
    count = lax.axis_size("ctx")
    gap = ring_place(lax.axis_index("ctx"), count) - ring_place(owner, count)
    gap = jnp.where(lax.axis_index("req") == 0, gap, -gap)
    return jnp.where(gap < 0, gap + count, gap)


def attention_body(kv_heads, group, tile, hops, paired, labels, which, carried, final, scalars, *refs):
    requests = scalars.shape[0] - 2 * DOCS
    offsets = scalars
    owners = [scalars[requests + number] for number in range(DOCS)]
    refs = list(refs)
    take = lambda number: [refs.pop(0) for _ in range(number)]
    (q_ref,) = take(1)
    blocks = [take(1 if stacked else 2) for stacked in paired]
    slots = [take(2) for _ in labels] if which else []
    before = take(3) if carried else None
    (out_ref,) = take(1)
    sum_ref, top_ref = (None, None) if final else take(2)
    keys, values = take(2)
    staged, sems = take(2) if final else (None, None)
    tokens = q_ref.shape[0]
    height = slots[0][0].shape[0] if which else 0
    base = len(hops) * tokens
    ring = len(labels) > 0 and labels[0] is not None
    count = lax.axis_size("ctx")
    documents = []
    if which and ring:
        gaps = [slot_gap(owners[number]) for number in range(DOCS)]
        late = (gaps[0] == count // 2) if count % 2 == 0 else False
        early = jnp.where(late, 1, 0)
        for place in which:
            number = early if place == 0 else 1 - early
            gap = jnp.where(number == 0, gaps[0], gaps[1])
            documents.append((number, gap))
    elif which:
        documents = [(place, place) for place in which]

    placed = lax.axis_index("ctx") - offsets[lax.axis_index("req")] + count
    placed = lax.rem(placed, count)
    ones = jnp.ones((values.shape[1], HD), jnp.bfloat16)
    for number, hop in enumerate(hops):
        bias_rows(keys, number * tokens, tokens, jnp.where(placed >= hop, tokens, 0))
    for place, (number, _) in enumerate(documents):
        bias_rows(keys, base + place * height, height, scalars[requests + DOCS + number])
    for g in range(kv_heads):
        values[g, :, HD:] = ones
        for number, ref in enumerate(blocks):
            rows = slice(number * tokens, (number + 1) * tokens)
            both = [part.at[i] for part in ref for i in range(2)] if len(ref) == 1 else ref
            keys[g, rows, :HD] = both[0][:, g * HD : (g + 1) * HD]
            values[g, rows, :HD] = both[1][:, g * HD : (g + 1) * HD]
    for place, (_, gap) in enumerate(documents):
        rows = slice(base + place * height, base + (place + 1) * height)
        for index, (key_ref, value_ref) in enumerate(slots):

            @pl.when(gap == (labels[index] if ring else index))
            def _():
                for g in range(kv_heads):
                    keys[g, rows, :HD] = key_ref[:, g * HD : (g + 1) * HD]
                    values[g, rows, :HD] = value_ref[:, g * HD : (g + 1) * HD]

    lane = lax.broadcasted_iota(jnp.int32, (tile * tokens, HD), 1)
    first = jnp.where(lane == 0, 1.0, 0.0).astype(jnp.bfloat16)
    if 0 in hops:
        query = lax.broadcasted_iota(jnp.int32, (tokens, tokens), 0)
        key = lax.broadcasted_iota(jnp.int32, (tokens, tokens), 1)
        causal = jnp.concatenate([key <= query] * tile, axis=0)

    def scored(g, head):
        begin = g * group + head
        heads = [q_ref[:, i * HD : (i + 1) * HD] for i in range(begin, begin + tile)]
        block = jnp.concatenate([jnp.concatenate(heads, axis=0), first], axis=1)
        scores = lax.dot_general(
            block, keys[g], (((1,), (1,)), ((), ())), preferred_element_type=jnp.float32
        )
        if 0 in hops:
            masked = jnp.where(causal, scores[:, :tokens], NEGATIVE)
            scores = jnp.concatenate([masked, scores[:, tokens:]], axis=1)
        return scores

    def weighed(g, head, scores, fast):
        rows = slice(head * tokens, (head + tile) * tokens)
        if fast:
            highest = before[2][g, rows]
        else:
            highest = jnp.max(scores, axis=1, keepdims=True) * SCALE
            highest = jnp.broadcast_to(highest, (tile * tokens, HD))
            if carried:
                highest = jnp.maximum(highest, before[2][g, rows])
        repeated = jnp.concatenate([highest] * (scores.shape[1] // HD), axis=1)
        exponents = scores * SCALE - repeated
        if fast:
            parts = [exponents[:, i : i + HD] for i in range(0, exponents.shape[1], HD)]
            peak = functools.reduce(jnp.maximum, parts)
            peaks.append(jnp.max(peak.reshape(-1, 8, HD), axis=0))
        weights = jnp.exp2(exponents).astype(jnp.bfloat16)
        return highest, jnp.dot(weights, values[g], preferred_element_type=jnp.float32)

    def finish(g, head, highest, summed, fast):
        rows = slice(head * tokens, (head + tile) * tokens)
        total, denominator = summed[:, :HD], summed[:, HD:]
        if fast:
            total = total + before[0][g, rows]
            denominator = denominator + before[1][g, rows]
        elif carried:
            share = jnp.exp2(before[2][g, rows] - highest)
            total = total + before[0][g, rows] * share
            denominator = denominator + before[1][g, rows] * share
        if final:
            result = (total / denominator).astype(jnp.bfloat16)
            for i in range(tile):
                begin = (g * group + head + i) * HD
                staged[:, begin : begin + HD] = result[i * tokens : (i + 1) * tokens]
            if head + tile == group:
                store(g).start()
        else:
            out_ref[g, rows] = total
            sum_ref[g, rows] = denominator
            top_ref[g, rows] = highest

    def store(g):
        columns = pl.ds(g * group * HD, group * HD)
        return pltpu.make_async_copy(staged.at[:, columns], out_ref.at[:, columns], sems.at[g])

    def run(fast):
        starts = [(g, head) for g in range(kv_heads) for head in range(0, group, tile)]
        scores = scored(*starts[0])
        pending = None
        for number, where in enumerate(starts):
            following = scored(*starts[number + 1]) if number + 1 < len(starts) else None
            result = weighed(*where, scores, fast)
            if pending is not None:
                finish(*pending, fast)
            pending = (*where, *result)
            scores = following
        finish(*pending, fast)
        if final:
            for g in range(kv_heads):
                store(g).wait()

    peaks = []
    run(carried)
    if carried:

        @pl.when(jnp.max(functools.reduce(jnp.maximum, peaks)) > HEADROOM)
        def _():
            run(False)


def fetch_body(queries, keys, values, to_queries, to_block, sems):
    pairs = [(queries, to_queries), (keys, to_block.at[0]), (values, to_block.at[1])]
    copies = [pltpu.make_async_copy(*pair, sems.at[i]) for i, pair in enumerate(pairs)]
    for copy in copies:
        copy.start()
    for copy in copies:
        copy.wait()


def fetch(queries, keys, values):
    return pl.pallas_call(
        fetch_body,
        out_shape=[
            jax.ShapeDtypeStruct(queries.shape, queries.dtype),
            jax.ShapeDtypeStruct((2,) + keys.shape, keys.dtype),
        ],
        in_specs=[pl.BlockSpec(memory_space=pl.ANY)] * 3,
        out_specs=[pl.BlockSpec(memory_space=pltpu.VMEM)] * 2,
        scratch_shapes=[pltpu.SemaphoreType.DMA((3,))],
        compiler_params=pltpu.CompilerParams(vmem_limit_bytes=4 << 20),
        name="fetch",
    )(queries, keys, values)


def attend(name, scalars, queries, blocks, slots, which, before, final):
    tokens, width = queries.shape
    kv_width = (blocks[0][1] if blocks else slots[0][1]).shape[-1]
    kv_heads = kv_width // HD
    group = width // kv_width
    rows = group * tokens
    whole = pl.BlockSpec(memory_space=pltpu.VMEM)
    total = len(blocks) * tokens + (len(which) * slots[0][1].shape[0] if which else 0)
    operands = [queries, *sum((list(block[1:]) for block in blocks), [])]
    for _, key_rows, value_rows in slots:
        operands += [key_rows, value_rows]
    if before is not None:
        operands += before
    stage = [pltpu.VMEM((tokens, width), jnp.bfloat16), pltpu.SemaphoreType.DMA((kv_heads,))]
    stage = stage if final else []
    partials = jax.ShapeDtypeStruct((kv_heads, rows, HD), jnp.float32)
    return pl.pallas_call(
        functools.partial(
            attention_body,
            kv_heads,
            group,
            math.gcd(group, TILE[name]),
            tuple(block[0] for block in blocks),
            tuple(len(block) == 2 for block in blocks),
            tuple(label for label, _, _ in slots),
            which,
            before is not None,
            final,
        ),
        out_shape=jax.ShapeDtypeStruct((tokens, width), jnp.bfloat16) if final else [partials] * 3,
        grid_spec=pltpu.PrefetchScalarGridSpec(
            num_scalar_prefetch=1,
            in_specs=[whole] * len(operands),
            out_specs=pl.BlockSpec(memory_space=pl.ANY) if final else [whole] * 3,
            scratch_shapes=[pltpu.VMEM((kv_heads, total, 2 * HD), jnp.bfloat16)] * 2 + stage,
        ),
        compiler_params=pltpu.CompilerParams(vmem_limit_bytes=24 << 20),
        cost_estimate=pl.CostEstimate(
            flops=4 * kv_heads * rows * total * HD,
            bytes_accessed=8 * kv_heads * rows * HD,
            transcendentals=kv_heads * rows * total,
        ),
    )(scalars, *operands)


def per_device(
    queries, keys, values, cache_keys, cache_values, doc_lengths, doc_owners, block_offsets
):
    count = lax.axis_size("ctx")
    even = lax.axis_index("ctx") % 2 == 0
    ring = lax.axis_size("req") == 2 and count <= RING_LIMIT
    own = (keys[0], values[0])
    slot = (cache_keys[0], cache_values[0])

    if ring:
        order = list(range(0, count, 2)) + list(range(1, count, 2))[::-1]
        onward = [(order[i], order[(i + 1) % count]) for i in range(count)]
        both = onward + [(count + target, count + source) for source, target in onward]
        pieces = [slot] + [[None, None] for _ in range(count - 1)]
        for step in range(1, count // 2 + 1):
            for part in range(2):
                pieces[step][part] = lax.ppermute(pieces[step - 1][part], ("req", "ctx"), both)
                if 2 * step < count:
                    pieces[count - step][part] = shifted(pieces[step][part], "req", 1)
    else:
        pieces = [
            [broadcast(part, "ctx", doc_owners[number]) for part in slot] for number in range(DOCS)
        ]

    two = [None, None]
    for part in range(2):
        two[part] = shifted(own[part], "ctx", 2)
    scalars = jnp.concatenate([block_offsets, doc_owners, doc_lengths])
    taken = jnp.stack([jnp.where(even, own[part], two[part]) for part in range(2)])
    taken, scalars = lax.optimization_barrier((taken, scalars))
    one = lax.ppermute(taken, "ctx", [(i, i ^ 1) for i in range(count)])
    three = shifted(one, "ctx", 2)

    labels = range(count) if ring else [None] * DOCS
    slots = [(label, *piece) for label, piece in zip(labels, pieces)]
    soon = [s for s in slots if not (ring and 2 * s[0] == count)]
    held, block = fetch(queries[0], *own)
    window = [(0, block), (1, one), (2, *two)]
    state = attend("near", scalars, held, window, [], (), None, False)
    state = attend("middle", scalars, held, [(3, three)], soon, (0,), state, False)
    return attend("far", scalars, held, [], slots, (1,), state, True)[None]


def solution(mesh):
    return jax.shard_map(
        per_device,
        mesh=mesh,
        in_specs=(
            P(("groups", "req"), "ctx", None),
            P(("groups", "req"), "ctx", None),
            P(("groups", "req"), "ctx", None),
            P(("groups", "ctx"), None, None),
            P(("groups", "ctx"), None, None),
            P("groups"),
            P("groups"),
            P("groups"),
        ),
        out_specs=P(("groups", "req"), "ctx", None),
        check_vma=False,
    )
```

time: 53.2 us -> 51.8 us (0.974)
  starting transfers between devices: 19.9 us -> 13.2 us
  waiting for transfers between devices: 15.4 us -> 21.4 us
  Pallas kernels: 13.7 us -> 10.5 us
  other arithmetic: 0.79 us -> 2.63 us
    ppermute x8, starting transfers between devices: 14.4 us -> 5.75 us  [per_device(): lax.ppermute(pieces[step - 1][part], ('req', 'ctx'), both)]
    ppermute x8, waiting for transfers between devices: 6.22 us -> 11.5 us  [per_device(): lax.ppermute(pieces[step - 1][part], ('req', 'ctx'), both)]
    pallas_call x3 -> x4, Pallas kernels: 13.7 us -> 10.5 us  [the longest x3 10 us: attend(): pl.pallas_call(functools.partial(attention_body, kv_heads, group, math.gc...]
    ppermute x8 -> x9, starting transfers between devices: 2.95 us -> 5.64 us  [shifted(): return lax.ppermute(value, axis, pairs)]
    another operation x0 -> x3, other arithmetic: none -> 1.87 us  [per_device(): jnp.stack([jnp.where(even, own[part], two[part]) for part in range(2)])]
    ppermute x8 -> x9, waiting for transfers between devices: 5.96 us -> 7.13 us  [shifted(): return lax.ppermute(value, axis, pairs)]
    another operation x1 -> x0, local copies, waits for them, and re-layouts: 0.97 us -> none  [per_device(): own = jnp.stack([keys[0], values[0]])]
    unnamed x7 -> x10, local copies, waits for them, and re-layouts: 2.15 us -> 3.04 us
  transfers between devices with their start and end apart: 17 -> 18, of which waited for: 7 -> 9; matrix products, arithmetic and copies ran while one was open for 5% -> 5% of each run, Pallas kernels for 17% -> 14%
where the time goes in v4:
time: 51.8 us; the launch traced here: 51.1 us
  waiting for transfers between devices  21.4 us (41%)
  starting transfers between devices  13.2 us (25%)
  Pallas kernels  10.5 us (20%)
  local copies, waits for them, and re-layouts  3.04 us (6%)
  other arithmetic  2.63 us (5%)
    ppermute x8, waiting for transfers between devices, per_device(): lax.ppermute(pieces[step - 1][part], ('req', 'ctx'), both)  11.5 us
    pallas_call x3, Pallas kernels, attend(): pl.pallas_call(functools.partial(attention_body, kv_heads, group, math.gc...  10 us
    ppermute x9, waiting for transfers between devices, shifted(): return lax.ppermute(value, axis, pairs)  7.13 us
    ppermute x8, starting transfers between devices, per_device(): lax.ppermute(pieces[step - 1][part], ('req', 'ctx'), both)  5.75 us
    ppermute x9, starting transfers between devices, shifted(): return lax.ppermute(value, axis, pairs)  5.64 us
    unnamed x10, local copies, waits for them, and re-layouts  3.04 us
    ppermute x1, waiting for transfers between devices, per_device(): one = lax.ppermute(taken, 'ctx', [(i, i ^ 1) for i in range(count)])  2.81 us
    another operation x3, other arithmetic, per_device(): jnp.stack([jnp.where(even, own[part], two[part]) for part in range(2)])  1.87 us
  transfers between devices with their start and end apart: 18, of which 9 were waited for; matrix products, arithmetic and copies ran while one was open for 5% of the time, Pallas kernels for 14%

profile of v4, /device:TPU:0, one launch (start us, length us, event | category | flops | bytes accessed | tf_op | source)
XLA Modules:
  0.0 51.1 jit_solution(8969795672319741738)
XLA Ops:
  0.0 3.1 %collective-permute-start = (bf16[128,512]{1,0:T(8,128)(2,1)}, bf16[128,512]{1,0:T(8,128)(2,1)S(1)}, u32[]{:S(2)}, u32[]{:S(2)}) collective-permute-start(bf16[128,512]{1,0:T(8,128)(2,1)} %bitcast.19), channel_id=1, source_target_pairs={{0,2},{1,3},{2,4},{3,5},{4,6},{5,7},{6,0},{7,1},{8,10},{9,11},{10,... | collective-permute-start | bytes 393224 | tf_op jit(solution)/shard_map/ppermute | solution.py:30
  3.1 1.6 %collective-permute-start.1 = (bf16[128,512]{1,0:T(8,128)(2,1)}, bf16[128,512]{1,0:T(8,128)(2,1)S(1)}, u32[]{:S(2)}, u32[]{:S(2)}) collective-permute-start(bf16[128,512]{1,0:T(8,128)(2,1)} %bitcast.21), channel_id=1, source_target_pairs={{0,2},{1,3},{2,4},{3,5},{4,6},{5,7},{6,0},{7,1},{8,10},{9,11},{10,... | collective-permute-start | bytes 393224 | tf_op jit(solution)/shard_map/ppermute | solution.py:30
  4.6 1.6 %collective-permute-start.2 = (bf16[256,512]{1,0:T(8,128)(2,1)}, bf16[256,512]{1,0:T(8,128)(2,1)S(1)}, u32[]{:S(2)}, u32[]{:S(2)}) collective-permute-start(bf16[256,512]{1,0:T(8,128)(2,1)} %bitcast.12), channel_id=1, source_target_pairs={{0,2},{2,4},{4,6},{6,7},{7,5},{5,3},{3,1},{1,0},{10,8},{12,10},{14... | collective-permute-start | bytes 786440 | tf_op jit(solution)/shard_map/ppermute | solution.py:281
  6.2 0.8 %pad_add_fusion.scalars = s32[6]{0:T(128)S(1)} fusion(s32[2]{0:T(128)} %param.13, s32[2]{0:T(128)} %param.14, s32[2]{0:T(128)} %param.15), kind=kLoop, calls=%fused_computation.3 | loop fusion | flops 12 | bytes 48 | tf_op jit(solution)/shard_map/concatenate | solution.py:292
  7.0 2.7 %collective-permute-done.refs_3_ = bf16[128,512]{1,0:T(8,128)(2,1)S(1)} collective-permute-done((bf16[128,512]{1,0:T(8,128)(2,1)}, bf16[128,512]{1,0:T(8,128)(2,1)S(1)}, u32[]{:S(2)}, u32[]{:S(2)}) %collective-permute-start) | collective-permute-done | bytes 131104 | tf_op jit(solution)/shard_map/ppermute | solution.py:30
  9.7 0.9 %select_bitcast_fusion.1 = bf16[1,128,512]{2,1,0:T(8,128)(2,1)S(1)} fusion(bf16[128,512]{1,0:T(8,128)(2,1)S(1)} %collective-permute-done.refs_3_, pred[]{:T(512)S(6)} %eq.5, bf16[1,128,512]{2,1,0:T(8,128)(2,1)} %param.9), kind=kLoop, calls=%fused_computation.2 | loop fusion | flops 65536 | bytes 393217 | tf_op jit(solution)/shard_map/stack | solution.py:293
  10.7 1.8 %collective-permute-done.1.refs_4_ = bf16[128,512]{1,0:T(8,128)(2,1)S(1)} collective-permute-done((bf16[128,512]{1,0:T(8,128)(2,1)}, bf16[128,512]{1,0:T(8,128)(2,1)S(1)}, u32[]{:S(2)}, u32[]{:S(2)}) %collective-permute-start.1) | collective-permute-done | bytes 131104 | tf_op jit(solution)/shard_map/ppermute | solution.py:30
  12.5 0.9 %select_bitcast_fusion = bf16[1,128,512]{2,1,0:T(8,128)(2,1)S(1)} fusion(bf16[128,512]{1,0:T(8,128)(2,1)S(1)} %collective-permute-done.1.refs_4_, pred[]{:T(512)S(6)} %eq.5, bf16[1,128,512]{2,1,0:T(8,128)(2,1)} %param.10), kind=kLoop, calls=%fused_computation.1 | loop fusion | flops 65536 | bytes 393217 | tf_op jit(solution)/shard_map/stack | solution.py:293
  13.4 0.7 %collective-permute-start.4 = (bf16[256,512]{1,0:T(8,128)(2,1)S(1)}, bf16[256,512]{1,0:T(8,128)(2,1)S(1)}, u32[]{:S(2)}, u32[]{:S(2)}) collective-permute-start(bf16[256,512]{1,0:T(8,128)(2,1)S(1)} %collective-permute-done.2.refs_4_.refs_3_), channel_id=1, source_target_pairs={{0,2},{2,4},{4,6},{6,7},{7,5},{5,3},{3,1},{1,0},{10,8},{12,10},{14... | collective-permute-start | bytes 786440 | tf_op jit(solution)/shard_map/ppermute | solution.py:281
  14.6 2.4 %collective-permute-start.5 = (bf16[256,512]{1,0:T(8,128)(2,1)S(1)}, bf16[256,512]{1,0:T(8,128)(2,1)S(1)}, u32[]{:S(2)}, u32[]{:S(2)}) collective-permute-start(bf16[256,512]{1,0:T(8,128)(2,1)S(1)} %collective-permute-done.3.refs_5_.refs_4_), channel_id=1, source_target_pairs={{0,2},{2,4},{4,6},{6,7},{7,5},{5,3},{3,1},{1,0},{10,8},{12,10},{14... | collective-permute-start | bytes 786440 | tf_op jit(solution)/shard_map/ppermute | solution.py:281
  17.0 1.8 %collective-permute-start.16 = (bf16[2,128,512]{2,1,0:T(8,128)(2,1)S(1)}, bf16[2,128,512]{2,1,0:T(8,128)(2,1)S(1)}, u32[]{:S(2)}, u32[]{:S(2)}) collective-permute-start(bf16[2,128,512]{2,1,0:T(8,128)(2,1)S(1)} %pad_maximum_fusion), channel_id=1, source_target_pairs={{0,1},{1,0},{2,3},{3,2},{4,5},{5,4},{6,7},{7,6},{8,9},{9,8},{10,11... | collective-permute-start | bytes 786440 | tf_op jit(solution)/shard_map/ppermute | solution.py:295
  19.3 1.4 %collective-permute-done.4.refs_6_.refs_5_ = bf16[256,512]{1,0:T(8,128)(2,1)S(1)} collective-permute-done((bf16[256,512]{1,0:T(8,128)(2,1)S(1)}, bf16[256,512]{1,0:T(8,128)(2,1)S(1)}, u32[]{:S(2)}, u32[]{:S(2)}) %collective-permute-start.4) | collective-permute-done | bytes 262176 | tf_op jit(solution)/shard_map/ppermute | solution.py:281
  20.8 0.6 %collective-permute-start.6 = (bf16[256,512]{1,0:T(8,128)(2,1)S(1)}, bf16[256,512]{1,0:T(8,128)(2,1)S(1)}, u32[]{:S(2)}, u32[]{:S(2)}) collective-permute-start(bf16[256,512]{1,0:T(8,128)(2,1)S(1)} %collective-permute-done.4.refs_6_.refs_5_), channel_id=1, source_target_pairs={{0,2},{2,4},{4,6},{6,7},{7,5},{5,3},{3,1},{1,0},{10,8},{12,10},{14... | collective-permute-start | bytes 786440 | tf_op jit(solution)/shard_map/ppermute | solution.py:281
  21.3 4.5 %collective-permute-done.5.refs_7_.refs_6_ = bf16[256,512]{1,0:T(8,128)(2,1)S(1)} collective-permute-done((bf16[256,512]{1,0:T(8,128)(2,1)S(1)}, bf16[256,512]{1,0:T(8,128)(2,1)S(1)}, u32[]{:S(2)}, u32[]{:S(2)}) %collective-permute-start.5) | collective-permute-done | bytes 262176 | tf_op jit(solution)/shard_map/ppermute | solution.py:281
  25.9 2.8 %collective-permute-done.16.refs_2_ = bf16[2,128,512]{2,1,0:T(8,128)(2,1)S(1)} collective-permute-done((bf16[2,128,512]{2,1,0:T(8,128)(2,1)S(1)}, bf16[2,128,512]{2,1,0:T(8,128)(2,1)S(1)}, u32[]{:S(2)}, u32[]{:S(2)}) %collective-permute-start.16) | collective-permute-done | bytes 262176 | tf_op jit(solution)/shard_map/ppermute | solution.py:295
  29.2 2.3 %collective-permute-done.6.refs_8_.refs_7_ = bf16[256,512]{1,0:T(8,128)(2,1)S(1)} collective-permute-done((bf16[256,512]{1,0:T(8,128)(2,1)S(1)}, bf16[256,512]{1,0:T(8,128)(2,1)S(1)}, u32[]{:S(2)}, u32[]{:S(2)}) %collective-permute-start.6) | collective-permute-done | bytes 262176 | tf_op jit(solution)/shard_map/ppermute | solution.py:281
  31.5 2.8 %collective-permute-done.7.refs_9_.refs_8_ = bf16[256,512]{1,0:T(8,128)(2,1)S(1)} collective-permute-done((bf16[256,512]{1,0:T(8,128)(2,1)S(1)}, bf16[256,512]{1,0:T(8,128)(2,1)S(1)}, u32[]{:S(2)}, u32[]{:S(2)}) %collective-permute-start.7) | collective-permute-done | bytes 262176 | tf_op jit(solution)/shard_map/ppermute | solution.py:281
  34.3 2.5 %collective-permute-done.17.refs_1_ = bf16[2,128,512]{2,1,0:T(8,128)(2,1)S(1)} collective-permute-done((bf16[2,128,512]{2,1,0:T(8,128)(2,1)S(1)}, bf16[2,128,512]{2,1,0:T(8,128)(2,1)S(1)}, u32[]{:S(2)}, u32[]{:S(2)}) %collective-permute-start.17) | collective-permute-done | bytes 262176 | tf_op jit(solution)/shard_map/ppermute | solution.py:30
  37.3 1.2 %copy-done.2 = bf16[1,128,4096]{2,1,0:T(8,128)(2,1)S(1)} copy-done((bf16[1,128,4096]{2,1,0:T(8,128)(2,1)S(1)}, bf16[1,128,4096]{2,1,0:T(8,128)(2,1)}, u32[]{:S(2)}) %copy-start.2) | copy-done | bytes 1048600
  38.6 0.9 %copy-done.3 = bf16[1,128,512]{2,1,0:T(8,128)(2,1)S(1)} copy-done((bf16[1,128,512]{2,1,0:T(8,128)(2,1)S(1)}, bf16[1,128,512]{2,1,0:T(8,128)(2,1)}, u32[]{:S(2)}) %copy-start.3) | copy-done | bytes 131096
  39.5 0.9 %copy-done.4 = bf16[1,128,512]{2,1,0:T(8,128)(2,1)S(1)} copy-done((bf16[1,128,512]{2,1,0:T(8,128)(2,1)S(1)}, bf16[1,128,512]{2,1,0:T(8,128)(2,1)}, u32[]{:S(2)}) %copy-start.4) | copy-done | bytes 131096
  40.8 3.4 %shard_map.82 = (f32[4,1024,128]{2,1,0:T(8,128)S(1)}, f32[4,1024,128]{2,1,0:T(8,128)S(1)}, f32[4,1024,128]{2,1,0:T(8,128)S(1)}) custom-call(s32[6]{0:T(128)S(1)} %pad_add_fusion.scalars, bf16[128,4096]{1,0:T(8,128)(2,1)S(1)} %get-tuple-element.16.refs_0_, bf16[2,128,512]{2,1,0:T(8,128)(2,1)S(1)} %get-tuple-element.18.refs_1_, ...), custom_call_target="tpu_custom_call" | custom-call | flops 805306368 | bytes 4194304 | tf_op jit(solution)/shard_map/pallas_call | solution.py:236
  44.3 3.4 %shard_map.83 = (f32[4,1024,128]{2,1,0:T(8,128)S(1)}, f32[4,1024,128]{2,1,0:T(8,128)S(1)}, f32[4,1024,128]{2,1,0:T(8,128)S(1)}) custom-call(s32[6]{0:T(128)S(1)} %pad_add_fusion.scalars, bf16[128,4096]{1,0:T(8,128)(2,1)S(1)} %get-tuple-element.16.refs_0_, bf16[2,128,512]{2,1,0:T(8,128)(2,1)S(1)} %collective-permute-done.17.refs_1_, ...), custom_call_target="tpu_custom_call" | custom-call | flops 805306368 | bytes 4194304 | tf_op jit(solution)/shard_map/pallas_call | solution.py:236
  47.7 3.2 %shard_map.84 = bf16[128,4096]{1,0:T(8,128)(2,1)} custom-call(s32[6]{0:T(128)S(1)} %pad_add_fusion.scalars, bf16[128,4096]{1,0:T(8,128)(2,1)S(1)} %get-tuple-element.16.refs_0_, bf16[256,512]{1,0:T(8,128)(2,1)S(1)} %bitcast.14, bf16[256,512]{1,0:T(8,128)(2,1)S(1)} %bitcast.17, bf16[256,512]{1,0:T(8,128)(2,1)S(1)} %collective-permute-done.2.refs_4_.refs_3_, ...), custom_call_target="tpu_custom_call" | custom-call | flops 536870912 | bytes 4194304 | tf_op jit(solution)/shard_map/pallas_call | solution.py:236
  (30 shorter events, 2.5 us)
Async XLA Ops:
  0.0 9.7 %collective-permute-start = (bf16[128,512]{1,0:T(8,128)(2,1)}, bf16[128,512]{1,0:T(8,128)(2,1)S(1)}, u32[]{:S(2)}, u32[]{:S(2)}) collective-permute-start(bf16[128,512]{1,0:T(8,128)(2,1)} %bitcast.19), channel_id=1, source_target_pairs={{0,2},{1,3},{2,4},{3,5},{4,6},{5,7},{6,0},{7,1},{8,10},{9,11},{10,... | collective-permute-start | bytes 393224 | tf_op jit(solution)/shard_map/ppermute | solution.py:30
  3.1 9.4 %collective-permute-start.1 = (bf16[128,512]{1,0:T(8,128)(2,1)}, bf16[128,512]{1,0:T(8,128)(2,1)S(1)}, u32[]{:S(2)}, u32[]{:S(2)}) collective-permute-start(bf16[128,512]{1,0:T(8,128)(2,1)} %bitcast.21), channel_id=1, source_target_pairs={{0,2},{1,3},{2,4},{3,5},{4,6},{5,7},{6,0},{7,1},{8,10},{9,11},{10,... | collective-permute-start | bytes 393224 | tf_op jit(solution)/shard_map/ppermute | solution.py:30
  4.6 8.8 %collective-permute-start.2 = (bf16[256,512]{1,0:T(8,128)(2,1)}, bf16[256,512]{1,0:T(8,128)(2,1)S(1)}, u32[]{:S(2)}, u32[]{:S(2)}) collective-permute-start(bf16[256,512]{1,0:T(8,128)(2,1)} %bitcast.12), channel_id=1, source_target_pairs={{0,2},{2,4},{4,6},{6,7},{7,5},{5,3},{3,1},{1,0},{10,8},{12,10},{14... | collective-permute-start | bytes 786440 | tf_op jit(solution)/shard_map/ppermute | solution.py:281
  6.2 8.3 %collective-permute-start.3 = (bf16[256,512]{1,0:T(8,128)(2,1)}, bf16[256,512]{1,0:T(8,128)(2,1)S(1)}, u32[]{:S(2)}, u32[]{:S(2)}) collective-permute-start(bf16[256,512]{1,0:T(8,128)(2,1)} %bitcast.15), channel_id=1, source_target_pairs={{0,2},{2,4},{4,6},{6,7},{7,5},{5,3},{3,1},{1,0},{10,8},{12,10},{14... | collective-permute-start | bytes 786440 | tf_op jit(solution)/shard_map/ppermute | solution.py:281
  13.4 7.3 %collective-permute-start.4 = (bf16[256,512]{1,0:T(8,128)(2,1)S(1)}, bf16[256,512]{1,0:T(8,128)(2,1)S(1)}, u32[]{:S(2)}, u32[]{:S(2)}) collective-permute-start(bf16[256,512]{1,0:T(8,128)(2,1)S(1)} %collective-permute-done.2.refs_4_.refs_3_), channel_id=1, source_target_pairs={{0,2},{2,4},{4,6},{6,7},{7,5},{5,3},{3,1},{1,0},{10,8},{12,10},{14... | collective-permute-start | bytes 786440 | tf_op jit(solution)/shard_map/ppermute | solution.py:281
  14.6 11.3 %collective-permute-start.5 = (bf16[256,512]{1,0:T(8,128)(2,1)S(1)}, bf16[256,512]{1,0:T(8,128)(2,1)S(1)}, u32[]{:S(2)}, u32[]{:S(2)}) collective-permute-start(bf16[256,512]{1,0:T(8,128)(2,1)S(1)} %collective-permute-done.3.refs_5_.refs_4_), channel_id=1, source_target_pairs={{0,2},{2,4},{4,6},{6,7},{7,5},{5,3},{3,1},{1,0},{10,8},{12,10},{14... | collective-permute-start | bytes 786440 | tf_op jit(solution)/shard_map/ppermute | solution.py:281
  17.0 11.7 %collective-permute-start.16 = (bf16[2,128,512]{2,1,0:T(8,128)(2,1)S(1)}, bf16[2,128,512]{2,1,0:T(8,128)(2,1)S(1)}, u32[]{:S(2)}, u32[]{:S(2)}) collective-permute-start(bf16[2,128,512]{2,1,0:T(8,128)(2,1)S(1)} %pad_maximum_fusion), channel_id=1, source_target_pairs={{0,1},{1,0},{2,3},{3,2},{4,5},{5,4},{6,7},{7,6},{8,9},{9,8},{10,11... | collective-permute-start | bytes 786440 | tf_op jit(solution)/shard_map/ppermute | solution.py:295
  18.8 9.9 %collective-permute-start.14 = (bf16[256,512]{1,0:T(8,128)(2,1)S(1)}, bf16[256,512]{1,0:T(8,128)(2,1)S(1)}, u32[]{:S(2)}, u32[]{:S(2)}) collective-permute-start(bf16[256,512]{1,0:T(8,128)(2,1)S(1)} %collective-permute-done.2.refs_4_.refs_3_), channel_id=1, source_target_pairs={{0,8},{8,0},{1,9},{9,1},{2,10},{10,2},{3,11},{11,3},{4,12},{12,4},... | collective-permute-start | bytes 786440 | tf_op jit(solution)/shard_map/ppermute | solution.py:30
  18.8 9.9 %collective-permute-start.15 = (bf16[256,512]{1,0:T(8,128)(2,1)S(1)}, bf16[256,512]{1,0:T(8,128)(2,1)S(1)}, u32[]{:S(2)}, u32[]{:S(2)}) collective-permute-start(bf16[256,512]{1,0:T(8,128)(2,1)S(1)} %collective-permute-done.3.refs_5_.refs_4_), channel_id=1, source_target_pairs={{0,8},{8,0},{1,9},{9,1},{2,10},{10,2},{3,11},{11,3},{4,12},{12,4},... | collective-permute-start | bytes 786440 | tf_op jit(solution)/shard_map/ppermute | solution.py:30
  20.8 10.7 %collective-permute-start.6 = (bf16[256,512]{1,0:T(8,128)(2,1)S(1)}, bf16[256,512]{1,0:T(8,128)(2,1)S(1)}, u32[]{:S(2)}, u32[]{:S(2)}) collective-permute-start(bf16[256,512]{1,0:T(8,128)(2,1)S(1)} %collective-permute-done.4.refs_6_.refs_5_), channel_id=1, source_target_pairs={{0,2},{2,4},{4,6},{6,7},{7,5},{5,3},{3,1},{1,0},{10,8},{12,10},{14... | collective-permute-start | bytes 786440 | tf_op jit(solution)/shard_map/ppermute | solution.py:281
  25.9 8.4 %collective-permute-start.7 = (bf16[256,512]{1,0:T(8,128)(2,1)S(1)}, bf16[256,512]{1,0:T(8,128)(2,1)S(1)}, u32[]{:S(2)}, u32[]{:S(2)}) collective-permute-start(bf16[256,512]{1,0:T(8,128)(2,1)S(1)} %collective-permute-done.5.refs_7_.refs_6_), channel_id=1, source_target_pairs={{0,2},{2,4},{4,6},{6,7},{7,5},{5,3},{3,1},{1,0},{10,8},{12,10},{14... | collective-permute-start | bytes 786440 | tf_op jit(solution)/shard_map/ppermute | solution.py:281
  28.7 8.2 %collective-permute-start.17 = (bf16[2,128,512]{2,1,0:T(8,128)(2,1)S(1)}, bf16[2,128,512]{2,1,0:T(8,128)(2,1)S(1)}, u32[]{:S(2)}, u32[]{:S(2)}) collective-permute-start(bf16[2,128,512]{2,1,0:T(8,128)(2,1)S(1)} %collective-permute-done.16.refs_2_), channel_id=1, source_target_pairs={{0,2},{1,3},{2,4},{3,5},{4,6},{5,7},{6,0},{7,1},{8,10},{9,11},{10,... | collective-permute-start | bytes 786440 | tf_op jit(solution)/shard_map/ppermute | solution.py:30
  28.7 8.6 %collective-permute-start.12 = (bf16[256,512]{1,0:T(8,128)(2,1)S(1)}, bf16[256,512]{1,0:T(8,128)(2,1)S(1)}, u32[]{:S(2)}, u32[]{:S(2)}) collective-permute-start(bf16[256,512]{1,0:T(8,128)(2,1)S(1)} %collective-permute-done.4.refs_6_.refs_5_), channel_id=1, source_target_pairs={{0,8},{8,0},{1,9},{9,1},{2,10},{10,2},{3,11},{11,3},{4,12},{12,4},... | collective-permute-start | bytes 786440 | tf_op jit(solution)/shard_map/ppermute | solution.py:30
  28.7 15.5 %collective-permute-start.13 = (bf16[256,512]{1,0:T(8,128)(2,1)S(1)}, bf16[256,512]{1,0:T(8,128)(2,1)S(1)}, u32[]{:S(2)}, u32[]{:S(2)}) collective-permute-start(bf16[256,512]{1,0:T(8,128)(2,1)S(1)} %collective-permute-done.5.refs_7_.refs_6_), channel_id=1, source_target_pairs={{0,8},{8,0},{1,9},{9,1},{2,10},{10,2},{3,11},{11,3},{4,12},{12,4},... | collective-permute-start | bytes 786440 | tf_op jit(solution)/shard_map/ppermute | solution.py:30
  31.5 12.8 %collective-permute-start.10 = (bf16[256,512]{1,0:T(8,128)(2,1)S(1)}, bf16[256,512]{1,0:T(8,128)(2,1)S(1)}, u32[]{:S(2)}, u32[]{:S(2)}) collective-permute-start(bf16[256,512]{1,0:T(8,128)(2,1)S(1)} %collective-permute-done.6.refs_8_.refs_7_), channel_id=1, source_target_pairs={{0,8},{8,0},{1,9},{9,1},{2,10},{10,2},{3,11},{11,3},{4,12},{12,4},... | collective-permute-start | bytes 786440 | tf_op jit(solution)/shard_map/ppermute | solution.py:30
  34.3 10.0 %collective-permute-start.11 = (bf16[256,512]{1,0:T(8,128)(2,1)S(1)}, bf16[256,512]{1,0:T(8,128)(2,1)S(1)}, u32[]{:S(2)}, u32[]{:S(2)}) collective-permute-start(bf16[256,512]{1,0:T(8,128)(2,1)S(1)} %collective-permute-done.7.refs_9_.refs_8_), channel_id=1, source_target_pairs={{0,8},{8,0},{1,9},{9,1},{2,10},{10,2},{3,11},{11,3},{4,12},{12,4},... | collective-permute-start | bytes 786440 | tf_op jit(solution)/shard_map/ppermute | solution.py:30
  36.8 10.8 %collective-permute-start.8 = (bf16[256,512]{1,0:T(8,128)(2,1)S(1)}, bf16[256,512]{1,0:T(8,128)(2,1)S(1)}, u32[]{:S(2)}, u32[]{:S(2)}) collective-permute-start(bf16[256,512]{1,0:T(8,128)(2,1)S(1)} %collective-permute-done.6.refs_8_.refs_7_), channel_id=1, source_target_pairs={{0,2},{2,4},{4,6},{6,7},{7,5},{5,3},{3,1},{1,0},{10,8},{12,10},{14... | collective-permute-start | bytes 786440 | tf_op jit(solution)/shard_map/ppermute | solution.py:281
  37.3 10.4 %collective-permute-start.9 = (bf16[256,512]{1,0:T(8,128)(2,1)S(1)}, bf16[256,512]{1,0:T(8,128)(2,1)S(1)}, u32[]{:S(2)}, u32[]{:S(2)}) collective-permute-start(bf16[256,512]{1,0:T(8,128)(2,1)S(1)} %collective-permute-done.7.refs_9_.refs_8_), channel_id=1, source_target_pairs={{0,2},{2,4},{4,6},{6,7},{7,5},{5,3},{3,1},{1,0},{10,8},{12,10},{14... | collective-permute-start | bytes 786440 | tf_op jit(solution)/shard_map/ppermute | solution.py:281
  37.3 1.2 %copy-start.2 = (bf16[1,128,4096]{2,1,0:T(8,128)(2,1)S(1)}, bf16[1,128,4096]{2,1,0:T(8,128)(2,1)}, u32[]{:S(2)}) copy-start(bf16[1,128,4096]{2,1,0:T(8,128)(2,1)} %param.8) | copy-start | bytes 3145732
  38.6 0.9 %copy-start.3 = (bf16[1,128,512]{2,1,0:T(8,128)(2,1)S(1)}, bf16[1,128,512]{2,1,0:T(8,128)(2,1)}, u32[]{:S(2)}) copy-start(bf16[1,128,512]{2,1,0:T(8,128)(2,1)} %param.9) | copy-start | bytes 393220
  39.5 0.9 %copy-start.4 = (bf16[1,128,512]{2,1,0:T(8,128)(2,1)S(1)}, bf16[1,128,512]{2,1,0:T(8,128)(2,1)}, u32[]{:S(2)}) copy-start(bf16[1,128,512]{2,1,0:T(8,128)(2,1)} %param.10) | copy-start | bytes 393220
  40.4 3.9 %copy-start = (bf16[1,256,512]{2,1,0:T(8,128)(2,1)S(1)}, bf16[1,256,512]{2,1,0:T(8,128)(2,1)}, u32[]{:S(2)}) copy-start(bf16[1,256,512]{2,1,0:T(8,128)(2,1)} %param.11) | copy-start | bytes 786436
  40.4 3.9 %copy-start.1 = (bf16[1,256,512]{2,1,0:T(8,128)(2,1)S(1)}, bf16[1,256,512]{2,1,0:T(8,128)(2,1)}, u32[]{:S(2)}) copy-start(bf16[1,256,512]{2,1,0:T(8,128)(2,1)} %param.12) | copy-start | bytes 786436

commit v5 on v4

--- a/solution.py
+++ b/solution.py
@@ -62,7 +62,8 @@
     before = take(3) if carried else None
     (out_ref,) = take(1)
     sum_ref, top_ref = (None, None) if final else take(2)
-    keys, values = take(2)
+    (both,) = take(1)
+    keys, values = both.at[0], both.at[1]
     staged, sems = take(2) if final else (None, None)
     tokens = q_ref.shape[0]
     height = slots[0][0].shape[0] if which else 0
@@ -92,18 +93,23 @@
         values[g, :, HD:] = ones
         for number, ref in enumerate(blocks):
             rows = slice(number * tokens, (number + 1) * tokens)
-            both = [part.at[i] for part in ref for i in range(2)] if len(ref) == 1 else ref
-            keys[g, rows, :HD] = both[0][:, g * HD : (g + 1) * HD]
-            values[g, rows, :HD] = both[1][:, g * HD : (g + 1) * HD]
+            pair = [part.at[i] for part in ref for i in range(2)] if len(ref) == 1 else ref
+            for kind in range(2):
+                both[kind, g, rows, :HD] = pair[kind][:, g * HD : (g + 1) * HD]
     for place, (_, gap) in enumerate(documents):
         rows = slice(base + place * height, base + (place + 1) * height)
-        for index, (key_ref, value_ref) in enumerate(slots):
+        for index, (first_ref, second_ref) in enumerate(slots):
 
             @pl.when(gap == (labels[index] if ring else index))
             def _():
+                kind = 0
+                if ring:
+                    core = lax.axis_index("req")
+                    kind = 1 - core if 2 * labels[index] > count else core
                 for g in range(kv_heads):
-                    keys[g, rows, :HD] = key_ref[:, g * HD : (g + 1) * HD]
-                    values[g, rows, :HD] = value_ref[:, g * HD : (g + 1) * HD]
+                    columns = slice(g * HD, (g + 1) * HD)
+                    both[kind, g, rows, :HD] = first_ref[:, columns]
+                    both[1 - kind, g, rows, :HD] = second_ref[:, columns]
 
     lane = lax.broadcasted_iota(jnp.int32, (tile * tokens, HD), 1)
     first = jnp.where(lane == 0, 1.0, 0.0).astype(jnp.bfloat16)
@@ -251,7 +257,7 @@
             num_scalar_prefetch=1,
             in_specs=[whole] * len(operands),
             out_specs=pl.BlockSpec(memory_space=pl.ANY) if final else [whole] * 3,
-            scratch_shapes=[pltpu.VMEM((kv_heads, total, 2 * HD), jnp.bfloat16)] * 2 + stage,
+            scratch_shapes=[pltpu.VMEM((2, kv_heads, total, 2 * HD), jnp.bfloat16)] + stage,
         ),
         compiler_params=pltpu.CompilerParams(vmem_limit_bytes=24 << 20),
         cost_estimate=pl.CostEstimate(
@@ -275,12 +281,18 @@
         order = list(range(0, count, 2)) + list(range(1, count, 2))[::-1]
         onward = [(order[i], order[(i + 1) % count]) for i in range(count)]
         both = onward + [(count + target, count + source) for source, target in onward]
+        turned = lax.axis_index("req") == 1
+        slot = (jnp.where(turned, slot[1], slot[0]), jnp.where(turned, slot[0], slot[1]))
         pieces = [slot] + [[None, None] for _ in range(count - 1)]
         for step in range(1, count // 2 + 1):
-            for part in range(2):
+            last = 2 * step == count
+            for part in range(1 if last else 2):
                 pieces[step][part] = lax.ppermute(pieces[step - 1][part], ("req", "ctx"), both)
-                if 2 * step < count:
-                    pieces[count - step][part] = shifted(pieces[step][part], "req", 1)
+                brought = shifted(pieces[step][part], "req", 1)
+                if last:
+                    pieces[step][1] = brought
+                else:
+                    pieces[count - step][part] = brought
     else:
         pieces = [
             [broadcast(part, "ctx", doc_owners[number]) for part in slot] for number in range(DOCS)
@@ -299,10 +311,9 @@
     slots = [(label, *piece) for label, piece in zip(labels, pieces)]
     soon = [s for s in slots if not (ring and 2 * s[0] == count)]
     held, block = fetch(queries[0], *own)
-    window = [(0, block), (1, one), (2, *two)]
-    state = attend("near", scalars, held, window, [], (), None, False)
-    state = attend("middle", scalars, held, [(3, three)], soon, (0,), state, False)
-    return attend("far", scalars, held, [], slots, (1,), state, True)[None]
+    state = attend("near", scalars, held, [(0, block), (2, *two)], [], (), None, False)
+    state = attend("middle", scalars, held, [(1, one)], soon, (0,), state, False)
+    return attend("far", scalars, held, [(3, three)], slots, (1,), state, True)[None]
 
 
 def solution(mesh):

time: 51.8 us -> 49.6 us (0.958)
  local copies, waits for them, and re-layouts: 3.04 us -> 0.01 us
  other arithmetic: 2.63 us -> 3.7 us
    ppermute x8 -> x7, waiting for transfers between devices: 11.5 us -> 16.6 us  [per_device(): lax.ppermute(pieces[step - 1][part], ('req', 'ctx'), both)]
    ppermute x9 -> x10, waiting for transfers between devices: 7.13 us -> 2.44 us  [shifted(): return lax.ppermute(value, axis, pairs)]
    unnamed x10 -> x6, local copies, waits for them, and re-layouts: 3.04 us -> 0.01 us
    select_n x0 -> x1, other arithmetic: none -> 1.07 us  [per_device(): jnp.where(turned, slot[0], slot[1])]
    ppermute x8 -> x7, starting transfers between devices: 5.75 us -> 5.63 us  [per_device(): lax.ppermute(pieces[step - 1][part], ('req', 'ctx'), both)]
    ppermute x9 -> x10, starting transfers between devices: 5.64 us -> 5.7 us  [shifted(): return lax.ppermute(value, axis, pairs)]
  transfers between devices with their start and end apart: 18 -> 18, of which waited for: 9 -> 9; matrix products, arithmetic and copies ran while one was open for 5% -> 7% of each run, Pallas kernels for 14% -> 12%
where the time goes in v5:
time: 49.6 us; the launch traced here: 49.4 us
  waiting for transfers between devices  21.8 us (44%)
  starting transfers between devices  13.2 us (27%)
  Pallas kernels  10.4 us (21%)
  other arithmetic  3.7 us (7%)
    ppermute x7, waiting for transfers between devices, per_device(): lax.ppermute(pieces[step - 1][part], ('req', 'ctx'), both)  16.6 us
    pallas_call x3, Pallas kernels, attend(): pl.pallas_call(functools.partial(attention_body, kv_heads, group, math.gc...  9.95 us
    ppermute x10, starting transfers between devices, shifted(): return lax.ppermute(value, axis, pairs)  5.7 us
    ppermute x7, starting transfers between devices, per_device(): lax.ppermute(pieces[step - 1][part], ('req', 'ctx'), both)  5.63 us
    ppermute x1, waiting for transfers between devices, per_device(): one = lax.ppermute(taken, 'ctx', [(i, i ^ 1) for i in range(count)])  2.81 us
    ppermute x10, waiting for transfers between devices, shifted(): return lax.ppermute(value, axis, pairs)  2.44 us
    another operation x3, other arithmetic, per_device(): jnp.stack([jnp.where(even, own[part], two[part]) for part in range(2)])  1.87 us
    ppermute x1, starting transfers between devices, per_device(): one = lax.ppermute(taken, 'ctx', [(i, i ^ 1) for i in range(count)])  1.85 us
  transfers between devices with their start and end apart: 18, of which 9 were waited for; matrix products, arithmetic and copies ran while one was open for 7% of the time, Pallas kernels for 12%

profile of v5, /device:TPU:0, one launch (start us, length us, event | category | flops | bytes accessed | tf_op | source)
XLA Modules:
  0.0 49.4 jit_solution(11078714655624927520)
XLA Ops:
  0.0 3.1 %collective-permute-start = (bf16[128,512]{1,0:T(8,128)(2,1)}, bf16[128,512]{1,0:T(8,128)(2,1)S(1)}, u32[]{:S(2)}, u32[]{:S(2)}) collective-permute-start(bf16[128,512]{1,0:T(8,128)(2,1)} %bitcast.15), channel_id=1, source_target_pairs={{0,2},{1,3},{2,4},{3,5},{4,6},{5,7},{6,0},{7,1},{8,10},{9,11},{10,... | collective-permute-start | bytes 393224 | tf_op jit(solution)/shard_map/ppermute | solution.py:30
  3.1 1.6 %collective-permute-start.1 = (bf16[128,512]{1,0:T(8,128)(2,1)}, bf16[128,512]{1,0:T(8,128)(2,1)S(1)}, u32[]{:S(2)}, u32[]{:S(2)}) collective-permute-start(bf16[128,512]{1,0:T(8,128)(2,1)} %bitcast.17), channel_id=1, source_target_pairs={{0,2},{1,3},{2,4},{3,5},{4,6},{5,7},{6,0},{7,1},{8,10},{9,11},{10,... | collective-permute-start | bytes 393224 | tf_op jit(solution)/shard_map/ppermute | solution.py:30
  4.7 1.1 %select_bitcast_fusion = (bf16[256,512]{1,0:T(8,128)(2,1)S(1)}, bf16[256,512]{1,0:T(8,128)(2,1)S(1)}) fusion(bf16[1,256,512]{2,1,0:T(8,128)(2,1)} %param.11, bf16[1,256,512]{2,1,0:T(8,128)(2,1)} %param.12, pred[]{:T(512)S(6)} %eq.9), kind=kLoop, calls=%fused_computation.1 | loop fusion | flops 262144 | bytes 1048577 | tf_op jit(solution)/shard_map/jit(_where)/select_n | solution.py:285
  5.8 1.6 %collective-permute-start.4 = (bf16[256,512]{1,0:T(8,128)(2,1)S(1)}, bf16[256,512]{1,0:T(8,128)(2,1)S(1)}, u32[]{:S(2)}, u32[]{:S(2)}) collective-permute-start(bf16[256,512]{1,0:T(8,128)(2,1)S(1)} %get-tuple-element.26.refs_2_), channel_id=1, source_target_pairs={{0,2},{2,4},{4,6},{6,7},{7,5},{5,3},{3,1},{1,0},{10,8},{12,10},{14... | collective-permute-start | bytes 786440 | tf_op jit(solution)/shard_map/ppermute | solution.py:290
  7.5 0.8 %pad_add_fusion.scalars = s32[6]{0:T(128)S(1)} fusion(s32[2]{0:T(128)} %param.13, s32[2]{0:T(128)} %param.14, s32[2]{0:T(128)} %param.15), kind=kLoop, calls=%fused_computation.5 | loop fusion | flops 12 | bytes 48 | tf_op jit(solution)/shard_map/concatenate | solution.py:304
  8.2 1.6 %collective-permute-done.refs_2_ = bf16[128,512]{1,0:T(8,128)(2,1)S(1)} collective-permute-done((bf16[128,512]{1,0:T(8,128)(2,1)}, bf16[128,512]{1,0:T(8,128)(2,1)S(1)}, u32[]{:S(2)}, u32[]{:S(2)}) %collective-permute-start) | collective-permute-done | bytes 131104 | tf_op jit(solution)/shard_map/ppermute | solution.py:30
  9.8 0.9 %select_bitcast_fusion.3 = bf16[1,128,512]{2,1,0:T(8,128)(2,1)S(1)} fusion(bf16[128,512]{1,0:T(8,128)(2,1)S(1)} %collective-permute-done.refs_2_, pred[]{:T(512)S(6)} %eq.8, bf16[1,128,512]{2,1,0:T(8,128)(2,1)} %param.9), kind=kLoop, calls=%fused_computation.4 | loop fusion | flops 65536 | bytes 393217 | tf_op jit(solution)/shard_map/stack | solution.py:305
  10.7 1.5 %collective-permute-done.4.refs_4_ = bf16[256,512]{1,0:T(8,128)(2,1)S(1)} collective-permute-done((bf16[256,512]{1,0:T(8,128)(2,1)S(1)}, bf16[256,512]{1,0:T(8,128)(2,1)S(1)}, u32[]{:S(2)}, u32[]{:S(2)}) %collective-permute-start.4) | collective-permute-done | bytes 262176 | tf_op jit(solution)/shard_map/ppermute | solution.py:290
  12.2 2.0 %collective-permute-start.6 = (bf16[256,512]{1,0:T(8,128)(2,1)S(1)}, bf16[256,512]{1,0:T(8,128)(2,1)S(1)}, u32[]{:S(2)}, u32[]{:S(2)}) collective-permute-start(bf16[256,512]{1,0:T(8,128)(2,1)S(1)} %collective-permute-done.4.refs_4_), channel_id=1, source_target_pairs={{0,2},{2,4},{4,6},{6,7},{7,5},{5,3},{3,1},{1,0},{10,8},{12,10},{14... | collective-permute-start | bytes 786440 | tf_op jit(solution)/shard_map/ppermute | solution.py:290
  14.2 0.9 %select_bitcast_fusion.2 = bf16[1,128,512]{2,1,0:T(8,128)(2,1)S(1)} fusion(bf16[128,512]{1,0:T(8,128)(2,1)S(1)} %collective-permute-done.1.refs_3_, pred[]{:T(512)S(6)} %eq.8, bf16[1,128,512]{2,1,0:T(8,128)(2,1)} %param.10), kind=kLoop, calls=%fused_computation.3 | loop fusion | flops 65536 | bytes 393217 | tf_op jit(solution)/shard_map/stack | solution.py:305
  15.1 1.9 %collective-permute-start.7 = (bf16[256,512]{1,0:T(8,128)(2,1)S(1)}, bf16[256,512]{1,0:T(8,128)(2,1)S(1)}, u32[]{:S(2)}, u32[]{:S(2)}) collective-permute-start(bf16[256,512]{1,0:T(8,128)(2,1)S(1)} %collective-permute-done.5.refs_5_), channel_id=1, source_target_pairs={{0,2},{2,4},{4,6},{6,7},{7,5},{5,3},{3,1},{1,0},{10,8},{12,10},{14... | collective-permute-start | bytes 786440 | tf_op jit(solution)/shard_map/ppermute | solution.py:290
  17.0 1.9 %collective-permute-start.2 = (bf16[2,128,512]{2,1,0:T(8,128)(2,1)S(1)}, bf16[2,128,512]{2,1,0:T(8,128)(2,1)S(1)}, u32[]{:S(2)}, u32[]{:S(2)}) collective-permute-start(bf16[2,128,512]{2,1,0:T(8,128)(2,1)S(1)} %pad_maximum_fusion), channel_id=1, source_target_pairs={{0,1},{1,0},{2,3},{3,2},{4,5},{5,4},{6,7},{7,6},{8,9},{9,8},{10,11... | collective-permute-start | bytes 786440 | tf_op jit(solution)/shard_map/ppermute | solution.py:307
  18.9 2.0 %collective-permute-done.6.refs_6_ = bf16[256,512]{1,0:T(8,128)(2,1)S(1)} collective-permute-done((bf16[256,512]{1,0:T(8,128)(2,1)S(1)}, bf16[256,512]{1,0:T(8,128)(2,1)S(1)}, u32[]{:S(2)}, u32[]{:S(2)}) %collective-permute-start.6) | collective-permute-done | bytes 262176 | tf_op jit(solution)/shard_map/ppermute | solution.py:290
  20.9 0.5 %collective-permute-start.17 = (bf16[256,512]{1,0:T(8,128)(2,1)S(1)}, bf16[256,512]{1,0:T(8,128)(2,1)S(1)}, u32[]{:S(2)}, u32[]{:S(2)}) collective-permute-start(bf16[256,512]{1,0:T(8,128)(2,1)S(1)} %collective-permute-done.5.refs_5_), channel_id=1, source_target_pairs={{0,8},{8,0},{1,9},{9,1},{2,10},{10,2},{3,11},{11,3},{4,12},{12,4},... | collective-permute-start | bytes 786440 | tf_op jit(solution)/shard_map/ppermute | solution.py:30
  21.4 4.5 %collective-permute-done.7.refs_7_ = bf16[256,512]{1,0:T(8,128)(2,1)S(1)} collective-permute-done((bf16[256,512]{1,0:T(8,128)(2,1)S(1)}, bf16[256,512]{1,0:T(8,128)(2,1)S(1)}, u32[]{:S(2)}, u32[]{:S(2)}) %collective-permute-start.7) | collective-permute-done | bytes 262176 | tf_op jit(solution)/shard_map/ppermute | solution.py:290
  25.9 2.8 %collective-permute-done.2.refs_1_ = bf16[2,128,512]{2,1,0:T(8,128)(2,1)S(1)} collective-permute-done((bf16[2,128,512]{2,1,0:T(8,128)(2,1)S(1)}, bf16[2,128,512]{2,1,0:T(8,128)(2,1)S(1)}, u32[]{:S(2)}, u32[]{:S(2)}) %collective-permute-start.2) | collective-permute-done | bytes 262176 | tf_op jit(solution)/shard_map/ppermute | solution.py:307
  28.7 2.8 %collective-permute-done.8.refs_8_ = bf16[256,512]{1,0:T(8,128)(2,1)S(1)} collective-permute-done((bf16[256,512]{1,0:T(8,128)(2,1)S(1)}, bf16[256,512]{1,0:T(8,128)(2,1)S(1)}, u32[]{:S(2)}, u32[]{:S(2)}) %collective-permute-start.8) | collective-permute-done | bytes 262176 | tf_op jit(solution)/shard_map/ppermute | solution.py:290
  31.6 0.5 %collective-permute-start.12 = (bf16[256,512]{1,0:T(8,128)(2,1)S(1)}, bf16[256,512]{1,0:T(8,128)(2,1)S(1)}, u32[]{:S(2)}, u32[]{:S(2)}) collective-permute-start(bf16[256,512]{1,0:T(8,128)(2,1)S(1)} %collective-permute-done.8.refs_8_), channel_id=1, source_target_pairs={{0,8},{8,0},{1,9},{9,1},{2,10},{10,2},{3,11},{11,3},{4,12},{12,4},... | collective-permute-start | bytes 786440 | tf_op jit(solution)/shard_map/ppermute | solution.py:30
  32.1 2.3 %collective-permute-done.9.refs_9_ = bf16[256,512]{1,0:T(8,128)(2,1)S(1)} collective-permute-done((bf16[256,512]{1,0:T(8,128)(2,1)S(1)}, bf16[256,512]{1,0:T(8,128)(2,1)S(1)}, u32[]{:S(2)}, u32[]{:S(2)}) %collective-permute-start.9) | collective-permute-done | bytes 262176 | tf_op jit(solution)/shard_map/ppermute | solution.py:290
  34.4 3.5 %collective-permute-done.10.refs_10_ = bf16[256,512]{1,0:T(8,128)(2,1)S(1)} collective-permute-done((bf16[256,512]{1,0:T(8,128)(2,1)S(1)}, bf16[256,512]{1,0:T(8,128)(2,1)S(1)}, u32[]{:S(2)}, u32[]{:S(2)}) %collective-permute-start.10) | collective-permute-done | bytes 262176 | tf_op jit(solution)/shard_map/ppermute | solution.py:290
  38.4 2.2 %shard_map.82 = (f32[4,1024,128]{2,1,0:T(8,128)S(1)}, f32[4,1024,128]{2,1,0:T(8,128)S(1)}, f32[4,1024,128]{2,1,0:T(8,128)S(1)}) custom-call(s32[6]{0:T(128)S(1)} %pad_add_fusion.scalars, bf16[128,4096]{1,0:T(8,128)(2,1)S(1)} %get-tuple-element.16.refs_0_, bf16[2,128,512]{2,1,0:T(8,128)(2,1)S(1)} %get-tuple-element.18.refs_1_, ...), custom_call_target="tpu_custom_call" | custom-call | flops 536870912 | bytes 4194304 | tf_op jit(solution)/shard_map/pallas_call | solution.py:242
  40.7 3.4 %shard_map.83 = (f32[4,1024,128]{2,1,0:T(8,128)S(1)}, f32[4,1024,128]{2,1,0:T(8,128)S(1)}, f32[4,1024,128]{2,1,0:T(8,128)S(1)}) custom-call(s32[6]{0:T(128)S(1)} %pad_add_fusion.scalars, bf16[128,4096]{1,0:T(8,128)(2,1)S(1)} %get-tuple-element.16.refs_0_, bf16[2,128,512]{2,1,0:T(8,128)(2,1)S(1)} %collective-permute-done.2.refs_1_, ...), custom_call_target="tpu_custom_call" | custom-call | flops 805306368 | bytes 4194304 | tf_op jit(solution)/shard_map/pallas_call | solution.py:242
  44.0 0.8 %collective-permute-done.3.refs_1_ = bf16[2,128,512]{2,1,0:T(8,128)(2,1)S(1)} collective-permute-done((bf16[2,128,512]{2,1,0:T(8,128)(2,1)S(1)}, bf16[2,128,512]{2,1,0:T(8,128)(2,1)S(1)}, u32[]{:S(2)}, u32[]{:S(2)}) %collective-permute-start.3) | collective-permute-done | bytes 262176 | tf_op jit(solution)/shard_map/ppermute | solution.py:30
  44.9 4.3 %shard_map.84 = bf16[128,4096]{1,0:T(8,128)(2,1)} custom-call(s32[6]{0:T(128)S(1)} %pad_add_fusion.scalars, bf16[128,4096]{1,0:T(8,128)(2,1)S(1)} %get-tuple-element.16.refs_0_, bf16[2,128,512]{2,1,0:T(8,128)(2,1)S(1)} %collective-permute-done.3.refs_1_, bf16[256,512]{1,0:T(8,128)(2,1)S(1)} %get-tuple-element.26.refs_2_, ...), custom_call_target="tpu_custom_call" | custom-call | flops 805306368 | bytes 4194304 | tf_op jit(solution)/shard_map/pallas_call | solution.py:242
  (27 shorter events, 0.7 us)
Async XLA Ops:
  0.0 37.9 %copy-start.1 = (bf16[1,128,512]{2,1,0:T(8,128)(2,1)S(1)}, bf16[1,128,512]{2,1,0:T(8,128)(2,1)}, u32[]{:S(2)}) copy-start(bf16[1,128,512]{2,1,0:T(8,128)(2,1)} %param.9) | copy-start | bytes 393220
  0.0 37.9 %copy-start.2 = (bf16[1,128,512]{2,1,0:T(8,128)(2,1)S(1)}, bf16[1,128,512]{2,1,0:T(8,128)(2,1)}, u32[]{:S(2)}) copy-start(bf16[1,128,512]{2,1,0:T(8,128)(2,1)} %param.10) | copy-start | bytes 393220
  0.0 37.9 %copy-start = (bf16[1,128,4096]{2,1,0:T(8,128)(2,1)S(1)}, bf16[1,128,4096]{2,1,0:T(8,128)(2,1)}, u32[]{:S(2)}) copy-start(bf16[1,128,4096]{2,1,0:T(8,128)(2,1)} %param.8) | copy-start | bytes 3145732
  0.0 9.8 %collective-permute-start = (bf16[128,512]{1,0:T(8,128)(2,1)}, bf16[128,512]{1,0:T(8,128)(2,1)S(1)}, u32[]{:S(2)}, u32[]{:S(2)}) collective-permute-start(bf16[128,512]{1,0:T(8,128)(2,1)} %bitcast.15), channel_id=1, source_target_pairs={{0,2},{1,3},{2,4},{3,5},{4,6},{5,7},{6,0},{7,1},{8,10},{9,11},{10,... | collective-permute-start | bytes 393224 | tf_op jit(solution)/shard_map/ppermute | solution.py:30
  3.1 11.1 %collective-permute-start.1 = (bf16[128,512]{1,0:T(8,128)(2,1)}, bf16[128,512]{1,0:T(8,128)(2,1)S(1)}, u32[]{:S(2)}, u32[]{:S(2)}) collective-permute-start(bf16[128,512]{1,0:T(8,128)(2,1)} %bitcast.17), channel_id=1, source_target_pairs={{0,2},{1,3},{2,4},{3,5},{4,6},{5,7},{6,0},{7,1},{8,10},{9,11},{10,... | collective-permute-start | bytes 393224 | tf_op jit(solution)/shard_map/ppermute | solution.py:30
  5.8 6.4 %collective-permute-start.4 = (bf16[256,512]{1,0:T(8,128)(2,1)S(1)}, bf16[256,512]{1,0:T(8,128)(2,1)S(1)}, u32[]{:S(2)}, u32[]{:S(2)}) collective-permute-start(bf16[256,512]{1,0:T(8,128)(2,1)S(1)} %get-tuple-element.26.refs_2_), channel_id=1, source_target_pairs={{0,2},{2,4},{4,6},{6,7},{7,5},{5,3},{3,1},{1,0},{10,8},{12,10},{14... | collective-permute-start | bytes 786440 | tf_op jit(solution)/shard_map/ppermute | solution.py:290
  7.4 7.7 %collective-permute-start.5 = (bf16[256,512]{1,0:T(8,128)(2,1)S(1)}, bf16[256,512]{1,0:T(8,128)(2,1)S(1)}, u32[]{:S(2)}, u32[]{:S(2)}) collective-permute-start(bf16[256,512]{1,0:T(8,128)(2,1)S(1)} %get-tuple-element.25.refs_3_), channel_id=1, source_target_pairs={{0,2},{2,4},{4,6},{6,7},{7,5},{5,3},{3,1},{1,0},{10,8},{12,10},{14... | collective-permute-start | bytes 786440 | tf_op jit(solution)/shard_map/ppermute | solution.py:290
  12.2 8.6 %collective-permute-start.6 = (bf16[256,512]{1,0:T(8,128)(2,1)S(1)}, bf16[256,512]{1,0:T(8,128)(2,1)S(1)}, u32[]{:S(2)}, u32[]{:S(2)}) collective-permute-start(bf16[256,512]{1,0:T(8,128)(2,1)S(1)} %collective-permute-done.4.refs_4_), channel_id=1, source_target_pairs={{0,2},{2,4},{4,6},{6,7},{7,5},{5,3},{3,1},{1,0},{10,8},{12,10},{14... | collective-permute-start | bytes 786440 | tf_op jit(solution)/shard_map/ppermute | solution.py:290
  15.1 10.8 %collective-permute-start.7 = (bf16[256,512]{1,0:T(8,128)(2,1)S(1)}, bf16[256,512]{1,0:T(8,128)(2,1)S(1)}, u32[]{:S(2)}, u32[]{:S(2)}) collective-permute-start(bf16[256,512]{1,0:T(8,128)(2,1)S(1)} %collective-permute-done.5.refs_5_), channel_id=1, source_target_pairs={{0,2},{2,4},{4,6},{6,7},{7,5},{5,3},{3,1},{1,0},{10,8},{12,10},{14... | collective-permute-start | bytes 786440 | tf_op jit(solution)/shard_map/ppermute | solution.py:290
  17.0 11.7 %collective-permute-start.2 = (bf16[2,128,512]{2,1,0:T(8,128)(2,1)S(1)}, bf16[2,128,512]{2,1,0:T(8,128)(2,1)S(1)}, u32[]{:S(2)}, u32[]{:S(2)}) collective-permute-start(bf16[2,128,512]{2,1,0:T(8,128)(2,1)S(1)} %pad_maximum_fusion), channel_id=1, source_target_pairs={{0,1},{1,0},{2,3},{3,2},{4,5},{5,4},{6,7},{7,6},{8,9},{9,8},{10,11... | collective-permute-start | bytes 786440 | tf_op jit(solution)/shard_map/ppermute | solution.py:307
  20.8 10.7 %collective-permute-start.8 = (bf16[256,512]{1,0:T(8,128)(2,1)S(1)}, bf16[256,512]{1,0:T(8,128)(2,1)S(1)}, u32[]{:S(2)}, u32[]{:S(2)}) collective-permute-start(bf16[256,512]{1,0:T(8,128)(2,1)S(1)} %collective-permute-done.6.refs_6_), channel_id=1, source_target_pairs={{0,2},{2,4},{4,6},{6,7},{7,5},{5,3},{3,1},{1,0},{10,8},{12,10},{14... | collective-permute-start | bytes 786440 | tf_op jit(solution)/shard_map/ppermute | solution.py:290
  20.9 10.7 %collective-permute-start.16 = (bf16[256,512]{1,0:T(8,128)(2,1)S(1)}, bf16[256,512]{1,0:T(8,128)(2,1)S(1)}, u32[]{:S(2)}, u32[]{:S(2)}) collective-permute-start(bf16[256,512]{1,0:T(8,128)(2,1)S(1)} %collective-permute-done.4.refs_4_), channel_id=1, source_target_pairs={{0,8},{8,0},{1,9},{9,1},{2,10},{10,2},{3,11},{11,3},{4,12},{12,4},... | collective-permute-start | bytes 786440 | tf_op jit(solution)/shard_map/ppermute | solution.py:30
  20.9 10.7 %collective-permute-start.17 = (bf16[256,512]{1,0:T(8,128)(2,1)S(1)}, bf16[256,512]{1,0:T(8,128)(2,1)S(1)}, u32[]{:S(2)}, u32[]{:S(2)}) collective-permute-start(bf16[256,512]{1,0:T(8,128)(2,1)S(1)} %collective-permute-done.5.refs_5_), channel_id=1, source_target_pairs={{0,8},{8,0},{1,9},{9,1},{2,10},{10,2},{3,11},{11,3},{4,12},{12,4},... | collective-permute-start | bytes 786440 | tf_op jit(solution)/shard_map/ppermute | solution.py:30
  25.9 8.4 %collective-permute-start.9 = (bf16[256,512]{1,0:T(8,128)(2,1)S(1)}, bf16[256,512]{1,0:T(8,128)(2,1)S(1)}, u32[]{:S(2)}, u32[]{:S(2)}) collective-permute-start(bf16[256,512]{1,0:T(8,128)(2,1)S(1)} %collective-permute-done.7.refs_7_), channel_id=1, source_target_pairs={{0,2},{2,4},{4,6},{6,7},{7,5},{5,3},{3,1},{1,0},{10,8},{12,10},{14... | collective-permute-start | bytes 786440 | tf_op jit(solution)/shard_map/ppermute | solution.py:290
  28.7 5.6 %collective-permute-start.14 = (bf16[256,512]{1,0:T(8,128)(2,1)S(1)}, bf16[256,512]{1,0:T(8,128)(2,1)S(1)}, u32[]{:S(2)}, u32[]{:S(2)}) collective-permute-start(bf16[256,512]{1,0:T(8,128)(2,1)S(1)} %collective-permute-done.6.refs_6_), channel_id=1, source_target_pairs={{0,8},{8,0},{1,9},{9,1},{2,10},{10,2},{3,11},{11,3},{4,12},{12,4},... | collective-permute-start | bytes 786440 | tf_op jit(solution)/shard_map/ppermute | solution.py:30
  31.6 6.4 %collective-permute-start.10 = (bf16[256,512]{1,0:T(8,128)(2,1)S(1)}, bf16[256,512]{1,0:T(8,128)(2,1)S(1)}, u32[]{:S(2)}, u32[]{:S(2)}) collective-permute-start(bf16[256,512]{1,0:T(8,128)(2,1)S(1)} %collective-permute-done.8.refs_8_), channel_id=1, source_target_pairs={{0,2},{2,4},{4,6},{6,7},{7,5},{5,3},{3,1},{1,0},{10,8},{12,10},{14... | collective-permute-start | bytes 786440 | tf_op jit(solution)/shard_map/ppermute | solution.py:290
  31.6 9.1 %collective-permute-start.15 = (bf16[256,512]{1,0:T(8,128)(2,1)S(1)}, bf16[256,512]{1,0:T(8,128)(2,1)S(1)}, u32[]{:S(2)}, u32[]{:S(2)}) collective-permute-start(bf16[256,512]{1,0:T(8,128)(2,1)S(1)} %collective-permute-done.7.refs_7_), channel_id=1, source_target_pairs={{0,8},{8,0},{1,9},{9,1},{2,10},{10,2},{3,11},{11,3},{4,12},{12,4},... | collective-permute-start | bytes 786440 | tf_op jit(solution)/shard_map/ppermute | solution.py:30
  31.6 9.1 %collective-permute-start.12 = (bf16[256,512]{1,0:T(8,128)(2,1)S(1)}, bf16[256,512]{1,0:T(8,128)(2,1)S(1)}, u32[]{:S(2)}, u32[]{:S(2)}) collective-permute-start(bf16[256,512]{1,0:T(8,128)(2,1)S(1)} %collective-permute-done.8.refs_8_), channel_id=1, source_target_pairs={{0,8},{8,0},{1,9},{9,1},{2,10},{10,2},{3,11},{11,3},{4,12},{12,4},... | collective-permute-start | bytes 786440 | tf_op jit(solution)/shard_map/ppermute | solution.py:30
  34.4 6.3 %collective-permute-start.13 = (bf16[256,512]{1,0:T(8,128)(2,1)S(1)}, bf16[256,512]{1,0:T(8,128)(2,1)S(1)}, u32[]{:S(2)}, u32[]{:S(2)}) collective-permute-start(bf16[256,512]{1,0:T(8,128)(2,1)S(1)} %collective-permute-done.9.refs_9_), channel_id=1, source_target_pairs={{0,8},{8,0},{1,9},{9,1},{2,10},{10,2},{3,11},{11,3},{4,12},{12,4},... | collective-permute-start | bytes 786440 | tf_op jit(solution)/shard_map/ppermute | solution.py:30
  34.4 10.5 %collective-permute-start.3 = (bf16[2,128,512]{2,1,0:T(8,128)(2,1)S(1)}, bf16[2,128,512]{2,1,0:T(8,128)(2,1)S(1)}, u32[]{:S(2)}, u32[]{:S(2)}) collective-permute-start(bf16[2,128,512]{2,1,0:T(8,128)(2,1)S(1)} %collective-permute-done.2.refs_1_), channel_id=1, source_target_pairs={{0,2},{1,3},{2,4},{3,5},{4,6},{5,7},{6,0},{7,1},{8,10},{9,11},{10,... | collective-permute-start | bytes 786440 | tf_op jit(solution)/shard_map/ppermute | solution.py:30
  37.9 7.0 %collective-permute-start.11 = (bf16[256,512]{1,0:T(8,128)(2,1)S(1)}, bf16[256,512]{1,0:T(8,128)(2,1)S(1)}, u32[]{:S(2)}, u32[]{:S(2)}) collective-permute-start(bf16[256,512]{1,0:T(8,128)(2,1)S(1)} %collective-permute-done.10.refs_10_), channel_id=1, source_target_pairs={{0,8},{8,0},{1,9},{9,1},{2,10},{10,2},{3,11},{11,3},{4,12},{12,4},... | collective-permute-start | bytes 786440 | tf_op jit(solution)/shard_map/ppermute | solution.py:30
